TPU v7x, 32 devices: a whole 2x2x4 slice. The times are simulated.
32 devices in a mesh: patch: 16 (over z, y, x), rep: 2 (over core).
Axes of the slice: x: 2, y: 2, z: 4, core: 2. Of those that a mesh axis runs over, the one named last changes fastest.
Arguments:
- tokens: bfloat16 [8192, 512], P(('patch', 'rep')), may hold values from -6 to 6
- cotangent: bfloat16 [8192, 512], P(('patch', 'rep')), may hold values from -6 to 6
- dest: int32 [8192], P(('patch', 'rep')), may hold values from 0 to 15, as said below
- neighbours: int32 [8192, 16], P(('patch', 'rep')), may hold values from 0 to 8191, as said below
- w_qkv: bfloat16 [512, 1536], replicated, may hold values from -0.25 to 0.25
- w_out: bfloat16 [512, 512], replicated, may hold values from -1 to 1
- w_up: bfloat16 [512, 2048], replicated, may hold values from -0.25 to 0.25
- w_down: bfloat16 [2048, 512], replicated, may hold values from -0.125 to 0.125
- ada_attn: float32 [32, 1024], replicated, may hold values from -0.5 to 0.5
- ada_mlp: float32 [32, 1024], replicated, may hold values from -0.5 to 0.5
- cond: float32 [32], replicated, may hold values from -4 to 4
Outputs:
- output: bfloat16 [8192, 512], P(('patch', 'rep'))
- grad_tokens: bfloat16 [8192, 512], P(('patch', 'rep'))
- grad_qkv: float32 [512, 1536], replicated
- grad_out: float32 [512, 512], replicated
- grad_up: float32 [512, 2048], replicated
- grad_down: float32 [2048, 512], replicated
- grad_ada_attn: float32 [32, 1024], replicated
- grad_ada_mlp: float32 [32, 1024], replicated
- grad_cond: float32 [32], replicated
Inputs may be any that keep to these rules, and one draw needn't show every extreme that they name: `dest`: within each index of rep, every patch receives exactly 256 rows; one device sends at most 17 rows to one patch, and each device sends exactly 17 rows to some patch. neighbours[i, 0] = i; every other neighbour of a node in patch q lies in the rows of the same index of rep in patch q - 1, q or q + 1, counted cyclically over 16 patches; positions may repeat.
All inputs are finite; a program needn't handle non-finite values.
Results may differ from a plain program's by a relative error of at most 0.013.
Values may be sent and summed in bfloat16 or wider, within the bound.
A program may use at most 128 MiB of HBM per device.

v0:
```python
import jax
import jax.numpy as jnp
from jax import lax
from jax.sharding import PartitionSpec as P

H = 4
HD = 128
NEIGH = 16


NORM_EPS = 1e-05


def extended(cells, sides, width):
    for axis, dim in sides:
        count = lax.axis_size(axis)
        head = lax.slice_in_dim(cells, 0, width, axis=dim)
        tail = lax.slice_in_dim(cells, cells.shape[dim] - width, cells.shape[dim], axis=dim)
        cells = jnp.concatenate(
            [
                lax.ppermute(tail, axis, [(i, (i + 1) % count) for i in range(count)]),
                cells,
                lax.ppermute(head, axis, [((i + 1) % count, i) for i in range(count)]),
            ],
            axis=dim,
        )
    return cells


def from_behind(array, axis, by):
    size = lax.axis_size(axis)
    return lax.ppermute(array, axis, [(i, (i + by) % size) for i in range(size)])


def norm_parts(values_in):
    centre = jnp.mean(values_in, axis=-1, keepdims=True)
    centred = values_in - centre
    inverse = lax.rsqrt(jnp.mean(centred * centred, axis=-1, keepdims=True) + NORM_EPS)
    return (centred * inverse, inverse)


def norm_back(grad_normed, plain, inverse, coeffs):
    feature_width = plain.shape[-1]
    scaled = grad_normed * (1.0 + coeffs[:feature_width])
    inner = (
        scaled
        - jnp.mean(scaled, axis=-1, keepdims=True)
        - plain * jnp.mean(scaled * plain, axis=-1, keepdims=True)
    )
    coeff_grad = jnp.concatenate(
        [jnp.sum(grad_normed * plain, axis=0), jnp.sum(grad_normed, axis=0)]
    )
    return (inverse * inner, coeff_grad)


def local(tokens, cotangent, dest, neighbours, w_qkv, w_out, w_up, w_down, ada_attn, ada_mlp, cond):
    highest = lax.Precision.HIGHEST
    row_count = tokens.shape[0]
    feature_width = tokens.shape[1]
    patch_count = lax.axis_size("patch")
    group_count = lax.axis_size("rep")
    capacity = row_count // patch_count + 1
    one_hot = (dest[:, None] == jnp.arange(patch_count, dtype=jnp.int32)[None, :]).astype(jnp.int32)
    earlier = jnp.cumsum(one_hot, axis=0) - one_hot
    slot_index = jnp.sum(earlier * one_hot, axis=1)
    sent_counts = jnp.sum(one_hot, axis=0)
    flat_slot = dest * capacity + slot_index
    outgoing = jnp.zeros((patch_count * capacity, 2 * feature_width), jnp.bfloat16)
    outgoing = outgoing.at[flat_slot].set(jnp.concatenate([tokens, cotangent], axis=1))
    arrived, arrived_counts = (
        lax.all_to_all(
            outgoing.reshape(patch_count, capacity, 2 * feature_width),
            "patch",
            split_axis=0,
            concat_axis=0,
            tiled=True,
        ),
        lax.all_to_all(sent_counts[:, None], "patch", split_axis=0, concat_axis=0, tiled=True),
    )
    counts_in = arrived_counts[:, 0]
    offsets = jnp.cumsum(counts_in) - counts_in
    columns = jnp.arange(capacity, dtype=jnp.int32)
    target = jnp.where(
        columns[None, :] < counts_in[:, None], offsets[:, None] + columns[None, :], row_count
    ).reshape(-1)
    placed = (
        jnp.zeros((row_count + 1, 2 * feature_width), jnp.bfloat16)
        .at[target]
        .set(arrived.reshape(-1, 2 * feature_width))[:row_count]
    )
    node_rows = placed[:, :feature_width].astype(jnp.float32)
    upstream = placed[:, feature_width:]
    coeff_attn = jnp.dot(cond, ada_attn, precision=highest)
    coeff_mlp = jnp.dot(cond, ada_mlp, precision=highest)
    plain_first, inv_first = norm_parts(node_rows)
    normed = (plain_first * (1.0 + coeff_attn[:feature_width]) + coeff_attn[feature_width:]).astype(
        jnp.bfloat16
    )
    projected = jnp.dot(normed, w_qkv, preferred_element_type=jnp.float32)
    queries = projected[:, :feature_width].astype(jnp.bfloat16)
    key_value = projected[:, feature_width:].astype(jnp.bfloat16)
    beside_all = extended(normed, (("patch", 0),), row_count)
    side_rows = jnp.concatenate([beside_all[:row_count], beside_all[2 * row_count :]], axis=0)
    side_kv = jnp.dot(
        side_rows, w_qkv[:, feature_width:], preferred_element_type=jnp.float32
    ).astype(jnp.bfloat16)
    kv_table = jnp.concatenate([side_kv[:row_count], key_value, side_kv[row_count:]], axis=0)
    my_patch = lax.axis_index("patch")
    owners = neighbours // row_count // group_count
    local_row = neighbours % row_count
    rel_patch = (owners - my_patch) % patch_count
    table_index = jnp.where(
        rel_patch == 0,
        row_count + local_row,
        jnp.where(rel_patch == 1, 2 * row_count + local_row, local_row),
    )
    block_rows = min(512, row_count)
    block_count = row_count // block_rows
    score_scale = 1.0 / HD**0.5

    def gather_block(index_block):
        gathered = kv_table[index_block]
        key_block = gathered[..., :feature_width].reshape(block_rows, NEIGH, H, HD)
        value_block = gathered[..., feature_width:].reshape(block_rows, NEIGH, H, HD)
        return (key_block, value_block)

    def forward_block(pieces):
        query_block, index_block = pieces
        key_block, value_block = gather_block(index_block)
        scores = (
            jnp.einsum(
                "bhd,bjhd->bhj",
                query_block.reshape(block_rows, H, HD),
                key_block,
                preferred_element_type=jnp.float32,
            )
            * score_scale
        )
        row_max = jnp.max(scores, axis=-1, keepdims=True)
        row_total = jnp.sum(jnp.exp(scores - row_max), axis=-1, keepdims=True)
        log_total = row_max + jnp.log(row_total)
        weights = jnp.exp(scores - log_total).astype(jnp.bfloat16)
        mixture = jnp.einsum(
            "bhj,bjhd->bhd", weights, value_block, preferred_element_type=jnp.float32
        )
        return (mixture.reshape(block_rows, feature_width).astype(jnp.bfloat16), log_total[..., 0])

    query_blocks = queries.reshape(block_count, block_rows, feature_width)
    index_blocks = table_index.reshape(block_count, block_rows, NEIGH)
    heads_out, log_totals = lax.map(forward_block, (query_blocks, index_blocks))
    heads_out = heads_out.reshape(row_count, feature_width)
    residual = node_rows + jnp.dot(heads_out, w_out, preferred_element_type=jnp.float32)
    plain_second, inv_second = norm_parts(residual)
    normed_mlp = (
        plain_second * (1.0 + coeff_mlp[:feature_width]) + coeff_mlp[feature_width:]
    ).astype(jnp.bfloat16)
    up_proj = jnp.dot(normed_mlp, w_up, preferred_element_type=jnp.float32)
    activation = jax.nn.silu(up_proj).astype(jnp.bfloat16)
    output_rows = residual + jnp.dot(activation, w_down, preferred_element_type=jnp.float32)
    gradient_down = jnp.einsum(
        "ri,rj->ij", activation, upstream, preferred_element_type=jnp.float32
    )
    grad_act = jnp.einsum("rj,ij->ri", upstream, w_down, preferred_element_type=jnp.float32)
    sigmoid_up = jax.nn.sigmoid(up_proj)
    grad_upproj = (grad_act * sigmoid_up * (1.0 + up_proj * (1.0 - sigmoid_up))).astype(
        jnp.bfloat16
    )
    gradient_up = jnp.einsum(
        "ri,rj->ij", normed_mlp, grad_upproj, preferred_element_type=jnp.float32
    )
    grad_normed_mlp = jnp.einsum("rj,ij->ri", grad_upproj, w_up, preferred_element_type=jnp.float32)
    grad_resid_norm, coeff_mlp_grad = norm_back(
        grad_normed_mlp, plain_second, inv_second, coeff_mlp
    )
    grad_residual = upstream.astype(jnp.float32) + grad_resid_norm
    grad_branch = grad_residual.astype(jnp.bfloat16)
    gradient_out = jnp.einsum(
        "ri,rj->ij", heads_out, grad_branch, preferred_element_type=jnp.float32
    )
    grad_heads = jnp.einsum(
        "rj,ij->ri", grad_branch, w_out, preferred_element_type=jnp.float32
    ).astype(jnp.bfloat16)

    def backward_block(table_grad, pieces):
        query_block, index_block, log_block, heads_grad = pieces
        key_block, value_block = gather_block(index_block)
        query_heads = query_block.reshape(block_rows, H, HD)
        scores = (
            jnp.einsum("bhd,bjhd->bhj", query_heads, key_block, preferred_element_type=jnp.float32)
            * score_scale
        )
        weights = jnp.exp(scores - log_block[..., None])
        weights_low = weights.astype(jnp.bfloat16)
        grad_heads_block = heads_grad.reshape(block_rows, H, HD)
        grad_weights = jnp.einsum(
            "bhd,bjhd->bhj", grad_heads_block, value_block, preferred_element_type=jnp.float32
        )
        grad_scores = weights * (
            grad_weights - jnp.sum(weights * grad_weights, axis=-1, keepdims=True)
        )
        scores_low = grad_scores.astype(jnp.bfloat16)
        grad_query = (
            jnp.einsum("bhj,bjhd->bhd", scores_low, key_block, preferred_element_type=jnp.float32)
            * score_scale
        )
        grad_key = (
            jnp.einsum("bhj,bhd->bjhd", scores_low, query_heads, preferred_element_type=jnp.float32)
            * score_scale
        )
        grad_value = jnp.einsum(
            "bhj,bhd->bjhd", weights_low, grad_heads_block, preferred_element_type=jnp.float32
        )
        pair_grad = jnp.concatenate(
            [
                grad_key.reshape(block_rows * NEIGH, feature_width),
                grad_value.reshape(block_rows * NEIGH, feature_width),
            ],
            axis=1,
        )
        table_grad = table_grad.at[index_block.reshape(-1)].add(pair_grad)
        return (table_grad, grad_query.reshape(block_rows, feature_width))

    table_grad, grad_queries = lax.scan(
        backward_block,
        jnp.zeros((3 * row_count, 2 * feature_width), jnp.float32),
        (
            query_blocks,
            index_blocks,
            log_totals,
            grad_heads.reshape(block_count, block_rows, feature_width),
        ),
    )
    returned = table_grad[row_count : 2 * row_count]
    for shift_by, side_piece in ((-1, table_grad[:row_count]), (1, table_grad[2 * row_count :])):
        returned = returned + from_behind(
            side_piece.astype(jnp.bfloat16), "patch", shift_by
        ).astype(side_piece.dtype)
    grad_projected = jnp.concatenate(
        [grad_queries.reshape(row_count, feature_width), returned], axis=1
    ).astype(jnp.bfloat16)
    gradient_proj = jnp.einsum(
        "ri,rj->ij", normed, grad_projected, preferred_element_type=jnp.float32
    )
    grad_normed = jnp.einsum("rj,ij->ri", grad_projected, w_qkv, preferred_element_type=jnp.float32)
    grad_input_norm, coeff_attn_grad = norm_back(grad_normed, plain_first, inv_first, coeff_attn)
    grad_input = (grad_residual + grad_input_norm).astype(jnp.bfloat16)
    gradient_proj, gradient_out, gradient_up, gradient_down, coeff_attn_grad, coeff_mlp_grad = (
        lax.psum(
            (
                gradient_proj,
                gradient_out,
                gradient_up,
                gradient_down,
                coeff_attn_grad,
                coeff_mlp_grad,
            ),
            ("patch", "rep"),
        )
    )
    gradient_ada_attn = jnp.outer(cond, coeff_attn_grad)
    gradient_ada_mlp = jnp.outer(cond, coeff_mlp_grad)
    gradient_cond = jnp.dot(ada_attn, coeff_attn_grad, precision=highest) + jnp.dot(
        ada_mlp, coeff_mlp_grad, precision=highest
    )
    leaving = jnp.concatenate([output_rows.astype(jnp.bfloat16), grad_input], axis=1)
    padded = jnp.concatenate([leaving, jnp.zeros((1, 2 * feature_width), jnp.bfloat16)], axis=0)
    going_back = padded[target].reshape(patch_count, capacity, 2 * feature_width)
    home_rows = lax.all_to_all(
        going_back, "patch", split_axis=0, concat_axis=0, tiled=True
    ).reshape(-1, 2 * feature_width)
    band_rows = home_rows[flat_slot]
    return (
        band_rows[:, :feature_width],
        band_rows[:, feature_width:],
        gradient_proj,
        gradient_out,
        gradient_up,
        gradient_down,
        gradient_ada_attn,
        gradient_ada_mlp,
        gradient_cond,
    )


def solution(mesh):
    return jax.shard_map(
        local,
        mesh=mesh,
        in_specs=(
            P(("patch", "rep"), None),
            P(("patch", "rep"), None),
            P(("patch", "rep")),
            P(("patch", "rep"), None),
            P(),
            P(),
            P(),
            P(),
            P(),
            P(),
            P(),
        ),
        out_specs=(
            P(("patch", "rep"), None),
            P(("patch", "rep"), None),
            P(),
            P(),
            P(),
            P(),
            P(),
            P(),
            P(),
        ),
        check_vma=False,
    )
```

profile of v0, /device:TPU:0, one launch (start us, length us, event | category | flops | bytes accessed | tf_op | source)
XLA Modules:
  0.0 489.6 jit_solution(324026931602704912)
XLA Ops:
  10.4 8.3 %all-to-all-start = ((s32[16,1,1]{2,1,0:T(1,128)}), s32[16,1,1]{2,1,0:T(1,128)S(1)}, u32[]{:S(2)}, u32[]{:S(2)}) async-start(s32[16,1,1]{2,1,0:T(1,128)} %copy.43), calls=%async_computation | async-start | bytes 16384 | tf_op jit(solution)/shard_map/all_to_all | solution.py:78
  26.0 5.3 %all-to-all-start.1 = ((bf16[16,17,1024]{2,1,0:T(8,128)(2,1)}), bf16[16,17,1024]{2,1,0:T(8,128)(2,1)S(1)}, u32[]{:S(2)}, u32[]{:S(2)}) async-start(bf16[16,17,1024]{2,1,0:T(8,128)(2,1)} %reshape.284), calls=%async_computation.1 | async-start | bytes 1572864 | tf_op jit(solution)/shard_map/all_to_all | solution.py:71
  32.7 17.8 %all-to-all-done.1 = bf16[16,17,1024]{2,1,0:T(8,128)(2,1)S(1)} async-done(((bf16[16,17,1024]{2,1,0:T(8,128)(2,1)}), bf16[16,17,1024]{2,1,0:T(8,128)(2,1)S(1)}, u32[]{:S(2)}, u32[]{:S(2)}) %all-to-all-start.1) | async-done | bytes 557088 | tf_op jit(solution)/shard_map/all_to_all | solution.py:71
  55.1 5.2 %collective-permute-start.1 = (bf16[256,512]{1,0:T(8,128)(2,1)S(1)}, bf16[256,512]{1,0:T(8,128)(2,1)}, u32[]{:S(2)}, u32[]{:S(2)}) collective-permute-start(bf16[256,512]{1,0:T(8,128)(2,1)S(1)} %fusion.38), channel_id=1, source_target_pairs={{2,0},{4,2},{6,4},{8,6},{10,8},{12,10},{14,12},{16,14},{18,16},{20... | collective-permute-start | bytes 786440 | tf_op jit(solution)/shard_map/ppermute | solution.py:23
  70.6 22.5 %gather_fusion = bf16[4096,1024]{1,0:T(8,128)(2,1)} fusion(bf16[768,1024]{1,0:T(8,128)(2,1)} %pad_maximum_fusion, s32[4096]{0:T(1024)S(1)} %broadcast_clamp_fusion), kind=kCustom, calls=%fused_computation | custom fusion | bytes 16793600 | tf_op jit(solution)/shard_map/while/body/eval_jaxpr/gather | solution.py:122
  93.1 5.9 %slice_bitcast_fusion = (bf16[256,2,4,8,128]{4,3,2,1,0:T(8,128)(2,1)}, bf16[256,2,4,8,128]{4,3,2,1,0:T(8,128)(2,1)S(1)}) fusion(bf16[256,16,1024]{2,1,0:T(8,128)(2,1)} %bitcast.129), kind=kLoop, calls=%fused_computation.22 | loop fusion | bytes 16777216
  105.5 3.5 fusion.7
  116.7 3.6 fusion.93
  126.9 4.4 fusion.9
  131.3 4.9 %multiply_multiply_fusion = f32[256,4,128,16]{2,1,3,0:T(4,128)S(1)} fusion(f32[256,4,16]{1,2,0:T(8,128)S(1)} %copy-done.2, f32[256,4,128]{2,1,0:T(4,128)S(1)} %copy-done.13), kind=kLoop, calls=%fused_computation.13 | loop fusion | flops 4194304 | bytes 8978432 | tf_op jit(solution)/shard_map/while/body/eval_jaxpr/mul | solution.py:207
  136.2 4.2 copy.98
  140.5 2.4 copy.49
  142.9 6.0 %broadcast_multiply_fusion = f32[256,4,128,16]{2,1,3,0:T(4,128)S(1)} fusion(f32[256,4,16]{1,2,0:T(8,128)} %copy.49, f32[256,4,128]{2,1,0:T(4,128)S(1)} %convert.31), kind=kLoop, calls=%fused_computation.24 | loop fusion | flops 2097152 | bytes 8978432 | tf_op jit(solution)/shard_map/while/body/eval_jaxpr/bhj,bhd->bjhd/dot_general | solution.py:210
  148.8 4.2 copy.97
  153.0 37.3 %scatter_custom_fusion.2 = f32[768,1024]{1,0:T(8,128)} fusion(s32[4096]{0:T(1024)} %bitcast.145, f32[4096,512]{1,0:T(8,128)} %bitcast.128, f32[]{:T(128)} %constant.147.clone.1, f32[4096,512]{1,0:T(8,128)} %bitcast.127, f32[]{:T(128)} %constant.132.clone.1), kind=kCustom, calls=%fused_computation.7 | custom fusion | flops 8388608 | bytes 19923968 | tf_op jit(solution)/shard_map/while/body/eval_jaxpr/scatter-add | solution.py:220
  192.6 3.2 collective-permute-start.2
  196.0 2.8 fusion.63
  198.9 8.6 %collective-permute-done.2 = bf16[256,1024]{1,0:T(8,128)(2,1)S(1)} collective-permute-done((bf16[256,1024]{1,0:T(8,128)(2,1)S(1)}, bf16[256,1024]{1,0:T(8,128)(2,1)S(1)}, u32[]{:S(2)}, u32[]{:S(2)}) %collective-permute-start.2) | collective-permute-done | bytes 524320 | tf_op jit(solution)/shard_map/ppermute | solution.py:32
  207.5 10.1 %collective-permute-done.3 = bf16[256,1024]{1,0:T(8,128)(2,1)S(1)} collective-permute-done((bf16[256,1024]{1,0:T(8,128)(2,1)S(1)}, bf16[256,1024]{1,0:T(8,128)(2,1)S(1)}, u32[]{:S(2)}, u32[]{:S(2)}) %collective-permute-start.3) | collective-permute-done | bytes 524320 | tf_op jit(solution)/shard_map/ppermute | solution.py:32
  222.1 3.1 fusion.20
  229.5 5.1 %all-to-all-start.2 = ((bf16[16,17,1024]{2,1,0:T(8,128)(2,1)}), bf16[16,17,1024]{2,1,0:T(8,128)(2,1)S(1)}, u32[]{:S(2)}, u32[]{:S(2)}) async-start(bf16[16,17,1024]{2,1,0:T(8,128)(2,1)} %reshape.294), calls=%async_computation.2 | async-start | bytes 1572864 | tf_op jit(solution)/shard_map/all_to_all | solution.py:268
  234.7 50.3 %all-reduce.1 = (f32[1024]{0:T(1024)S(1)}, f32[1024]{0:T(1024)S(1)}) all-reduce(f32[1024]{0:T(1024)S(1)} %pad_maximum_fusion.4, f32[1024]{0:T(1024)S(1)} %pad_maximum_fusion.5), channel_id=1, replica_groups=mesh['patch'=16,'rep'=2] {'patch','rep'}, use_global_device_ids=true, to_apply=%region_25.26 | all-reduce | flops 2048 | bytes 16384 | tf_op jit(solution)/shard_map/psum | solution.py:248
  288.9 181.6 %all-reduce.5.cloned.1.call-done = (f32[512,1536]{1,0:T(8,128)}, f32[512,512]{1,0:T(8,128)}, f32[512,2048]{1,0:T(8,128)}, f32[2048,512]{1,0:T(8,128)}) async-done(((f32[512,1536]{1,0:T(8,128)}, f32[512,512]{1,0:T(8,128)}, f32[512,2048]{1,0:T(8,128)}, f32[2048,512]{1,0:T(8,128)}), (f32[512,1536]{1,0:T(8,128)}, f32[512,512]{1,0:T(8,128)}, f32[512,2048]{1,0:T(8,128)}, ...) | async-done | bytes 12582928 | tf_op jit(solution)/shard_map/psum | solution.py:248
  470.6 3.9 copy.104
  (200 shorter events, 70.0 us)
Async XLA Ops:
  7.2 103.3 %copy-start = (bf16[512,2048]{1,0:T(8,128)(2,1)S(1)}, bf16[512,2048]{1,0:T(8,128)(2,1)}, u32[]{:S(2)}) copy-start(bf16[512,2048]{1,0:T(8,128)(2,1)} %param.17) | copy-start | bytes 6291460
  7.2 15.7 %copy-start.21 = (f32[32,1024]{1,0:T(8,128)S(1)}, f32[32,1024]{1,0:T(8,128)}, u32[]{:S(2)}) copy-start(f32[32,1024]{1,0:T(8,128)} %param.19) | copy-start | bytes 393220
  7.2 15.7 %copy-start.40 = (f32[32]{0:T(128)S(1)}, f32[32]{0:T(128)}, u32[]{:S(2)}) copy-start(f32[32]{0:T(128)} %param.21) | copy-start | bytes 388
  7.2 15.9 %copy-start.33 = (s32[256,16]{0,1:T(8,128)S(1)}, s32[256,16]{0,1:T(8,128)}, u32[]{:S(2)}) copy-start(s32[256,16]{0,1:T(8,128)} %param.14) | copy-start | bytes 49156
  7.2 16.1 %copy-start.23 = (f32[32,1024]{1,0:T(8,128)S(1)}, f32[32,1024]{1,0:T(8,128)}, u32[]{:S(2)}) copy-start(f32[32,1024]{1,0:T(8,128)} %param.20) | copy-start | bytes 393220
  10.4 15.5 %all-to-all-start = ((s32[16,1,1]{2,1,0:T(1,128)}), s32[16,1,1]{2,1,0:T(1,128)S(1)}, u32[]{:S(2)}, u32[]{:S(2)}) async-start(s32[16,1,1]{2,1,0:T(1,128)} %copy.43), calls=%async_computation | async-start | bytes 16384 | tf_op jit(solution)/shard_map/all_to_all | solution.py:78
  23.1 31.2 %copy-start.29 = (f32[512]{0:T(512)}, f32[512]{0:T(512)S(1)}, u32[]{:S(2)}) copy-start(f32[512]{0:T(512)S(1)} %get-tuple-element.81) | copy-start | bytes 6148
  26.0 24.5 %all-to-all-start.1 = ((bf16[16,17,1024]{2,1,0:T(8,128)(2,1)}), bf16[16,17,1024]{2,1,0:T(8,128)(2,1)S(1)}, u32[]{:S(2)}, u32[]{:S(2)}) async-start(bf16[16,17,1024]{2,1,0:T(8,128)(2,1)} %reshape.284), calls=%async_computation.1 | async-start | bytes 1572864 | tf_op jit(solution)/shard_map/all_to_all | solution.py:71
  31.3 439.3 %all-reduce.5.cloned.1.call-start = ((), (), s32[]{:S(2)}) async-start(), calls=%async_computation.3 | async-start | bytes 25165824 | tf_op jit(solution)/shard_map/psum | solution.py:248
  32.7 21.6 %copy-start.38 = (s32[272]{0:T(512)}, s32[272]{0:T(512)S(1)}, u32[]{:S(2)}) copy-start(s32[272]{0:T(512)S(1)} %fusion.84) | copy-start | bytes 3268
  54.5 10.7 %collective-permute-start = (bf16[256,512]{1,0:T(8,128)(2,1)S(1)}, bf16[256,512]{1,0:T(8,128)(2,1)}, u32[]{:S(2)}, u32[]{:S(2)}) collective-permute-start(bf16[256,512]{1,0:T(8,128)(2,1)S(1)} %fusion.38), channel_id=1, source_target_pairs={{0,2},{2,4},{4,6},{6,8},{8,10},{10,12},{12,14},{14,16},{16,18},{18... | collective-permute-start | bytes 786440 | tf_op jit(solution)/shard_map/ppermute | solution.py:21
  55.1 12.1 %collective-permute-start.1 = (bf16[256,512]{1,0:T(8,128)(2,1)S(1)}, bf16[256,512]{1,0:T(8,128)(2,1)}, u32[]{:S(2)}, u32[]{:S(2)}) collective-permute-start(bf16[256,512]{1,0:T(8,128)(2,1)S(1)} %fusion.38), channel_id=1, source_target_pairs={{2,0},{4,2},{6,4},{8,6},{10,8},{12,10},{14,12},{16,14},{18,16},{20... | collective-permute-start | bytes 786440 | tf_op jit(solution)/shard_map/ppermute | solution.py:23
  93.1 7.9 %copy-start.19 = (bf16[256,4,128,1]{2,3,1,0:T(2,128)(2,1)S(1)}, bf16[256,4,128,1]{2,3,1,0:T(2,128)(2,1)}, u32[]{:S(2)}) copy-start(bf16[256,4,128,1]{2,3,1,0:T(2,128)(2,1)} %reshape.365) | copy-start | bytes 786436
  116.6 5.0 %copy-start.6 = (bf16[256,2,4,8,128]{4,3,2,1,0:T(8,128)(2,1)S(1)}, bf16[256,2,4,8,128]{4,3,2,1,0:T(8,128)(2,1)}, u32[]{:S(2)}) copy-start(bf16[256,2,4,8,128]{4,3,2,1,0:T(8,128)(2,1)} %get-tuple-element.69) | copy-start | bytes 12582916
  190.3 5.5 %copy-start.18 = (f32[256,4,1,128]{3,2,1,0:T(1,128)S(1)}, f32[256,4,1,128]{3,2,1,0:T(1,128)}, u32[]{:S(2)}) copy-start(f32[256,4,1,128]{3,2,1,0:T(1,128)} %fusion.9) | copy-start | bytes 1572868
  192.6 14.9 %collective-permute-start.2 = (bf16[256,1024]{1,0:T(8,128)(2,1)S(1)}, bf16[256,1024]{1,0:T(8,128)(2,1)S(1)}, u32[]{:S(2)}, u32[]{:S(2)}) collective-permute-start(bf16[256,1024]{1,0:T(8,128)(2,1)S(1)} %get-tuple-element.71), channel_id=1, source_target_pairs={{0,30},{2,0},{4,2},{6,4},{8,6},{10,8},{12,10},{14,12},{16,14},{18,... | collective-permute-start | bytes 1572872 | tf_op jit(solution)/shard_map/ppermute | solution.py:32
  195.8 21.8 %collective-permute-start.3 = (bf16[256,1024]{1,0:T(8,128)(2,1)S(1)}, bf16[256,1024]{1,0:T(8,128)(2,1)S(1)}, u32[]{:S(2)}, u32[]{:S(2)}) collective-permute-start(bf16[256,1024]{1,0:T(8,128)(2,1)S(1)} %get-tuple-element.72), channel_id=1, source_target_pairs={{0,2},{2,4},{4,6},{6,8},{8,10},{10,12},{12,14},{14,16},{16,18},{18... | collective-permute-start | bytes 1572872 | tf_op jit(solution)/shard_map/ppermute | solution.py:32
  228.4 6.3 %copy-start.43 = (s32[256]{0:T(256)S(1)}, s32[256]{0:T(256)}, u32[]{:S(2)}) copy-start(s32[256]{0:T(256)} %copy-done.42) | copy-start | bytes 3076
  228.4 6.3 %copy-start.44 = (f32[512]{0:T(512)S(1)}, f32[512]{0:T(512)}, u32[]{:S(2)}) copy-start(f32[512]{0:T(512)} %get-tuple-element.45) | copy-start | bytes 6148
  228.4 6.3 %copy-start.45 = (f32[512]{0:T(512)S(1)}, f32[512]{0:T(512)}, u32[]{:S(2)}) copy-start(f32[512]{0:T(512)} %get-tuple-element.57) | copy-start | bytes 6148
  228.4 56.6 %copy-start.22 = (f32[32,1024]{1,0:T(8,128)S(1)}, f32[32,1024]{1,0:T(8,128)}, u32[]{:S(2)}) copy-start(f32[32,1024]{1,0:T(8,128)} %param.19) | copy-start | bytes 393220
  228.4 56.7 %copy-start.24 = (f32[32,1024]{1,0:T(8,128)S(1)}, f32[32,1024]{1,0:T(8,128)}, u32[]{:S(2)}) copy-start(f32[32,1024]{1,0:T(8,128)} %param.20) | copy-start | bytes 393220
  228.4 57.5 %copy-start.41 = (f32[32]{0:T(128)S(1)}, f32[32]{0:T(128)}, u32[]{:S(2)}) copy-start(f32[32]{0:T(128)} %param.21) | copy-start | bytes 388
  229.5 57.2 %all-to-all-start.2 = ((bf16[16,17,1024]{2,1,0:T(8,128)(2,1)}), bf16[16,17,1024]{2,1,0:T(8,128)(2,1)S(1)}, u32[]{:S(2)}, u32[]{:S(2)}) async-start(bf16[16,17,1024]{2,1,0:T(8,128)(2,1)} %reshape.294), calls=%async_computation.2 | async-start | bytes 1572864 | tf_op jit(solution)/shard_map/all_to_all | solution.py:268
  (32 other events, 87.4 us)
Sparse Core Ops, SparseCore 0:
  221.5 249.0 all-reduce.4
where the time goes:
time: 495 us; the launch traced here: 490 us
  waiting for transfers between devices  222 us (45%)
  local copies, waits for them, and re-layouts  74.3 us (15%)
  other arithmetic  64.3 us (13%)
  blocking collectives  50.3 us (10%)
  matrix products  35.6 us (7%)
  starting transfers between devices  27.8 us (6%)
  between operations  15.4 us (3%)
    psum x1, waiting for transfers between devices, local(): lax.psum((gradient_proj, gradient_out, gradient_up, gradient_down, coeff_...  182 us
    psum x1, blocking collectives, local(): lax.psum((gradient_proj, gradient_out, gradient_up, gradient_down, coeff_...  50.3 us
    scatter-add x1, other arithmetic, backward_block(): table_grad = table_grad.at[index_block.reshape(-1)].add(pair_grad)  37.3 us
    unnamed x102, local copies, waits for them, and re-layouts  31.4 us
    gather x1, local copies, waits for them, and re-layouts, gather_block(): gathered = kv_table[index_block]  22.5 us
    ppermute x2, waiting for transfers between devices, from_behind(): lax.ppermute(array, axis, [(i, (i + by) % size) for i in range(size)])  18.7 us
    all_to_all x1, waiting for transfers between devices, local(): lax.all_to_all(outgoing.reshape(patch_count, capacity, 2 * feature_width)...  17.8 us
  transfers between devices with their start and end apart: 8, of which 6 were waited for; matrix products, arithmetic and copies ran while one was open for 5% of the time, Pallas kernels for 0%

commit v1 on v0

v1 whole, which is shorter than its diff:
```python
import jax
import jax.numpy as jnp
from jax import lax
from jax.sharding import PartitionSpec as P

H = 4
HD = 128
NORM_EPS = 1e-05
F32 = jnp.float32
BF16 = jnp.bfloat16


def norm_parts(v):
    centred = v - jnp.mean(v, axis=-1, keepdims=True)
    inverse = lax.rsqrt(jnp.mean(centred * centred, axis=-1, keepdims=True) + NORM_EPS)
    return centred * inverse, inverse


def norm_back(grad, plain, inverse, coeffs):
    width = plain.shape[-1]
    scaled = grad * (1.0 + coeffs[:width])
    inner = (
        scaled
        - jnp.mean(scaled, axis=-1, keepdims=True)
        - plain * jnp.mean(scaled * plain, axis=-1, keepdims=True)
    )
    coeff_grad = jnp.concatenate([jnp.sum(grad * plain, axis=0), jnp.sum(grad, axis=0)])
    return inverse * inner, coeff_grad


def dot(a, b, ca, cb):
    return lax.dot_general(a, b, (((ca,), (cb,)), ((), ())), preferred_element_type=F32)


def local(tokens, cotangent, dest, neighbours, w_qkv, w_out, w_up, w_down, ada_attn, ada_mlp, cond):
    highest = lax.Precision.HIGHEST
    rows, width = tokens.shape
    patches = lax.axis_size("patch")
    groups = lax.axis_size("rep")
    cap = rows // patches + 1
    me = lax.axis_index("patch")

    def from_side(array, by):
        return lax.ppermute(array, "patch", [(i, (i + by) % patches) for i in range(patches)])

    hot = dest[None, :] == jnp.arange(patches, dtype=jnp.int32)[:, None]
    hot_low = hot.astype(BF16)
    before = jnp.arange(rows)[:, None] < jnp.arange(rows)[None, :]
    earlier = dot(hot_low, before.astype(BF16), 1, 0)
    rank = jnp.sum(jnp.where(hot, earlier, 0.0), axis=0).astype(jnp.int32)
    slot = dest * cap + rank
    counts = jnp.sum(hot.astype(jnp.int32), axis=1)
    pick_out = (slot[None, :] == jnp.arange(patches * cap, dtype=jnp.int32)[:, None]).astype(BF16)
    outgoing = dot(pick_out, jnp.concatenate([tokens, cotangent], axis=1), 1, 0).astype(BF16)
    arrived = lax.all_to_all(
        outgoing.reshape(patches, cap, 2 * width), "patch", split_axis=0, concat_axis=0, tiled=True
    ).reshape(patches * cap, 2 * width)
    counts_in = lax.all_to_all(counts[:, None], "patch", split_axis=0, concat_axis=0, tiled=True)[:, 0]
    lower = jnp.arange(patches)[:, None] > jnp.arange(patches)[None, :]
    offsets = jnp.sum(jnp.where(lower, counts_in[None, :], 0), axis=1)
    step = jnp.arange(cap, dtype=jnp.int32)
    place = jnp.where(step[None, :] < counts_in[:, None], offsets[:, None] + step[None, :], rows).reshape(-1)
    pick_in = (place[None, :] == jnp.arange(rows, dtype=jnp.int32)[:, None]).astype(BF16)
    placed = dot(pick_in, arrived, 1, 0)
    x = placed[:, :width]
    upstream = placed[:, width:].astype(BF16)

    c1 = jnp.dot(cond, ada_attn, precision=highest)
    c2 = jnp.dot(cond, ada_mlp, precision=highest)
    plain1, inv1 = norm_parts(x)
    normed = (plain1 * (1.0 + c1[:width]) + c1[width:]).astype(BF16)
    sides = jnp.concatenate([from_side(normed, 1), normed, from_side(normed, -1)], axis=0)
    qkv = dot(sides, w_qkv, 1, 0).astype(BF16)
    q_all, k_all, v_all = qkv[:, :width], qkv[:, width : 2 * width], qkv[:, 2 * width :]

    owner = neighbours // (rows * groups)
    within = neighbours % rows
    rel = (owner - me + 1 + patches) % patches
    column = (rel * rows + within).T
    column_before, column_after = from_side(column, 1), from_side(column, -1)
    ids = jnp.arange(3 * rows, dtype=jnp.int32)
    counts_q = jnp.sum((column.T[:, :, None] == ids[None, None, :]).astype(F32), axis=1)
    mine = jnp.arange(rows, dtype=jnp.int32)

    def by_key(col, at):
        return jnp.sum((col[:, None, :] == (mine + at * rows)[None, :, None]).astype(F32), axis=0)

    counts_k = jnp.concatenate([by_key(column_before, 2), by_key(column, 1), by_key(column_after, 0)], axis=1)

    scale = 1.0 / HD**0.5
    q = q_all[rows : 2 * rows]
    k = k_all[rows : 2 * rows]
    v = v_all[rows : 2 * rows]
    weights_all, heads, logs = [], [], []
    for h in range(H):
        c = slice(h * HD, (h + 1) * HD)
        s = dot(q[:, c], k_all[:, c], 1, 1) * scale
        s = jnp.where(counts_q > 0, s, -1e30)
        top = jnp.max(s, axis=-1, keepdims=True)
        e = jnp.exp(s - top)
        total = jnp.sum(e * counts_q, axis=-1, keepdims=True)
        p = e / total
        weights_all.append(p * counts_q)
        heads.append(dot((p * counts_q).astype(BF16), v_all[:, c], 1, 0))
        logs.append(top + jnp.log(total))
    o = jnp.concatenate(heads, axis=1).astype(BF16)

    resid = x + dot(o, w_out, 1, 0)
    plain2, inv2 = norm_parts(resid)
    normed2 = (plain2 * (1.0 + c2[:width]) + c2[width:]).astype(BF16)
    u = dot(normed2, w_up, 1, 0)
    sig = jax.nn.sigmoid(u)
    a = (u * sig).astype(BF16)
    y = (resid + dot(a, w_down, 1, 0)).astype(BF16)
    grad_down = dot(a, upstream, 0, 0)
    ga = dot(upstream, w_down, 1, 1)
    gu = (ga * sig * (1.0 + u * (1.0 - sig))).astype(BF16)
    grad_up = dot(normed2, gu, 0, 0)
    gn2 = dot(gu, w_up, 1, 1)
    gw2, gc2 = norm_back(gn2, plain2, inv2, c2)
    gresid = upstream.astype(F32) + gw2
    gr = gresid.astype(BF16)
    grad_out = dot(o, gr, 0, 0)
    go = dot(gr, w_out, 1, 1).astype(BF16)

    gq, deltas = [], []
    for h in range(H):
        c = slice(h * HD, (h + 1) * HD)
        gp = dot(go[:, c], v_all[:, c], 1, 1)
        delta = jnp.sum(weights_all[h] * gp, axis=-1, keepdims=True)
        gs = (weights_all[h] * (gp - delta)).astype(BF16)
        gq.append(dot(gs, k_all[:, c], 1, 0) * scale)
        deltas.append(delta)
    stats = jnp.concatenate(logs + deltas, axis=1).T
    go_all = jnp.concatenate([from_side(go, 1), go, from_side(go, -1)], axis=0)
    stats_all = jnp.concatenate([from_side(stats, 1), stats, from_side(stats, -1)], axis=1)
    gk, gv = [], []
    for h in range(H):
        c = slice(h * HD, (h + 1) * HD)
        s = dot(k[:, c], q_all[:, c], 1, 1) * scale
        s = jnp.where(counts_k > 0, s, -1e30)
        w = jnp.exp(s - stats_all[h : h + 1]) * counts_k
        gp = dot(v[:, c], go_all[:, c], 1, 1)
        gs = (w * (gp - stats_all[H + h : H + h + 1])).astype(BF16)
        gk.append(dot(gs, q_all[:, c], 1, 0) * scale)
        gv.append(dot(w.astype(BF16), go_all[:, c], 1, 0))
    gqkv = jnp.concatenate(gq + gk + gv, axis=1).astype(BF16)
    grad_qkv = dot(normed, gqkv, 0, 0)
    gn1 = dot(gqkv, w_qkv, 1, 1)
    gw1, gc1 = norm_back(gn1, plain1, inv1, c1)
    gx = (gresid + gw1).astype(BF16)

    both = ("patch", "rep")
    grad_down, grad_up, grad_out, grad_qkv = (
        lax.psum(g.astype(BF16), both).astype(F32) for g in (grad_down, grad_up, grad_out, grad_qkv)
    )
    gc1, gc2 = lax.psum((gc1, gc2), both)
    grad_ada_attn = jnp.outer(cond, gc1)
    grad_ada_mlp = jnp.outer(cond, gc2)
    grad_cond = jnp.dot(ada_attn, gc1, precision=highest) + jnp.dot(ada_mlp, gc2, precision=highest)

    leaving = dot(pick_in, jnp.concatenate([y, gx], axis=1), 0, 0).astype(BF16)
    home = lax.all_to_all(
        leaving.reshape(patches, cap, 2 * width), "patch", split_axis=0, concat_axis=0, tiled=True
    ).reshape(patches * cap, 2 * width)
    band = dot(pick_out, home, 0, 0).astype(BF16)
    return (
        band[:, :width],
        band[:, width:],
        grad_qkv,
        grad_out,
        grad_up,
        grad_down,
        grad_ada_attn,
        grad_ada_mlp,
        grad_cond,
    )


def solution(mesh):
    row = P(("patch", "rep"), None)
    return jax.shard_map(
        local,
        mesh=mesh,
        in_specs=(row, row, P(("patch", "rep")), row) + (P(),) * 7,
        out_specs=(row, row) + (P(),) * 7,
        check_vma=False,
    )
```

time: 495 us -> 332 us (0.67)
  waiting for transfers between devices: 222 us -> 127 us
  local copies, waits for them, and re-layouts: 74.3 us -> 9.9 us
  other arithmetic: 64.3 us -> 31.1 us
  matrix products: 35.6 us -> 60.5 us
  starting transfers between devices: 27.8 us -> 39 us
    psum x1, waiting for transfers between devices: 182 us -> 110 us  [local(): lax.psum(g.astype(BF16), both).astype(F32)]
    scatter-add x1 -> x0, other arithmetic: 37.3 us -> none  [backward_block(): table_grad = table_grad.at[index_block.reshape(-1)].add(pair_grad)]
    unnamed x102 -> x128, local copies, waits for them, and re-layouts: 31.4 us -> 2.29 us
    gather x3 -> x0, local copies, waits for them, and re-layouts: 25.7 us -> none  [the longest x1 22.5 us: gather_block(): gathered = kv_table[index_block]]
    dot_general x21 -> x49, matrix products: 35.6 us -> 60.5 us  [the longest x45 57.3 us: dot(): lax.dot_general(a, b, (((ca,), (cb,)), ((), ())), preferred_element_type=...]
    ppermute x4 -> x8, waiting for transfers between devices: 20.8 us -> 7.82 us  [from_side(): lax.ppermute(array, 'patch', [(i, (i + by) % patches) for i in range(patc...]
    reduce_sum x3 -> x8, other arithmetic: 1.03 us -> 13.4 us  [the longest x1 7.87 us: local(): jnp.sum((column.T[:, :, None] == ids[None, None, :]).astype(F32), axis=1)]
    all_to_all x3, waiting for transfers between devices: 19.4 us -> 8.81 us  [the longest x1 8.66 us: local(): lax.all_to_all(outgoing.reshape(patches, cap, 2 * width), 'patch', split_...]
  transfers between devices with their start and end apart: 8 -> 12, of which waited for: 6 -> 5; matrix products, arithmetic and copies ran while one was open for 5% -> 15% of each run, Pallas kernels for 0% -> 0%
where the time goes in v1:
time: 332 us; the launch traced here: 331 us
  waiting for transfers between devices  127 us (38%)
  matrix products  60.5 us (18%)
  blocking collectives  48.7 us (15%)
  starting transfers between devices  39 us (12%)
  other arithmetic  31.1 us (9%)
  between operations  14.9 us (4%)
  local copies, waits for them, and re-layouts  9.9 us (3%)
    psum x1, waiting for transfers between devices, local(): lax.psum(g.astype(BF16), both).astype(F32)  110 us
    dot_general x45, matrix products, dot(): lax.dot_general(a, b, (((ca,), (cb,)), ((), ())), preferred_element_type=...  57.3 us
    psum x1, blocking collectives, local(): gc1, gc2 = lax.psum((gc1, gc2), both)  48.7 us
    ppermute x8, starting transfers between devices, from_side(): lax.ppermute(array, 'patch', [(i, (i + by) % patches) for i in range(patc...  18.1 us
    convert_element_type x4, other arithmetic, local(): lax.psum(g.astype(BF16), both).astype(F32)  9.88 us
    all_to_all x1, waiting for transfers between devices, local(): lax.all_to_all(outgoing.reshape(patches, cap, 2 * width), 'patch', split_...  8.66 us
    reduce_sum x1, other arithmetic, local(): jnp.sum((column.T[:, :, None] == ids[None, None, :]).astype(F32), axis=1)  7.87 us
    ppermute x8, waiting for transfers between devices, from_side(): lax.ppermute(array, 'patch', [(i, (i + by) % patches) for i in range(patc...  7.82 us
  transfers between devices with their start and end apart: 12, of which 5 were waited for; matrix products, arithmetic and copies ran while one was open for 15% of the time, Pallas kernels for 0%

profile of v1, /device:TPU:0, one launch (start us, length us, event | category | flops | bytes accessed | tf_op | source)
XLA Modules:
  0.0 330.6 jit_solution(17798290362266124096)
XLA Ops:
  8.1 7.0 %collective-permute-start.3 = (s32[16,256]{1,0:T(8,128)S(1)}, s32[16,256]{1,0:T(8,128)S(1)}, u32[]{:S(2)}, u32[]{:S(2)}) collective-permute-start(s32[16,256]{1,0:T(8,128)S(1)} %fusion.200), channel_id=1, source_target_pairs={{0,30},{2,0},{4,2},{6,4},{8,6},{10,8},{12,10},{14,12},{16,14},{18,... | collective-permute-start | bytes 49160 | tf_op jit(solution)/shard_map/ppermute | solution.py:44
  16.6 7.0 %all-to-all-start = ((s32[16,1,1]{2,1,0:T(1,128)}), s32[16,1,1]{2,1,0:T(1,128)S(1)}, u32[]{:S(2)}, u32[]{:S(2)}) async-start(s32[16,1,1]{2,1,0:T(1,128)} %copy.26), calls=%async_computation | async-start | bytes 16384 | tf_op jit(solution)/shard_map/all_to_all | solution.py:58
  30.8 6.8 %all-to-all-start.1 = ((bf16[16,17,1024]{2,1,0:T(8,128)(2,1)}), bf16[16,17,1024]{2,1,0:T(8,128)(2,1)}, u32[]{:S(2)}, u32[]{:S(2)}) async-start(bf16[16,17,1024]{2,1,0:T(8,128)(2,1)} %reshape.213), calls=%async_computation.1 | async-start | bytes 1572864 | tf_op jit(solution)/shard_map/all_to_all | solution.py:55
  38.9 7.9 %convert_reduce_fusion = f32[256,768]{1,0:T(8,128)S(1)} fusion(s32[256,16]{1,0:T(8,128)S(1)} %copy.27), kind=kLoop, calls=%fused_computation | loop fusion | flops 9240576 | bytes 802816 | tf_op jit(solution)/shard_map/reduce_sum | solution.py:82
  47.6 8.7 %all-to-all-done.1 = bf16[16,17,1024]{2,1,0:T(8,128)(2,1)} async-done(((bf16[16,17,1024]{2,1,0:T(8,128)(2,1)}), bf16[16,17,1024]{2,1,0:T(8,128)(2,1)}, u32[]{:S(2)}, u32[]{:S(2)}) %all-to-all-start.1) | async-done | bytes 557088 | tf_op jit(solution)/shard_map/all_to_all | solution.py:55
  56.3 2.1 reshape.214
  60.6 3.6 %collective-permute-start.1 = (bf16[256,512]{1,0:T(8,128)(2,1)S(1)}, bf16[256,512]{1,0:T(8,128)(2,1)S(1)}, u32[]{:S(2)}, u32[]{:S(2)}) collective-permute-start(bf16[256,512]{1,0:T(8,128)(2,1)S(1)} %add_convert_fusion.2), channel_id=1, source_target_pairs={{0,30},{2,0},{4,2},{6,4},{8,6},{10,8},{12,10},{14,12},{16,14},{18,... | collective-permute-start | bytes 786440 | tf_op jit(solution)/shard_map/ppermute | solution.py:44
  68.6 5.8 %collective-permute-done = bf16[256,512]{1,0:T(8,128)(2,1)S(1)} collective-permute-done((bf16[256,512]{1,0:T(8,128)(2,1)S(1)}, bf16[256,512]{1,0:T(8,128)(2,1)S(1)}, u32[]{:S(2)}, u32[]{:S(2)}) %collective-permute-start) | collective-permute-done | bytes 262176 | tf_op jit(solution)/shard_map/ppermute | solution.py:44
  98.6 5.5 %collective-permute-start.7 = (bf16[256,512]{1,0:T(8,128)(2,1)}, bf16[256,512]{1,0:T(8,128)(2,1)S(1)}, u32[]{:S(2)}, u32[]{:S(2)}) collective-permute-start(bf16[256,512]{1,0:T(8,128)(2,1)} %copy-done.22), channel_id=1, source_target_pairs={{0,30},{2,0},{4,2},{6,4},{8,6},{10,8},{12,10},{14,12},{16,14},{18,... | collective-permute-start | bytes 786440 | tf_op jit(solution)/shard_map/ppermute | solution.py:44
  104.1 3.4 %convolution_convert_fusion.2 = bf16[512,2048]{1,0:T(8,128)(2,1)} fusion(bf16[256,2048]{1,0:T(8,128)(2,1)} %copy-done.30, f32[256,512]{1,0:T(8,128)S(1)} %get-tuple-element.56, f32[512]{0:T(512)S(1)} %get-tuple-element.42, f32[512]{0:T(512)S(1)} %get-tuple-element.41, f32[256]{0:T(256)S(1)} %add_rsqrt_fusion, f32[256]{0:T(256)S(1)} %broadcast_multiply_fusion.6), kind=kOutput, calls=%fused_computation.8 | convolution fusion | flops 538574848 | bytes 3676160 | tf_op jit(solution)/shard_map/dot_general | solution.py:32
  107.6 2.2 convolution_convert_fusion.1
  120.7 2.3 fusion.46
  123.0 2.3 fusion.44
  125.2 2.3 fusion.42
  127.5 2.3 fusion.40
  129.8 2.2 fusion.55
  135.9 2.9 convolution_convert_fusion.3
  138.9 3.1 fusion.30
  144.9 7.0 %all-to-all-start.2 = ((bf16[16,17,1024]{2,1,0:T(8,128)(2,1)}), bf16[16,17,1024]{2,1,0:T(8,128)(2,1)S(1)}, u32[]{:S(2)}, u32[]{:S(2)}) async-start(bf16[16,17,1024]{2,1,0:T(8,128)(2,1)} %reshape.215), calls=%async_computation.2 | async-start | bytes 1572864 | tf_op jit(solution)/shard_map/all_to_all | solution.py:163
  151.9 48.7 %all-reduce = (f32[1024]{0:T(1024)S(1)}, f32[1024]{0:T(1024)S(1)}) all-reduce(f32[1024]{0:T(1024)S(1)} %pad_maximum_fusion.6, f32[1024]{0:T(1024)S(1)} %pad_maximum_fusion.7), channel_id=1, replica_groups=mesh['patch'=16,'rep'=2] {'patch','rep'}, use_global_device_ids=true, to_apply=%region_33.34 | all-reduce | flops 2048 | bytes 16384 | tf_op jit(solution)/shard_map/psum | solution.py:157
  203.9 109.9 %all-reduce.4.cloned.1.call-done = (bf16[512,1536]{1,0:T(8,128)(2,1)}, bf16[512,512]{1,0:T(8,128)(2,1)}, bf16[512,2048]{1,0:T(8,128)(2,1)}, bf16[2048,512]{1,0:T(8,128)(2,1)}) async-done(((bf16[512,1536]{1,0:T(8,128)(2,1)}, bf16[512,512]{1,0:T(8,128)(2,1)}, bf16[512,2048]{1,0:T(8,128)(2,1)}, bf16[2048,512]{1,0:T(8,128)(2,1)}), (bf16[512,1536]{1,0:T(8,128)(2,1)}, bf16[512,512]{1,0:T(8,128)(2,1)}, ...) | async-done | bytes 6291472 | tf_op jit(solution)/shard_map/psum | solution.py:155
  313.9 3.6 %convert_element_type.172 = f32[512,1536]{1,0:T(8,128)} convert(bf16[512,1536]{1,0:T(8,128)(2,1)} %get-tuple-element.31) | non-fusion elementwise | flops 786432 | bytes 4718592 | tf_op jit(solution)/shard_map/convert_element_type | solution.py:155
  318.6 2.5 convert_element_type.176
  321.1 2.6 convert_element_type.178
  (231 shorter events, 64.0 us)
Async XLA Ops:
  7.2 75.0 %copy-start = (bf16[512,2048]{1,0:T(8,128)(2,1)S(1)}, bf16[512,2048]{1,0:T(8,128)(2,1)}, u32[]{:S(2)}) copy-start(bf16[512,2048]{1,0:T(8,128)(2,1)} %param.17) | copy-start | bytes 6291460
  8.1 56.1 %collective-permute-start.3 = (s32[16,256]{1,0:T(8,128)S(1)}, s32[16,256]{1,0:T(8,128)S(1)}, u32[]{:S(2)}, u32[]{:S(2)}) collective-permute-start(s32[16,256]{1,0:T(8,128)S(1)} %fusion.200), channel_id=1, source_target_pairs={{0,30},{2,0},{4,2},{6,4},{8,6},{10,8},{12,10},{14,12},{16,14},{18,... | collective-permute-start | bytes 49160 | tf_op jit(solution)/shard_map/ppermute | solution.py:44
  15.1 50.3 %collective-permute-start.2 = (s32[16,256]{1,0:T(8,128)S(1)}, s32[16,256]{1,0:T(8,128)S(1)}, u32[]{:S(2)}, u32[]{:S(2)}) collective-permute-start(s32[16,256]{1,0:T(8,128)S(1)} %fusion.200), channel_id=1, source_target_pairs={{0,2},{2,4},{4,6},{6,8},{8,10},{10,12},{12,14},{14,16},{16,18},{18... | collective-permute-start | bytes 49160 | tf_op jit(solution)/shard_map/ppermute | solution.py:44
  16.6 14.2 %all-to-all-start = ((s32[16,1,1]{2,1,0:T(1,128)}), s32[16,1,1]{2,1,0:T(1,128)S(1)}, u32[]{:S(2)}, u32[]{:S(2)}) async-start(s32[16,1,1]{2,1,0:T(1,128)} %copy.26), calls=%async_computation | async-start | bytes 16384 | tf_op jit(solution)/shard_map/all_to_all | solution.py:58
  26.4 34.1 %copy-start.44 = (f32[512]{0:T(512)}, f32[512]{0:T(512)S(1)}, u32[]{:S(2)}) copy-start(f32[512]{0:T(512)S(1)} %get-tuple-element.43) | copy-start | bytes 6148
  27.1 19.7 %copy-start.57 = (s32[256]{0:T(256)}, s32[256]{0:T(256)S(1)}, u32[]{:S(2)}) copy-start(s32[256]{0:T(256)S(1)} %convert_add_fusion) | copy-start | bytes 3076
  30.8 25.5 %all-to-all-start.1 = ((bf16[16,17,1024]{2,1,0:T(8,128)(2,1)}), bf16[16,17,1024]{2,1,0:T(8,128)(2,1)}, u32[]{:S(2)}, u32[]{:S(2)}) async-start(bf16[16,17,1024]{2,1,0:T(8,128)(2,1)} %reshape.213), calls=%async_computation.1 | async-start | bytes 1572864 | tf_op jit(solution)/shard_map/all_to_all | solution.py:55
  37.6 276.3 %all-reduce.4.cloned.1.call-start = ((), (), s32[]{:S(2)}) async-start(), calls=%async_computation.3 | async-start | bytes 12582912 | tf_op jit(solution)/shard_map/psum | solution.py:155
  46.8 30.5 %copy-start.7 = (f32[256,768]{1,0:T(8,128)}, f32[256,768]{1,0:T(8,128)S(1)}, u32[]{:S(2)}) copy-start(f32[256,768]{1,0:T(8,128)S(1)} %convert_reduce_fusion) | copy-start | bytes 2359300
  58.4 16.0 %copy-start.62 = (bf16[512,1536]{1,0:T(8,128)(2,1)S(1)}, bf16[512,1536]{1,0:T(8,128)(2,1)}, u32[]{:S(2)}) copy-start(bf16[512,1536]{1,0:T(8,128)(2,1)} %param.15) | copy-start | bytes 4718596
  60.0 26.5 %copy-start.8 = (f32[256,1024]{1,0:T(8,128)}, f32[256,1024]{1,0:T(8,128)S(1)}, u32[]{:S(2)}) copy-start(f32[256,1024]{1,0:T(8,128)S(1)} %fusion.88) | copy-start | bytes 3145732
  60.2 15.6 %copy-start.46 = (f32[256]{0:T(256)}, f32[256]{0:T(256)S(1)}, u32[]{:S(2)}) copy-start(f32[256]{0:T(256)S(1)} %broadcast_multiply_fusion.7) | copy-start | bytes 3076
  60.6 8.0 %collective-permute-start.1 = (bf16[256,512]{1,0:T(8,128)(2,1)S(1)}, bf16[256,512]{1,0:T(8,128)(2,1)S(1)}, u32[]{:S(2)}, u32[]{:S(2)}) collective-permute-start(bf16[256,512]{1,0:T(8,128)(2,1)S(1)} %add_convert_fusion.2), channel_id=1, source_target_pairs={{0,30},{2,0},{4,2},{6,4},{8,6},{10,8},{12,10},{14,12},{16,14},{18,... | collective-permute-start | bytes 786440 | tf_op jit(solution)/shard_map/ppermute | solution.py:44
  64.2 10.2 %collective-permute-start = (bf16[256,512]{1,0:T(8,128)(2,1)S(1)}, bf16[256,512]{1,0:T(8,128)(2,1)S(1)}, u32[]{:S(2)}, u32[]{:S(2)}) collective-permute-start(bf16[256,512]{1,0:T(8,128)(2,1)S(1)} %add_convert_fusion.2), channel_id=1, source_target_pairs={{0,2},{2,4},{4,6},{6,8},{8,10},{10,12},{12,14},{14,16},{16,18},{18... | collective-permute-start | bytes 786440 | tf_op jit(solution)/shard_map/ppermute | solution.py:44
  75.8 16.5 %copy-start.11 = (bf16[768,1536]{1,0:T(8,128)(2,1)}, bf16[768,1536]{1,0:T(8,128)(2,1)S(1)}, u32[]{:S(2)}) copy-start(bf16[768,1536]{1,0:T(8,128)(2,1)S(1)} %convolution_convert_fusion) | copy-start | bytes 7077892
  96.5 19.0 %collective-permute-start.5 = (f32[8,256]{1,0:T(8,128)}, f32[8,256]{1,0:T(8,128)S(1)}, u32[]{:S(2)}, u32[]{:S(2)}) collective-permute-start(f32[8,256]{1,0:T(8,128)} %bitcast.49), channel_id=1, source_target_pairs={{0,30},{2,0},{4,2},{6,4},{8,6},{10,8},{12,10},{14,12},{16,14},{18,... | collective-permute-start | bytes 24584 | tf_op jit(solution)/shard_map/ppermute | solution.py:44
  98.5 17.0 %collective-permute-start.4 = (f32[8,256]{1,0:T(8,128)}, f32[8,256]{1,0:T(8,128)S(1)}, u32[]{:S(2)}, u32[]{:S(2)}) collective-permute-start(f32[8,256]{1,0:T(8,128)} %bitcast.50), channel_id=1, source_target_pairs={{0,2},{2,4},{4,6},{6,8},{8,10},{10,12},{12,14},{14,16},{16,18},{18... | collective-permute-start | bytes 24584 | tf_op jit(solution)/shard_map/ppermute | solution.py:44
  98.6 22.0 %collective-permute-start.7 = (bf16[256,512]{1,0:T(8,128)(2,1)}, bf16[256,512]{1,0:T(8,128)(2,1)S(1)}, u32[]{:S(2)}, u32[]{:S(2)}) collective-permute-start(bf16[256,512]{1,0:T(8,128)(2,1)} %copy-done.22), channel_id=1, source_target_pairs={{0,30},{2,0},{4,2},{6,4},{8,6},{10,8},{12,10},{14,12},{16,14},{18,... | collective-permute-start | bytes 786440 | tf_op jit(solution)/shard_map/ppermute | solution.py:44
  104.1 16.5 %collective-permute-start.6 = (bf16[256,512]{1,0:T(8,128)(2,1)}, bf16[256,512]{1,0:T(8,128)(2,1)S(1)}, u32[]{:S(2)}, u32[]{:S(2)}) collective-permute-start(bf16[256,512]{1,0:T(8,128)(2,1)} %copy-done.22), channel_id=1, source_target_pairs={{0,2},{2,4},{4,6},{6,8},{8,10},{10,12},{12,14},{14,16},{16,18},{18... | collective-permute-start | bytes 786440 | tf_op jit(solution)/shard_map/ppermute | solution.py:44
  143.4 57.2 %copy-start.34 = (f32[32,1024]{1,0:T(8,128)S(1)}, f32[32,1024]{1,0:T(8,128)}, u32[]{:S(2)}) copy-start(f32[32,1024]{1,0:T(8,128)} %param.19) | copy-start | bytes 393220
  143.4 57.4 %copy-start.35 = (f32[32,1024]{1,0:T(8,128)S(1)}, f32[32,1024]{1,0:T(8,128)}, u32[]{:S(2)}) copy-start(f32[32,1024]{1,0:T(8,128)} %param.20) | copy-start | bytes 393220
  143.4 58.2 %copy-start.56 = (f32[32]{0:T(128)S(1)}, f32[32]{0:T(128)}, u32[]{:S(2)}) copy-start(f32[32]{0:T(128)} %param.21) | copy-start | bytes 388
  143.8 58.8 %copy-start.58 = (s32[256]{0:T(256)S(1)}, s32[256]{0:T(256)}, u32[]{:S(2)}) copy-start(s32[256]{0:T(256)} %copy-done.57) | copy-start | bytes 3076
  144.9 57.5 %all-to-all-start.2 = ((bf16[16,17,1024]{2,1,0:T(8,128)(2,1)}), bf16[16,17,1024]{2,1,0:T(8,128)(2,1)S(1)}, u32[]{:S(2)}, u32[]{:S(2)}) async-start(bf16[16,17,1024]{2,1,0:T(8,128)(2,1)} %reshape.215), calls=%async_computation.2 | async-start | bytes 1572864 | tf_op jit(solution)/shard_map/all_to_all | solution.py:163
  (52 other events, 230.9 us)
Sparse Core Ops, SparseCore 0:
  139.0 174.8 all-reduce.3

commit v2 on v1

v2 whole, which is shorter than its diff:
```python
import functools
import types

import jax
import jax.numpy as jnp
from jax import lax
from jax.experimental import pallas as pl
from jax.experimental.pallas import tpu as pltpu
from jax.sharding import PartitionSpec as P

H = 4
HD = 128
EPS = 1e-05
F32 = jnp.float32
BF16 = jnp.bfloat16
I32 = jnp.int32
MESH = pl.DeviceIdType.MESH
NN = (((1,), (0,)), ((), ()))
NT = (((1,), (1,)), ((), ()))
TN = (((0,), (0,)), ((), ()))
TILE = 32
PARTS = 4
BLOCK = (512, 256)
MIN_ROWS = 16


def mm(a, b, dims=NN):
    return lax.dot_general(a, b, dims, preferred_element_type=F32)


def iota(shape, axis):
    return lax.broadcasted_iota(I32, shape, axis).astype(F32)


def hot(cond):
    return jnp.where(cond, 1.0, 0.0)


def sizes(patches, rows, width, hidden):
    cap = rows // patches + 1
    block = -(-(cap + 1) // 16) * 16
    bits = patches.bit_length() - 1
    halvings = 0
    while halvings < bits and BLOCK[0] >> (halvings + 1) >= MIN_ROWS:
        halvings += 1
    return types.SimpleNamespace(
        P=patches, R=rows, D=width, FF=hidden, cap=cap, T=block, PT=patches * block, bits=bits, halvings=halvings
    )


def bit_orders(bits):
    first = [(0, 1, 2), (1, 2, 0), (2, 0, 1), (1, 0, 2)]
    return [tuple(b for b in f if b < bits) + tuple(range(3, bits)) for f in first]


def scratch(z, nb):
    R, D, FF, PT = z.R, z.D, z.FF, z.PT
    recv_rows = []
    for k in range(z.bits):
        recv_rows.append(BLOCK[0] >> (min(k + 1, z.halvings)))
    vm, dma = pltpu.VMEM, pltpu.SemaphoreType.DMA
    s = dict(
        tok=vm((R, D), BF16),
        cot=vm((R, D), BF16),
        wqkv=vm((D, 3 * D), BF16),
        wout=vm((D, D), BF16),
        wup=vm((D, FF), BF16),
        wdown=vm((FF, D), BF16),
        ada1=vm((32, 2 * D), F32),
        ada2=vm((32, 2 * D), F32),
        c=vm((16, 2 * D), F32),
        pick=vm((R, PT), BF16),
        place=vm((PT, R), BF16),
        out_t=vm((PT, D), BF16),
        out_c=vm((PT, D), BF16),
        in_t=vm((PT, D), BF16),
        in_c=vm((PT, D), BF16),
        home_y=vm((PT, D), BF16),
        home_g=vm((PT, D), BF16),
        x=vm((R, D), F32),
        plain1=vm((R, D), F32),
        inv1=vm((R, 128), F32),
        plain2=vm((R, D), F32),
        inv2=vm((R, 128), F32),
        resid=vm((R, D), F32),
        gresid=vm((R, D), F32),
        tmp=vm((R, D), F32),
        ups=vm((2, R, D), BF16),
        normed=vm((3, R, D), BF16),
        normed_p=vm((R, D), BF16),
        qkv=vm((3, R, 3 * D), BF16),
        cols=vm((3, nb, R), F32),
        colq=vm((R, nb), F32),
        cq=vm((R, 3 * R), F32),
        ck=vm((3, R, R), F32),
        s=vm((R, 3 * R), F32),
        s2=vm((R, 3 * R), F32),
        w=vm((H, R, 3 * R), F32),
        low=vm((R, 3 * R), BF16),
        low2=vm((R, 3 * R), BF16),
        o=vm((2, R, D), BF16),
        u=vm((R, D), F32),
        ga=vm((R, FF), F32),
        a=vm((R, FF), BF16),
        a_p=vm((R, FF // 2), BF16),
        gu=vm((R, FF), BF16),
        gu_p=vm((R, FF // 2), BF16),
        normed2=vm((2, R, D), BF16),
        gr=vm((R, D), BF16),
        gr_p=vm((R, D // 2), BF16),
        go=vm((3, R, D), BF16),
        stat=vm((R, 128), F32),
        stats=vm((3, 2 * H, R), F32),
        gqkv=vm((R, 3 * D), BF16),
        gqkv_p=vm((R, 3 * D // 2), BF16),
        acc=vm((3, PARTS) + BLOCK, BF16),
        **{f"rcv{k}": vm((3, PARTS, n, BLOCK[1]), BF16) for k, n in enumerate(recv_rows)},
        grads=vm((3, 2, PARTS) + BLOCK, BF16),
        gcs=vm((z.bits + 2, 8, D), F32),
        gcr=vm((z.bits + 1, 8, D), F32),
        load_sem=dma((8,)),
        row_ss=dma((4,)),
        row_rs=dma((4,)),
        own_sem=dma((4,)),
        side_ss=dma((4, 2)),
        side_rs=dma((4, 2)),
        pair_ss=dma((8,)),
        pair_rs=dma((8,)),
        rs_ss=dma((3, z.bits, PARTS)),
        rs_rs=dma((3, z.bits, PARTS)),
        ag_ss=dma((3, z.bits, PARTS)),
        ag_rs=dma((3, z.bits, PARTS)),
        core_ss=dma((3,)),
        core_rs=dma((3,)),
        gc_ss=dma((z.bits + 1,)),
        gc_rs=dma((z.bits + 1,)),
        store_sem=dma((3,)),
    )
    return s


def layer(z, names, *refs):
    n = types.SimpleNamespace(**dict(zip(names, refs, strict=True)))
    Pn, R, D, FF, T, PT, cap = z.P, z.R, z.D, z.FF, z.T, z.PT, z.cap
    me = lax.axis_index("patch")
    rp = lax.axis_index("rep")
    mate = 1 - rp
    nxt = lax.rem(me + 1, Pn)
    prv = lax.rem(me + Pn - 1, Pn)
    started = []

    def tiles(total, fn, init=0, size=TILE):
        return lax.fori_loop(
            0, total // size, lambda i, c: fn(pl.ds(pl.multiple_of(i * size, size), size), c), init
        )

    def load(i, src, dst):
        copy = pltpu.make_async_copy(src, dst, n.load_sem.at[i])
        copy.start()
        return copy

    get_tok = load(0, n.tokens, n.tok)
    get_cot = load(1, n.cotangent, n.cot)
    get_ada1 = load(2, n.ada_attn, n.ada1)
    get_ada2 = load(3, n.ada_mlp, n.ada2)
    get_wqkv = load(4, n.w_qkv, n.wqkv)
    get_wdown = load(5, n.w_down, n.wdown)
    get_wout = load(6, n.w_out, n.wout)
    get_wup = load(7, n.w_up, n.wup)

    barrier = pltpu.get_barrier_semaphore()

    def greet(i, carry):
        pl.semaphore_signal(barrier, inc=1, device_id=(lax.rem(me + i, Pn), rp), device_id_type=MESH)
        return carry

    lax.fori_loop(1, Pn, greet, 0)
    pl.semaphore_signal(barrier, inc=1, device_id=(me, mate), device_id_type=MESH)

    def remote(src, dst, ss, rs, to):
        copy = pltpu.make_async_remote_copy(
            src_ref=src, dst_ref=dst, send_sem=ss, recv_sem=rs, device_id=to, device_id_type=MESH
        )
        copy.start()
        started.append(copy)
        return copy

    def send_rows(i, src, dst):
        def one(j, carry):
            to = lax.rem(me + j, Pn)
            pltpu.make_async_remote_copy(
                src_ref=src.at[pl.ds(pl.multiple_of(to * T, 16), T)],
                dst_ref=dst.at[pl.ds(pl.multiple_of(me * T, 16), T)],
                send_sem=n.row_ss.at[i],
                recv_sem=n.row_rs.at[i],
                device_id=(to, rp),
                device_id_type=MESH,
            ).start()
            return carry

        lax.fori_loop(1, Pn, one, 0)
        mine = pl.ds(pl.multiple_of(me * T, 16), T)
        pltpu.make_async_copy(src.at[mine], dst.at[mine], n.own_sem.at[i]).start()

    def rows_in(i, dst):
        most = dst.at[pl.ds(0, PT - T)]
        pltpu.make_async_copy(most, most, n.row_rs.at[i]).wait()
        mine = dst.at[pl.ds(0, T)]
        pltpu.make_async_copy(mine, mine, n.own_sem.at[i]).wait()

    def rows_gone(i, src):
        most = src.at[pl.ds(0, PT - T)]
        pltpu.make_async_copy(most, most, n.row_ss.at[i]).wait()

    def to_sides(i, ref):
        return (
            remote(ref.at[1], ref.at[0], n.side_ss.at[i, 0], n.side_rs.at[i, 0], (nxt, rp)),
            remote(ref.at[1], ref.at[2], n.side_ss.at[i, 1], n.side_rs.at[i, 1], (prv, rp)),
        )

    def to_mate(i, src, dst):
        return remote(src, dst, n.pair_ss.at[i], n.pair_rs.at[i], (me, mate))

    dest = n.dest[...].astype(F32)
    mine_hot = iota((Pn, R), 0) == dest
    before = hot(iota((R, R), 0) < iota((R, R), 1)).astype(BF16)
    earlier = mm(hot(mine_hot).astype(BF16), before)
    rank = jnp.sum(jnp.where(mine_hot, earlier, 0.0), axis=0, keepdims=True)
    slot = iota((PT, R), 0)
    pick = hot(dest * T + rank == slot)
    sent = jnp.sum(hot(dest * T + cap == slot), axis=1, keepdims=True)
    pick_low = pick.astype(BF16)
    get_tok.wait()
    n.out_t[...] = (mm(pick_low, n.tok[...]) + sent).astype(BF16)
    n.cols[1] = lists_of(z, n.neighbours[...], me)
    pl.semaphore_wait(barrier, Pn)
    send_rows(0, n.out_t, n.in_t)
    side_lists = to_sides(0, n.cols)
    get_cot.wait()
    n.out_c[...] = mm(pick_low, n.cot[...]).astype(BF16)
    send_rows(1, n.out_c, n.in_c)
    n.pick[...] = pick.T.astype(BF16)

    get_ada1.wait()
    get_ada2.wait()
    cond = jnp.broadcast_to(n.cond[...], (8, n.cond.shape[1]))
    n.c[0:8] = jnp.dot(cond, n.ada1[...], precision=lax.Precision.HIGHEST, preferred_element_type=F32)
    n.c[8:16] = jnp.dot(cond, n.ada2[...], precision=lax.Precision.HIGHEST, preferred_element_type=F32)
    n.colq[...] = n.cols[1].T
    lists = n.cols.shape[1]

    def count_q(t, carry):
        ids = iota((TILE, 3 * R), 1)
        col = n.colq[t, :]
        total = jnp.zeros((TILE, 3 * R), F32)
        for j in range(lists):
            total = total + hot(col[:, j : j + 1] == ids)
        n.cq[t, :] = total
        return carry

    tiles(R, count_q)

    def count_k(side, base):
        def one(t, carry):
            ids = iota((TILE, R), 0) + (t.start + base).astype(F32)
            total = jnp.zeros((TILE, R), F32)
            for j in range(lists):
                total = total + hot(n.cols[side, j : j + 1, :] == ids)
            n.ck[side, t, :] = total
            return carry

        tiles(R, one)

    count_k(1, R)
    for lists_copy in side_lists:
        lists_copy.wait_recv()
    count_k(0, 2 * R)
    count_k(2, 0)

    src_c = jnp.floor((iota((PT, 1), 0) + 0.5) * (1.0 / T))
    src_r = jnp.floor((iota((1, PT), 1) + 0.5) * (1.0 / T))
    step_c = iota((PT, 1), 0) - src_c * T
    step_r = iota((1, PT), 1) - src_r * T
    counting = step_r == cap
    lower = hot((src_r < src_c) & counting).astype(BF16)
    same = hot((src_r == src_c) & counting).astype(BF16)
    rows_in(0, n.in_t)
    first = n.in_t[:, 0:128]
    offset = mm(lower, first)[:, 0:1]
    count = mm(same, first)[:, 0:1]
    position = jnp.where(step_c < count, offset + step_c, -1.0)
    place = hot(position == iota((PT, R), 1))
    n.place[...] = place.astype(BF16)
    place_t = place.T.astype(BF16)
    n.x[...] = mm(place_t, n.in_t[...])

    def norm(src, coeffs, plain_ref, inv_ref, out):
        def one(t, carry):
            v = src[t, :]
            centred = v - jnp.sum(v, axis=-1, keepdims=True) * (1.0 / D)
            inverse = lax.rsqrt(jnp.sum(centred * centred, axis=-1, keepdims=True) * (1.0 / D) + EPS)
            plain = centred * inverse
            plain_ref[t, :] = plain
            inv_ref[t, :] = jnp.broadcast_to(inverse, (TILE, 128))
            out[t, :] = (plain * (1.0 + n.c[coeffs : coeffs + 1, :D]) + n.c[coeffs : coeffs + 1, D:]).astype(BF16)
            return carry

        tiles(R, one)

    def norm_back(grad, coeffs, plain_ref, inv_ref, finish):
        def one(t, carry):
            g = grad[t, :]
            plain = plain_ref[t, :]
            scaled = g * (1.0 + n.c[coeffs : coeffs + 1, :D])
            mean = jnp.sum(scaled, axis=-1, keepdims=True) * (1.0 / D)
            along = jnp.sum(scaled * plain, axis=-1, keepdims=True) * (1.0 / D)
            finish(t, inv_ref[t, 0:1] * (scaled - mean - plain * along))
            return (
                carry[0] + jnp.sum(g * plain, axis=0, keepdims=True),
                carry[1] + jnp.sum(g, axis=0, keepdims=True),
            )

        zero = jnp.zeros((1, D), F32)
        return tiles(R, one, (zero, zero))

    norm(n.x, 0, n.plain1, n.inv1, n.normed.at[1])
    side_normed = to_sides(1, n.normed)
    mate_normed = to_mate(0, n.normed.at[1], n.normed_p)
    get_wqkv.wait()

    def project(side):
        for j in range(3):
            c = slice(j * D, (j + 1) * D)
            n.qkv[side, :, c] = mm(n.normed[side], n.wqkv[:, c]).astype(BF16)

    project(1)
    rows_in(1, n.in_c)
    n.ups[0] = mm(place_t, n.in_c[...]).astype(BF16)
    mate_ups = to_mate(1, n.ups.at[0], n.ups.at[1])
    get_wdown.wait()
    for j in range(FF // D):
        c = slice(j * D, (j + 1) * D)
        n.ga[:, c] = mm(n.ups[0], n.wdown[c, :], NT)
    side_normed[0].wait_recv()
    project(0)
    side_normed[1].wait_recv()
    project(2)

    scale = 1.0 / HD**0.5

    def part(which, h):
        return slice(which * D + h * HD, which * D + (h + 1) * HD)

    for h in range(H):
        for side in range(3):
            n.s[:, side * R : (side + 1) * R] = mm(n.qkv[1, :, part(0, h)], n.qkv[side, :, part(1, h)], NT)

        def soft(t, carry, h=h):
            counts = n.cq[t, :]
            s = jnp.where(counts > 0.0, n.s[t, :] * scale, -1e30)
            top = jnp.max(s, axis=-1, keepdims=True)
            e = jnp.exp(s - top) * counts
            total = jnp.sum(e, axis=-1, keepdims=True)
            w = e * (1.0 / total)
            n.w[h, t, :] = w
            n.low[t, :] = w.astype(BF16)
            n.stat[t, h : h + 1] = top + jnp.log(total)
            return carry

        tiles(R, soft)
        mixed = jnp.zeros((R, HD), F32)
        for side in range(3):
            mixed = mixed + mm(n.low[:, side * R : (side + 1) * R], n.qkv[side, :, part(2, h)])
        n.o[0, :, h * HD : (h + 1) * HD] = mixed.astype(BF16)
    mate_o = to_mate(2, n.o.at[0], n.o.at[1])

    get_wout.wait()
    n.resid[...] = n.x[...] + mm(n.o[0], n.wout[...])
    norm(n.resid, 8, n.plain2, n.inv2, n.normed2.at[0])
    mate_normed2 = to_mate(3, n.normed2.at[0], n.normed2.at[1])
    get_wup.wait()
    half = FF // 2
    for j in range(FF // D):
        c = slice(j * D, (j + 1) * D)
        n.u[...] = mm(n.normed2[0], n.wup[:, c])

        def gate(t, carry, c=c):
            u = n.u[t, :]
            sig = 1.0 / (1.0 + jnp.exp(-u))
            n.a[t, c] = (u * sig).astype(BF16)
            n.gu[t, c] = (n.ga[t, c] * sig * (1.0 + u * (1.0 - sig))).astype(BF16)
            return carry

        tiles(R, gate)
    theirs = pl.ds(pl.multiple_of(mate * half, 128), half)
    ours = pl.ds(pl.multiple_of(rp * half, 128), half)
    mate_a = to_mate(4, n.a.at[:, theirs], n.a_p)
    mate_gu = to_mate(5, n.gu.at[:, theirs], n.gu_p)
    n.tmp[...] = mm(n.gu[...], n.wup[...], NT)

    def keep2(t, gw):
        total = n.ups[0, t, :].astype(F32) + gw
        n.gresid[t, :] = total
        n.gr[t, :] = total.astype(BF16)

    gc2 = norm_back(n.tmp, 8, n.plain2, n.inv2, keep2)
    n.go[1] = mm(n.gr[...], n.wout[...], NT).astype(BF16)
    side_go = to_sides(2, n.go)
    quarter = D // 2
    mate_gr = to_mate(6, n.gr.at[:, pl.ds(pl.multiple_of(mate * quarter, 128), quarter)], n.gr_p)
    y = (n.resid[...] + mm(n.a[...], n.wdown[...])).astype(BF16)
    rows_gone(0, n.out_t)
    n.out_t[...] = mm(n.place[...], y).astype(BF16)
    send_rows(2, n.out_t, n.home_y)

    orders = bit_orders(z.bits)

    def start_of(p, k):
        at = 0
        for i in range(k):
            at = at + ((me >> orders[p][i]) & 1) * (BLOCK[0] >> (i + 1))
        return at

    def span(p, k):
        k = min(k, z.halvings)
        rows = BLOCK[0] >> k
        at = start_of(p, k)
        return pl.ds(pl.multiple_of(at, rows) if k else 0, rows)

    def partner(p, k):
        return (me ^ (1 << orders[p][k]), rp)

    live = {}

    def reduce_start(c, k):
        for p in range(PARTS):
            if k < z.halvings:
                rows = BLOCK[0] >> (k + 1)
                gone = (1 - ((me >> orders[p][k]) & 1)) * rows + start_of(p, k)
                src = n.acc.at[c, p, pl.ds(pl.multiple_of(gone, rows), rows)]
            else:
                src = n.acc.at[c, p, span(p, k)]
            dst = getattr(n, f"rcv{k}").at[c, p]
            live[c, k, p] = remote(src, dst, n.rs_ss.at[c, k, p], n.rs_rs.at[c, k, p], partner(p, k))

    def reduce_end(c, k):
        for p in range(PARTS):
            copy = live[c, k, p]
            copy.wait_recv()
            if k >= z.halvings:
                copy.wait_send()
                started[:] = [s for s in started if s is not copy]
            kept = span(p, k + 1)
            n.acc[c, p, kept] = (n.acc[c, p, kept].astype(F32) + getattr(n, f"rcv{k}")[c, p].astype(F32)).astype(BF16)

    def gather_start(c, k):
        for p in range(PARTS):
            if k == z.halvings - 1:
                kept = span(p, k + 1)
                n.grads[c, rp, p, kept] = n.acc[c, p, kept]
            ref = n.grads.at[c, rp, p, span(p, k + 1)]
            live[c, -k - 1, p] = remote(ref, ref, n.ag_ss.at[c, k, p], n.ag_rs.at[c, k, p], partner(p, k))

    def gather_end(c, k):
        for p in range(PARTS):
            live[c, -k - 1, p].wait_recv()

    def core_start(c):
        ref = n.grads.at[c, rp]
        live[c, "core"] = remote(ref, ref, n.core_ss.at[c], n.core_rs.at[c], (me, mate))

    def core_end(c):
        live[c, "core"].wait_recv()
        pltpu.make_async_copy(n.grads.at[c], n.grads_out.at[c], n.store_sem.at[c]).start()

    plan = {}
    for c in range(3):
        steps = [(reduce_start, (c, 0))]
        for k in range(z.bits):
            steps.append((reduce_end, (c, k)))
            if k + 1 < z.bits:
                steps.append((reduce_start, (c, k + 1)))
        for k in range(z.halvings - 1, -1, -1):
            steps.append((gather_start, (c, k)))
            steps.append((gather_end, (c, k)))
        steps.append((core_start, (c,)))
        steps.append((core_end, (c,)))
        plan[c] = steps

    def advance(c, count=None):
        while plan[c] and (count is None or count > 0):
            fn, args = plan[c].pop(0)
            fn(*args)
            if fn in (reduce_start, gather_start, core_start) and count is not None:
                count -= 1

    mate_ups.wait_recv()
    mate_a.wait_recv()
    for j in range(2):
        r = pl.ds(pl.multiple_of(rp * half + j * BLOCK[0], 128), BLOCK[0])
        for i in range(2):
            c = slice(i * BLOCK[1], (i + 1) * BLOCK[1])
            total = mm(n.a[:, r], n.ups[0, :, c], TN) + mm(n.a_p[:, j * BLOCK[0] : (j + 1) * BLOCK[0]], n.ups[1, :, c], TN)
            n.acc[0, 2 * j + i] = total.astype(BF16)
    advance(0, 1)
    mate_normed2.wait_recv()
    mate_gu.wait_recv()
    for p in range(PARTS):
        c = pl.ds(pl.multiple_of(rp * half + p * BLOCK[1], 128), BLOCK[1])
        d = slice(p * BLOCK[1], (p + 1) * BLOCK[1])
        n.acc[1, p] = (mm(n.normed2[0], n.gu[:, c], TN) + mm(n.normed2[1], n.gu_p[:, d], TN)).astype(BF16)
    advance(1, 1)

    for h in range(H):
        head = slice(h * HD, (h + 1) * HD)
        for side in range(3):
            n.s[:, side * R : (side + 1) * R] = mm(n.go[1, :, head], n.qkv[side, :, part(2, h)], NT)

        def soft_back(t, carry, h=h):
            w = n.w[h, t, :]
            gp = n.s[t, :]
            delta = jnp.sum(w * gp, axis=-1, keepdims=True)
            n.low[t, :] = (w * (gp - delta)).astype(BF16)
            n.stat[t, H + h : H + h + 1] = delta
            return carry

        tiles(R, soft_back)
        total = jnp.zeros((R, HD), F32)
        for side in range(3):
            total = total + mm(n.low[:, side * R : (side + 1) * R], n.qkv[side, :, part(1, h)])
        n.gqkv[:, part(0, h)] = (total * scale).astype(BF16)
    n.stats[1] = n.stat[...].T[0 : 2 * H]
    side_stats = to_sides(3, n.stats)
    advance(0, 1)
    advance(1, 1)

    for i in range(2):
        side_go[i].wait_recv()
        side_stats[i].wait_recv()
    for h in range(H):
        head = slice(h * HD, (h + 1) * HD)
        for side in range(3):
            span_q = slice(side * R, (side + 1) * R)
            n.s[:, span_q] = mm(n.qkv[1, :, part(1, h)], n.qkv[side, :, part(0, h)], NT)
            n.s2[:, span_q] = mm(n.qkv[1, :, part(2, h)], n.go[side, :, head], NT)

        def key_back(t, carry, h=h):
            for side in range(3):
                span_q = slice(side * R, (side + 1) * R)
                counts = n.ck[side, t, :]
                s = n.s[t, span_q] * scale - n.stats[side, h : h + 1, :]
                w = jnp.exp(jnp.where(counts > 0.0, s, -1e30)) * counts
                n.low[t, span_q] = w.astype(BF16)
                n.low2[t, span_q] = (w * (n.s2[t, span_q] - n.stats[side, H + h : H + h + 1, :])).astype(BF16)
            return carry

        tiles(R, key_back)
        total_k = jnp.zeros((R, HD), F32)
        total_v = jnp.zeros((R, HD), F32)
        for side in range(3):
            span_q = slice(side * R, (side + 1) * R)
            total_k = total_k + mm(n.low2[:, span_q], n.qkv[side, :, part(0, h)])
            total_v = total_v + mm(n.low[:, span_q], n.go[side, :, head])
        n.gqkv[:, part(1, h)] = (total_k * scale).astype(BF16)
        n.gqkv[:, part(2, h)] = total_v.astype(BF16)
    wide = 3 * D // 2
    mate_gqkv = to_mate(7, n.gqkv.at[:, pl.ds(pl.multiple_of(mate * wide, 128), wide)], n.gqkv_p)
    advance(0, 1)
    advance(1, 1)

    n.tmp[...] = mm(n.gqkv[...], n.wqkv[...], NT)
    gx_ref = n.tok

    def keep1(t, gw):
        gx_ref[t, :] = (n.gresid[t, :] + gw).astype(BF16)

    gc1 = norm_back(n.tmp, 0, n.plain1, n.inv1, keep1)
    row = lax.broadcasted_iota(I32, (8, D), 0)
    sums = jnp.zeros((8, D), F32)
    for i, value in enumerate((*gc1, *gc2)):
        sums = jnp.where(row == i, value, sums)
    n.gcs[0] = sums

    def small_start(k):
        to = (me, mate) if k == 0 else (me ^ (1 << (k - 1)), rp)
        live["gc"] = remote(n.gcs.at[k], n.gcr.at[k], n.gc_ss.at[k], n.gc_rs.at[k], to)

    def small_end(k):
        live["gc"].wait_recv()
        n.gcs[k + 1] = n.gcs[k] + n.gcr[k]

    small_start(0)
    mate_gqkv.wait_recv()
    mate_normed.wait_recv()
    mate_o.wait_recv()
    mate_gr.wait_recv()
    for p in range(3):
        c = pl.ds(pl.multiple_of(rp * wide + p * BLOCK[1], 128), BLOCK[1])
        d = slice(p * BLOCK[1], (p + 1) * BLOCK[1])
        n.acc[2, p] = (mm(n.normed[1], n.gqkv[:, c], TN) + mm(n.normed_p[...], n.gqkv_p[:, d], TN)).astype(BF16)
    c = pl.ds(pl.multiple_of(rp * quarter, 128), quarter)
    n.acc[2, 3] = (mm(n.o[0], n.gr[:, c], TN) + mm(n.o[1], n.gr_p[...], TN)).astype(BF16)
    advance(2, 1)
    small_end(0)
    rows_gone(1, n.out_c)
    n.out_c[...] = mm(n.place[...], gx_ref[...]).astype(BF16)
    send_rows(3, n.out_c, n.home_g)
    small = 1
    while plan[0] or plan[1] or plan[2]:
        if small <= z.bits:
            small_start(small)
        for c in range(3):
            advance(c, 1)
        if small <= z.bits:
            small_end(small)
            small += 1
    n.sums_out[...] = n.gcs[z.bits + 1]
    rows_in(2, n.home_y)
    n.y_out[...] = mm(n.pick[...], n.home_y[...]).astype(BF16)
    rows_in(3, n.home_g)
    n.g_out[...] = mm(n.pick[...], n.home_g[...]).astype(BF16)

    rows_gone(2, n.out_t)
    rows_gone(3, n.out_c)
    for copy in started:
        copy.wait_send()
    for c in range(3):
        pltpu.make_async_copy(n.grads.at[c], n.grads_out.at[c], n.store_sem.at[c]).wait()


def lists_of(z, neighbours, me):
    within = neighbours & (z.R - 1)
    shift = (2 * z.R).bit_length() - 1
    away = (neighbours >> shift) - me
    after = (away == 1) | (away == 1 - z.P)
    base = jnp.where(away == 0, z.R, jnp.where(after, 2 * z.R, 0))
    return (base + within).astype(F32).T


def finish(z, g_ref, sums_ref, y_ref, gx_ref, ada1_ref, ada2_ref, cond_ref, *outs):
    y_out, gx_out, qkv_out, out_out, up_out, down_out, ga1_out, ga2_out, gcond_out = outs
    i, p = pl.program_id(0), pl.program_id(1)
    down_out[...] = g_ref[0, 0, 0].astype(F32)
    up_out[...] = g_ref[1, 0, 0].astype(F32)

    @pl.when(p < 3)
    def _():
        qkv_out[...] = g_ref[2, 0, 0].astype(F32)

    @pl.when(p == 3)
    def _():
        out_out[...] = g_ref[2, 0, 0].astype(F32)

    @pl.when((i == 0) & (p == 0))
    def _():
        y_out[...] = y_ref[...]
        gx_out[...] = gx_ref[...]
        count = cond_ref.shape[1]
        eye = lax.broadcasted_iota(I32, (count, count), 0) == lax.broadcasted_iota(I32, (count, count), 1)
        cond = jnp.sum(jnp.where(eye, cond_ref[...], 0.0), axis=1, keepdims=True)
        d = z.D
        total = jnp.zeros((count, 1), F32)
        for row, ada, out in ((0, ada1_ref, ga1_out), (2, ada2_ref, ga2_out)):
            for j in range(2):
                c = slice(j * d, (j + 1) * d)
                sums = sums_ref[row + j : row + j + 1, :]
                out[:, c] = cond * sums
                total = total + jnp.sum(ada[:, c] * sums, axis=1, keepdims=True)
        gcond_out[...] = jnp.sum(jnp.where(eye, total, 0.0), axis=0, keepdims=True)


def local(tokens, cotangent, dest, neighbours, w_qkv, w_out, w_up, w_down, ada_attn, ada_mlp, cond):
    rows, width = tokens.shape
    z = sizes(lax.axis_size("patch"), rows, width, w_up.shape[1])
    dest = dest.reshape(1, rows)
    cond = cond.reshape(1, cond.shape[0])
    inputs = dict(
        tokens=tokens,
        cotangent=cotangent,
        dest=dest,
        neighbours=neighbours,
        w_qkv=w_qkv,
        w_out=w_out,
        w_up=w_up,
        w_down=w_down,
        ada_attn=ada_attn,
        ada_mlp=ada_mlp,
        cond=cond,
    )
    small = ("dest", "neighbours", "cond")
    any_space = pl.BlockSpec(memory_space=pl.ANY)
    vmem = pl.BlockSpec(memory_space=pltpu.VMEM)
    shape = jax.ShapeDtypeStruct
    outs = dict(
        grads_out=shape((3, 2, PARTS) + BLOCK, BF16),
        sums_out=shape((8, width), F32),
        y_out=shape((rows, width), BF16),
        g_out=shape((rows, width), BF16),
    )
    held = scratch(z, neighbours.shape[1])
    grads, sums, y, gx = pl.pallas_call(
        functools.partial(layer, z, [*inputs, *outs, *held]),
        out_shape=list(outs.values()),
        in_specs=[vmem if k in small else any_space for k in inputs],
        out_specs=[any_space, vmem, vmem, vmem],
        scratch_shapes=list(held.values()),
        compiler_params=pltpu.CompilerParams(collective_id=0, has_side_effects=True, vmem_limit_bytes=62 << 20),
        name="layer",
    )(*inputs.values())

    whole = lambda i, p: (0, 0)
    block = pl.BlockSpec(BLOCK, None)
    rows_spec = pl.BlockSpec((rows, width), whole)
    ada_spec = pl.BlockSpec(ada_attn.shape, whole)
    cond_spec = pl.BlockSpec((1, cond.shape[1]), whole)
    y, gx, g_qkv, g_out, g_up, g_down, g_ada1, g_ada2, g_cond = pl.pallas_call(
        functools.partial(finish, z),
        grid=(2, PARTS),
        in_specs=[
            pl.BlockSpec((3, 1, 1) + BLOCK, lambda i, p: (0, i, p, 0, 0)),
            pl.BlockSpec((8, width), whole),
            rows_spec,
            rows_spec,
            ada_spec,
            ada_spec,
            cond_spec,
        ],
        out_specs=[
            rows_spec,
            rows_spec,
            pl.BlockSpec(BLOCK, lambda i, p: (0, i * 3 + jnp.minimum(p, 2))),
            pl.BlockSpec(BLOCK, lambda i, p: (0, i)),
            pl.BlockSpec(BLOCK, lambda i, p: (0, i * PARTS + p)),
            pl.BlockSpec(BLOCK, lambda i, p: (i * 2 + p // 2, p % 2)),
            ada_spec,
            ada_spec,
            cond_spec,
        ],
        out_shape=[
            shape((rows, width), BF16),
            shape((rows, width), BF16),
            shape(w_qkv.shape, F32),
            shape(w_out.shape, F32),
            shape(w_up.shape, F32),
            shape(w_down.shape, F32),
            shape(ada_attn.shape, F32),
            shape(ada_mlp.shape, F32),
            shape(cond.shape, F32),
        ],
        name="finish",
    )(grads, sums, y, gx, ada_attn, ada_mlp, cond)
    return y, gx, g_qkv, g_out, g_up, g_down, g_ada1, g_ada2, g_cond.reshape(cond.shape[1])


def solution(mesh):
    row = P(("patch", "rep"), None)
    return jax.shard_map(
        local,
        mesh=mesh,
        in_specs=(row, row, P(("patch", "rep")), row) + (P(),) * 7,
        out_specs=(row, row) + (P(),) * 7,
        check_vma=False,
    )
```

time: 332 us -> 161 us (0.48)
  Pallas kernels: 0 us -> 157 us
  waiting for transfers between devices: 127 us -> 0 us
  matrix products: 60.5 us -> 0 us
  blocking collectives: 48.7 us -> 0 us
  starting transfers between devices: 39 us -> 0 us
  other arithmetic: 31.1 us -> 0 us
  between operations: 14.9 us -> 0.81 us
  local copies, waits for them, and re-layouts: 9.9 us -> 1.47 us
    pallas_call x0 -> x2, Pallas kernels: none -> 157 us  [the longest x1 148 us: local(): pl.pallas_call(functools.partial(layer, z, [*inputs, *outs, *held]), out_...]
    psum x1 -> x0, waiting for transfers between devices: 110 us -> none  [local(): lax.psum(g.astype(BF16), both).astype(F32)]
    dot_general x49 -> x0, matrix products: 60.5 us -> none  [the longest x45 57.3 us: dot(): lax.dot_general(a, b, (((ca,), (cb,)), ((), ())), preferred_element_type=...]
    psum x1 -> x0, blocking collectives: 48.7 us -> none  [local(): gc1, gc2 = lax.psum((gc1, gc2), both)]
    all_to_all x3 -> x0, starting transfers between devices: 20.8 us -> none  [the longest x1 7 us: local(): lax.all_to_all(leaving.reshape(patches, cap, 2 * width), 'patch', split_a...]
    ppermute x8 -> x0, starting transfers between devices: 18.1 us -> none  [from_side(): lax.ppermute(array, 'patch', [(i, (i + by) % patches) for i in range(patc...]
    reduce_sum x10 -> x0, other arithmetic: 13.8 us -> none  [the longest x1 7.87 us: local(): jnp.sum((column.T[:, :, None] == ids[None, None, :]).astype(F32), axis=1)]
    convert_element_type x6 -> x0, other arithmetic: 10.3 us -> none  [the longest x4 9.88 us: local(): lax.psum(g.astype(BF16), both).astype(F32)]
  transfers between devices with their start and end apart: 12 -> 0, of which waited for: 5 -> 0; matrix products, arithmetic and copies ran while one was open for 15% -> 0% of each run, Pallas kernels for 0% -> 0%
where the time goes in v2:
time: 161 us; the launch traced here: 160 us
  Pallas kernels  157 us (98%)
    pallas_call x1, Pallas kernels, local(): pl.pallas_call(functools.partial(layer, z, [*inputs, *outs, *held]), out_...  148 us
    pallas_call x1, Pallas kernels, local(): pl.pallas_call(functools.partial(finish, z), grid=(2, PARTS), in_specs=[p...  9.86 us

profile of v2, /device:TPU:0, one launch (start us, length us, event | category | flops | bytes accessed | tf_op | source)
XLA Modules:
  0.0 159.7 jit_solution(15768264341770833366)
XLA Ops:
  0.6 1.5 copy.20.refs_3_
  2.1 147.6 %layer.1 = (bf16[3,2,4,512,256]{4,3,2,1,0:T(8,128)(2,1)}, f32[8,512]{1,0:T(8,128)}, bf16[256,512]{1,0:T(8,128)(2,1)}, bf16[256,512]{1,0:T(8,128)(2,1)}) custom-call(bf16[256,512]{1,0:T(8,128)(2,1)} %refs_0_.1, bf16[256,512]{1,0:T(8,128)(2,1)} %refs_1_.1, s32[1,256]{1,0:T(1,128)} %bitcast.5, s32[256,16]{1,0:T(8,128)} %copy.20.refs_3_, ...), custom_call_target="tpu_custom_call" | custom-call | tf_op jit(solution)/shard_map/layer/pallas_call | solution.py:701
  149.7 9.9 %finish.1 = (bf16[256,512]{1,0:T(8,128)(2,1)}, bf16[256,512]{1,0:T(8,128)(2,1)}, f32[512,1536]{1,0:T(8,128)}, f32[512,512]{1,0:T(8,128)}, f32[512,2048]{1,0:T(8,...) custom-call(bf16[3,2,4,512,256]{4,3,2,1,0:T(8,128)(2,1)} %get-tuple-element.22.g_ref, ...), custom_call_target="tpu_custom_call" | custom-call | tf_op jit(solution)/shard_map/finish/pallas_call | solution.py:716

commit v3 on v2

v3 whole, which is shorter than its diff:
```python
import functools
import heapq
import itertools
import types

import jax
import jax.numpy as jnp
from jax import lax
from jax.experimental import pallas as pl
from jax.experimental.pallas import tpu as pltpu
from jax.sharding import PartitionSpec as P

H = 4
HD = 128
EPS = 1e-05
F32 = jnp.float32
BF16 = jnp.bfloat16
I32 = jnp.int32
MESH = pl.DeviceIdType.MESH
NN = (((1,), (0,)), ((), ()))
NT = (((1,), (1,)), ((), ()))
TN = (((0,), (0,)), ((), ()))
TILE = 32
NEVER = -1e30
LOG2E = 1.4426950408889634
BLOCK = (512, 256)
MIN_ROWS = 16


def mm(a, b, dims=NN):
    return lax.dot_general(a, b, dims, preferred_element_type=F32)


def iota(shape, axis):
    return lax.broadcasted_iota(I32, shape, axis).astype(F32)


def hot(cond):
    return jnp.where(cond, 1.0, 0.0)


def sizes(patches, rows, width, hidden):
    cap = rows // patches + 1
    block = -(-(cap - 1) // 16) * 16
    bits = patches.bit_length() - 1
    halvings = 0
    while halvings < bits and BLOCK[0] >> (halvings + 1) >= MIN_ROWS:
        halvings += 1
    return types.SimpleNamespace(
        P=patches, R=rows, D=width, FF=hidden, T=block, PT=patches * block, bits=bits, halvings=halvings
    )


XYZ, XZY, YXZ, YZX, ZXY, ZYX = itertools.permutations(range(3))
ORDERS = [XZY, YXZ, ZYX, XZY, XYZ, YZX, ZYX, YXZ, ZYX, YXZ, XZY, XYZ]
DOWN, UP, OUT, QKV = range(0, 4), range(4, 8), range(8, 9), range(9, 12)
STREAMS = len(ORDERS)
QKV_AT = 15.3
FREE_AT = (4.0, 5.0, 5.0)
COMPUTES = ((-1.0, 1.2), (1.2, 2.3), (2.3, 3.4), (3.4, 4.5), (4.5, 5.6), (8.5, 9.5), (9.5, 10.5), (10.5, 11.5), (11.5, 12.5), (12.5, 14.0), (14.0, 15.3))
PIECES = 4


def bit_orders(bits):
    return [tuple(b for b in f if b < bits) + tuple(range(3, bits)) for f in ORDERS]


def sum_plan(bits, halvings):
    whole, delay, turn, depth = 5.7, 1.8, 0.12, 2
    steps = []
    for order in bit_orders(bits):
        places = [(order[k], min(k + 1, halvings)) for k in range(bits)]
        places += [(order[k], k + 1) for k in range(halvings - 1, -1, -1)]
        far = 2.0 if bits == 4 else 1.0
        steps.append([(b, whole / (1 << k) * (far if b == 3 else 1.0)) for b, k in places] + [(None, 0.5)])
    at = [0] * STREAMS
    free, queued, waiting, plan = {}, {}, [], []
    number = itertools.count()
    events = [(QKV_AT if p in QKV else FREE_AT[ORDERS[p][0]], next(number), "ready", p) for p in range(STREAMS)]
    heapq.heapify(events)
    now = 0.0

    def able(t):
        return next((b for a, b in COMPUTES if a < t < b), t)

    while events:
        t, _, kind, p = heapq.heappop(events)
        if kind == "free":
            queued[p] -= 1
            kind = "look"
        if able(max(now, t)) > max(now, t):
            heapq.heappush(events, (able(max(now, t)), next(number), kind, p))
            continue
        now = max(now, t)
        if kind == "ready":
            waiting.append(p)
        elif kind == "end":
            now += turn
            plan.append((now, "await", p))
            at[p] += 1
            if at[p] < len(steps[p]):
                waiting.append(p)
        for q in sorted(waiting):
            link, time = steps[q][at[q]]
            if link is not None and queued.get(link, 0) >= depth:
                continue
            waiting.remove(q)
            now += 0.03
            plan.append((now, "start", q))
            queued[link] = queued.get(link, 0) + 1
            free[link] = max(free.get(link, 0.0), now) + time
            heapq.heappush(events, (free[link] + delay, next(number), "end", q))
            heapq.heappush(events, (free[link], next(number), "free", link))
    return plan


def scratch(z, nb):
    R, D, FF, PT, PS = z.R, z.D, z.FF, z.PT, z.PT + z.P
    recv_rows = []
    for k in range(z.bits):
        recv_rows.append(BLOCK[0] >> (min(k + 1, z.halvings)))
    vm, dma = pltpu.VMEM, pltpu.SemaphoreType.DMA
    s = dict(
        tok=vm((R, D), BF16),
        cot=vm((R, D), BF16),
        wqkv=vm((D, 3 * D), BF16),
        wout=vm((D, D), BF16),
        wup=vm((D, FF), BF16),
        wdown=vm((FF, D), BF16),
        ada1=vm((32, 2 * D), F32),
        ada2=vm((32, 2 * D), F32),
        c=vm((16, 2 * D), F32),
        pick=vm((R, PS), BF16),
        place=vm((PS, R), BF16),
        out_t=vm((PT, D), BF16),
        out_c=vm((PT, D), BF16),
        in_t=vm((PS, D), BF16),
        in_c=vm((PS, D), BF16),
        home_y=vm((PS, D), BF16),
        home_g=vm((PS, D), BF16),
        more_out=vm((4, z.P, 1, D + 128), F32),
        more_in=vm((4, z.P, 1, D + 128), F32),
        x=vm((R, D), F32),
        plain1=vm((R, D), F32),
        inv1=vm((R, 128), F32),
        plain2=vm((R, D), F32),
        inv2=vm((R, 128), F32),
        resid=vm((R, D), F32),
        gresid=vm((R, D), F32),
        tmp=vm((R, D), F32),
        ups=vm((2, R, D), BF16),
        normed=vm((3, R, D), BF16),
        normed_p=vm((R, D), BF16),
        qkv=vm((3, R, 3 * D), BF16),
        cols=vm((3, nb, R), F32),
        colq=vm((R, nb), F32),
        cq=vm((R, 3 * R), F32),
        ck=vm((3, R, R), F32),
        s=vm((R, 3 * R), F32),
        s2=vm((R, 3 * R), F32),
        w=vm((H, R, 3 * R), BF16),
        low=vm((R, 3 * R), BF16),
        low2=vm((R, 3 * R), BF16),
        o=vm((2, R, D), BF16),
        u=vm((R, D), F32),
        ga=vm((R, D), F32),
        a=vm((R, FF), BF16),
        a_p=vm((R, FF // 2), BF16),
        gu=vm((R, FF), BF16),
        gu_p=vm((R, FF // 2), BF16),
        normed2=vm((2, R, D), BF16),
        gr=vm((R, D), BF16),
        gr_p=vm((R, D // 2), BF16),
        go=vm((3, R, D), BF16),
        stat=vm((R, 128), F32),
        stats=vm((3, 2 * H, R), F32),
        gqkv=vm((R, 3 * D), BF16),
        gqkv_p=vm((R, 3 * D // 2), BF16),
        acc=vm((STREAMS,) + BLOCK, BF16),
        **{f"rcv{k}": vm((STREAMS, n, BLOCK[1]), BF16) for k, n in enumerate(recv_rows)},
        gcs=vm((z.bits + 2, 8, D), F32),
        gcr=vm((z.bits + 1, 8, D), F32),
        load_sem=dma((8,)),
        row_ss=dma((4,)),
        row_rs=dma((4,)),
        own_sem=dma((4,)),
        more_ss=dma((4,)),
        more_rs=dma((4,)),
        more_own=dma((4,)),
        side_ss=dma((4, 2)),
        side_rs=dma((4, 2)),
        piece_rs=dma((2, PIECES)),
        pair_ss=dma((8,)),
        pair_rs=dma((8,)),
        sum_ss=dma((1,)),
        late_ss=dma((STREAMS, max(z.bits - z.halvings, 1))),
        rs_rs=dma((STREAMS, z.bits)),
        ag_rs=dma((STREAMS, z.halvings)),
        core_ss=dma((1,)),
        core_rs=dma((1,)),
        gc_ss=dma((1,)),
        gc_rs=dma((z.bits + 1,)),
    )
    return s


def marker():
    def phase(name):
        del name

    return phase


def layer(z, names, *refs):
    n = types.SimpleNamespace(**dict(zip(names, refs, strict=True)))
    Pn, R, D, FF, T, PT, PS = z.P, z.R, z.D, z.FF, z.T, z.PT, z.PT + z.P
    me = lax.axis_index("patch")
    rp = lax.axis_index("rep")
    mate = 1 - rp
    nxt = lax.rem(me + 1, Pn)
    prv = lax.rem(me + Pn - 1, Pn)
    started = []
    phase = marker()

    def tiles(total, fn, init=0, size=TILE, together=1):
        def some(i, carry):
            for j in range(together):
                carry = fn(pl.ds(pl.multiple_of((i * together + j) * size, size), size), carry)
            return carry

        return lax.fori_loop(0, total // (size * together), some, init)

    def load(i, src, dst):
        copy = pltpu.make_async_copy(src, dst, n.load_sem.at[i])
        copy.start()
        return copy

    phase("entry")
    get_tok = load(0, n.tokens, n.tok)
    get_cot = load(1, n.cotangent, n.cot)
    get_ada1 = load(2, n.ada_attn, n.ada1)
    get_ada2 = load(3, n.ada_mlp, n.ada2)
    get_wqkv = load(4, n.w_qkv, n.wqkv)
    get_wdown = load(5, n.w_down, n.wdown)
    get_wout = load(6, n.w_out, n.wout)
    get_wup = load(7, n.w_up, n.wup)

    barrier = pltpu.get_barrier_semaphore()

    def greet(i, carry):
        pl.semaphore_signal(barrier, inc=1, device_id=(lax.rem(me + i, Pn), rp), device_id_type=MESH)
        return carry

    lax.fori_loop(1, Pn, greet, 0)
    pl.semaphore_signal(barrier, inc=1, device_id=(me, mate), device_id_type=MESH)

    def remote(src, dst, ss, rs, to, keep=False):
        copy = pltpu.make_async_remote_copy(
            src_ref=src, dst_ref=dst, send_sem=ss, recv_sem=rs, device_id=to, device_id_type=MESH
        )
        copy.start()
        if keep:
            started.append(copy)
        return copy

    def send_rows(i, src, dst):
        def one(j, carry):
            to = lax.rem(me + j, Pn)
            pltpu.make_async_remote_copy(
                src_ref=src.at[pl.ds(pl.multiple_of(to * T, 16), T)],
                dst_ref=dst.at[pl.ds(pl.multiple_of(me * T, 16), T)],
                send_sem=n.row_ss.at[i],
                recv_sem=n.row_rs.at[i],
                device_id=(to, rp),
                device_id_type=MESH,
            ).start()
            pltpu.make_async_remote_copy(
                src_ref=n.more_out.at[i, to],
                dst_ref=n.more_in.at[i, me],
                send_sem=n.more_ss.at[i],
                recv_sem=n.more_rs.at[i],
                device_id=(to, rp),
                device_id_type=MESH,
            ).start()
            return carry

        lax.fori_loop(1, Pn, one, 0)
        mine = pl.ds(pl.multiple_of(me * T, 16), T)
        pltpu.make_async_copy(src.at[mine], dst.at[mine], n.own_sem.at[i]).start()
        pltpu.make_async_copy(n.more_out.at[i, me], n.more_in.at[i, me], n.more_own.at[i]).start()

    def waits_for(ref, sem):
        pltpu.make_async_copy(ref, ref, sem).wait()

    def rows_in(i, dst):
        waits_for(n.more_in.at[i, pl.ds(0, Pn - 1)], n.more_rs.at[i])
        waits_for(n.more_in.at[i, 0], n.more_own.at[i])
        waits_for(dst.at[pl.ds(0, PT - T)], n.row_rs.at[i])
        waits_for(dst.at[pl.ds(0, T)], n.own_sem.at[i])
        dst[PT:PS] = n.more_in[i, :, 0, :D].astype(BF16)

    def rows_gone(i, src):
        waits_for(src.at[pl.ds(0, PT - T)], n.row_ss.at[i])
        waits_for(n.more_out.at[i, pl.ds(0, Pn - 1)], n.more_ss.at[i])

    def set_rows(i, hot_rows, values, out):
        total = mm(hot_rows, values)
        out[...] = total[:PT].astype(BF16)
        n.more_out[i, :, 0, :D] = total[PT:]

    even = lax.rem(me, 2) == 0
    near = me ^ 1
    near_slot = jnp.where(even, 2, 0)
    far_slot = 2 - near_slot
    onward = lax.rem(jnp.where(even, me + 2, me + Pn - 2), Pn)

    def to_sides(i, ref):
        return (
            remote(ref.at[1], ref.at[0], n.side_ss.at[i, 0], n.side_rs.at[i, 0], (nxt, rp), True),
            remote(ref.at[1], ref.at[2], n.side_ss.at[i, 1], n.side_rs.at[i, 1], (prv, rp), True),
        )

    def to_near(i, ref):
        size = R // PIECES
        return [
            remote(
                ref.at[1, pl.ds(c * size, size)],
                ref.at[far_slot, pl.ds(c * size, size)],
                n.side_ss.at[i, 0],
                n.piece_rs.at[i - 1, c],
                (near, rp),
            )
            for c in range(PIECES)
        ]

    def hand_on(i, ref, copies):
        size = R // PIECES
        for copy in copies:
            c = len(handed[i])
            copy.wait_recv()
            handed[i].append(
                remote(
                    ref.at[near_slot, pl.ds(c * size, size)],
                    ref.at[far_slot, pl.ds(c * size, size)],
                    n.side_ss.at[i, 1],
                    n.side_rs.at[i, 1],
                    (onward, rp),
                )
            )

    handed = {1: [], 2: []}

    def far_in(i, ref):
        waits_for(ref.at[far_slot], n.side_rs.at[i, 1])

    def to_mate(i, src, dst):
        return remote(src, dst, n.pair_ss.at[i], n.pair_rs.at[i], (me, mate), True)

    n.cols[1] = lists_of(z, n.neighbours[...], me)
    dest = n.dest[...].astype(F32)
    mine_hot = iota((Pn, R), 0) == dest
    before = hot(iota((R, R), 0) < iota((R, R), 1)).astype(BF16)
    earlier = mm(hot(mine_hot).astype(BF16), before)
    rank = jnp.sum(jnp.where(mine_hot, earlier, 0.0), axis=0, keepdims=True)
    code = jnp.where(rank < T, dest * T + rank, PT + dest)
    pick = hot(code == iota((PS, R), 0))
    pick_low = pick.astype(BF16)
    get_tok.wait()
    set_rows(0, pick_low, n.tok[...], n.out_t)
    n.more_out[0, :, 0, D:] = jnp.broadcast_to(jnp.sum(hot(mine_hot), axis=1, keepdims=True), (Pn, 128))
    phase("barrier")
    pl.semaphore_wait(barrier, Pn)
    phase("send tokens")
    side_lists = to_sides(0, n.cols)
    send_rows(0, n.out_t, n.in_t)
    get_cot.wait()
    set_rows(1, pick_low, n.cot[...], n.out_c)
    n.pick[...] = pick.T.astype(BF16)

    phase("counts")
    get_ada1.wait()
    get_ada2.wait()
    cond = jnp.broadcast_to(n.cond[...], (8, n.cond.shape[1]))
    n.c[0:8] = jnp.dot(cond, n.ada1[...], precision=lax.Precision.HIGHEST, preferred_element_type=F32)
    n.c[8:16] = jnp.dot(cond, n.ada2[...], precision=lax.Precision.HIGHEST, preferred_element_type=F32)
    n.colq[...] = n.cols[1].T
    lists = n.cols.shape[1]

    def count_q(t, carry):
        ids = iota((TILE, 3 * R), 1)
        col = n.colq[t, :]
        total = jnp.zeros((TILE, 3 * R), F32)
        for j in range(lists):
            total = total + hot(col[:, j : j + 1] == ids)
        n.cq[t, :] = jnp.where(total > 0.0, jnp.log2(total), NEVER)
        return carry

    tiles(R, count_q)

    def count_k(side, base):
        def one(t, carry):
            ids = iota((TILE, R), 0) + (t.start + base).astype(F32)
            total = jnp.zeros((TILE, R), F32)
            for j in range(lists):
                total = total + hot(n.cols[side, j : j + 1, :] == ids)
            n.ck[side, t, :] = jnp.where(total > 0.0, jnp.log2(total), NEVER)
            return carry

        tiles(R, one)

    count_k(1, R)
    phase("side counts")
    for lists_copy in side_lists:
        lists_copy.wait_recv()
    count_k(0, 2 * R)
    count_k(2, 0)

    phase("places")
    row = iota((PS, 1), 0)
    source = jnp.where(row < PT, jnp.floor((row + 0.5) * (1.0 / T)), row - PT)
    step = jnp.where(row < PT, row - source * T, T * 1.0)
    spread = hot(source == iota((PS, Pn), 1)).astype(BF16)
    earlier_sources = hot(iota((Pn, Pn), 0) > iota((Pn, Pn), 1)).astype(BF16)
    phase("wait tokens")
    rows_in(0, n.in_t)
    phase("place rows")
    count = n.more_in[0, :, 0, D:].astype(BF16)
    offset = mm(earlier_sources, count).astype(BF16)
    position = jnp.where(step < mm(spread, count)[:, 0:1], mm(spread, offset)[:, 0:1] + step, -1.0)
    place = hot(position == iota((PS, R), 1))
    n.place[...] = place.astype(BF16)
    place_t = place.T.astype(BF16)
    n.x[...] = mm(place_t, n.in_t[...])

    def norm(src, coeffs, plain_ref, inv_ref, out):
        def one(t, carry):
            v = src[t, :]
            centred = v - jnp.sum(v, axis=-1, keepdims=True) * (1.0 / D)
            inverse = lax.rsqrt(jnp.sum(centred * centred, axis=-1, keepdims=True) * (1.0 / D) + EPS)
            plain = centred * inverse
            plain_ref[t, :] = plain
            inv_ref[t, :] = jnp.broadcast_to(inverse, (TILE, 128))
            out[t, :] = (plain * (1.0 + n.c[coeffs : coeffs + 1, :D]) + n.c[coeffs : coeffs + 1, D:]).astype(BF16)
            return carry

        tiles(R, one)

    def norm_back(grad, coeffs, plain_ref, inv_ref, finish):
        def one(t, carry):
            g = grad[t, :]
            plain = plain_ref[t, :]
            scaled = g * (1.0 + n.c[coeffs : coeffs + 1, :D])
            mean = jnp.sum(scaled, axis=-1, keepdims=True) * (1.0 / D)
            along = jnp.sum(scaled * plain, axis=-1, keepdims=True) * (1.0 / D)
            finish(t, inv_ref[t, 0:1] * (scaled - mean - plain * along))
            return (
                carry[0] + jnp.sum(g * plain, axis=0, keepdims=True),
                carry[1] + jnp.sum(g, axis=0, keepdims=True),
            )

        zero = jnp.zeros((1, D), F32)
        return tiles(R, one, (zero, zero))

    phase("norm")
    norm(n.x, 0, n.plain1, n.inv1, n.normed.at[1])
    side_normed = to_near(1, n.normed)
    mate_normed = to_mate(0, n.normed.at[1], n.normed_p)
    phase("project")
    get_wqkv.wait()

    def project(side):
        for j in range(3):
            c = slice(j * D, (j + 1) * D)
            n.qkv[side, :, c] = mm(n.normed[side], n.wqkv[:, c]).astype(BF16)

    project(1)
    phase("wait halo")
    hand_on(1, n.normed, side_normed)
    send_rows(1, n.out_c, n.in_c)
    project(near_slot)
    phase("wait far")
    far_in(1, n.normed)
    project(far_slot)

    phase("attention")
    scale = 1.0 / HD**0.5

    def part(which, h):
        return slice(which * D + h * HD, which * D + (h + 1) * HD)

    for h in range(H):
        for side in range(3):
            n.s[:, side * R : (side + 1) * R] = mm(n.qkv[1, :, part(0, h)], n.qkv[side, :, part(1, h)], NT)

        def soft(t, carry, h=h):
            s = n.s[t, :] * (scale * LOG2E) + n.cq[t, :]
            top = jnp.max(s, axis=-1, keepdims=True)
            e = jnp.exp2(s - top)
            total = jnp.sum(e, axis=-1, keepdims=True)
            w = e * (1.0 / total)
            n.w[h, t, :] = w.astype(BF16)
            n.stat[t, h : h + 1] = top + jnp.log2(total)
            return carry

        tiles(R, soft, together=4)
        mixed = jnp.zeros((R, HD), F32)
        for side in range(3):
            mixed = mixed + mm(n.w[h, :, side * R : (side + 1) * R], n.qkv[side, :, part(2, h)])
        n.o[0, :, h * HD : (h + 1) * HD] = mixed.astype(BF16)
    mate_o = to_mate(2, n.o.at[0], n.o.at[1])

    phase("wait upstream")
    rows_in(1, n.in_c)
    n.ups[0] = mm(place_t, n.in_c[...]).astype(BF16)
    mate_ups = to_mate(1, n.ups.at[0], n.ups.at[1])
    phase("resid")
    get_wout.wait()
    n.resid[...] = n.x[...] + mm(n.o[0], n.wout[...])
    norm(n.resid, 8, n.plain2, n.inv2, n.normed2.at[0])
    mate_normed2 = to_mate(3, n.normed2.at[0], n.normed2.at[1])
    get_wup.wait()
    get_wdown.wait()
    phase("mlp")
    half = FF // 2
    for j in range(FF // D):
        c = slice(j * D, (j + 1) * D)
        n.u[...] = mm(n.normed2[0], n.wup[:, c])
        n.ga[...] = mm(n.ups[0], n.wdown[c, :], NT)

        def gate(t, carry, c=c):
            u = n.u[t, :]
            sig = 1.0 / (1.0 + jnp.exp(-u))
            n.a[t, c] = (u * sig).astype(BF16)
            n.gu[t, c] = (n.ga[t, :] * sig * (1.0 + u * (1.0 - sig))).astype(BF16)
            return carry

        tiles(R, gate)
    theirs = pl.ds(pl.multiple_of(mate * half, 128), half)
    ours = pl.ds(pl.multiple_of(rp * half, 128), half)
    mate_a = to_mate(4, n.a.at[:, theirs], n.a_p)
    mate_gu = to_mate(5, n.gu.at[:, theirs], n.gu_p)
    phase("mlp back")
    n.tmp[...] = mm(n.gu[...], n.wup[...], NT)

    def keep2(t, gw):
        total = n.ups[0, t, :].astype(F32) + gw
        n.gresid[t, :] = total
        n.gr[t, :] = total.astype(BF16)

    gc2 = norm_back(n.tmp, 8, n.plain2, n.inv2, keep2)
    phase("go")
    n.go[1] = mm(n.gr[...], n.wout[...], NT).astype(BF16)
    side_go = to_near(2, n.go)
    quarter = D // 2
    mate_gr = to_mate(6, n.gr.at[:, pl.ds(pl.multiple_of(mate * quarter, 128), quarter)], n.gr_p)
    orders = bit_orders(z.bits)
    top_rows = BLOCK[0]

    def bit(p, k):
        return (me >> orders[p][k]) & 1

    def start_of(p, k):
        at = 0
        for i in range(k):
            at = at + bit(p, i) * (top_rows >> (i + 1))
        return at

    def span(p, k):
        k = min(k, z.halvings)
        rows = top_rows >> k
        return pl.ds(pl.multiple_of(start_of(p, k), rows) if k else 0, rows)

    def partner(p, k):
        return (me ^ (1 << orders[p][k]), rp)

    live = {}

    def reduce_start(p, k):
        if k < z.halvings:
            rows = top_rows >> (k + 1)
            gone = (1 - bit(p, k)) * rows + start_of(p, k)
            src = n.acc.at[p, pl.ds(pl.multiple_of(gone, rows), rows)]
        else:
            src = n.acc.at[p, span(p, k)]
        ss = n.sum_ss.at[0] if k < z.halvings else n.late_ss.at[p, k - z.halvings]
        live[p] = remote(src, getattr(n, f"rcv{k}").at[p], ss, n.rs_rs.at[p, k], partner(p, k))

    def reduce_end(p, k):
        live[p].wait_recv()
        if k >= z.halvings:
            live[p].wait_send()
        kept = span(p, k + 1)
        total = n.acc[p, kept].astype(F32) + getattr(n, f"rcv{k}")[p].astype(F32)
        into = n.grads_out.at[rp, p, kept] if k + 1 == z.bits else n.acc.at[p, kept]
        into[...] = total.astype(BF16)

    def gather_start(p, k):
        ref = n.grads_out.at[rp, p, span(p, k + 1)]
        live[p] = remote(ref, ref, n.sum_ss.at[0], n.ag_rs.at[p, k], partner(p, k))

    def core_start(p):
        ref = n.grads_out.at[rp, p]
        remote(ref, ref, n.core_ss.at[0], n.core_rs.at[0], (me, mate))

    steps_left = {}
    for p in range(STREAMS):
        steps = []
        for k in range(z.bits):
            steps += [functools.partial(reduce_start, p, k), functools.partial(reduce_end, p, k)]
        for k in range(z.halvings - 1, -1, -1):
            steps += [functools.partial(gather_start, p, k), lambda p=p: live[p].wait_recv()]
        steps += [functools.partial(core_start, p), lambda: None]
        steps_left[p] = steps
    actions = sum_plan(z.bits, z.halvings)

    def service(until=None, most=None):
        while actions and (until is None or actions[0][0] <= until) and (most is None or most > 0):
            most = None if most is None else most - 1
            steps_left[actions.pop(0)[2]].pop(0)()

    phase("grad down")
    mate_ups.wait_recv()
    mate_a.wait_recv()
    for j in range(2):
        r = pl.ds(pl.multiple_of(rp * half + j * BLOCK[0], 128), BLOCK[0])
        for i in range(2):
            c = slice(i * BLOCK[1], (i + 1) * BLOCK[1])
            total = mm(n.a[:, r], n.ups[0, :, c], TN) + mm(n.a_p[:, j * BLOCK[0] : (j + 1) * BLOCK[0]], n.ups[1, :, c], TN)
            n.acc[2 * j + i] = total.astype(BF16)
    phase("grad up")
    mate_normed2.wait_recv()
    mate_gu.wait_recv()
    for p in range(len(UP)):
        c = pl.ds(pl.multiple_of(rp * half + p * BLOCK[1], 128), BLOCK[1])
        d = slice(p * BLOCK[1], (p + 1) * BLOCK[1])
        n.acc[UP[p]] = (mm(n.normed2[0], n.gu[:, c], TN) + mm(n.normed2[1], n.gu_p[:, d], TN)).astype(BF16)
    mate_o.wait_recv()
    mate_gr.wait_recv()
    c = pl.ds(pl.multiple_of(rp * quarter, 128), quarter)
    n.acc[OUT[0]] = (mm(n.o[0], n.gr[:, c], TN) + mm(n.o[1], n.gr_p[...], TN)).astype(BF16)

    phase("query back")
    for h in range(H):
        head = slice(h * HD, (h + 1) * HD)
        for side in range(3):
            n.s[:, side * R : (side + 1) * R] = mm(n.go[1, :, head], n.qkv[side, :, part(2, h)], NT)

        def soft_back(t, carry, h=h):
            w = n.w[h, t, :].astype(F32)
            gp = n.s[t, :]
            delta = jnp.sum(w * gp, axis=-1, keepdims=True)
            n.low[t, :] = (w * (gp - delta)).astype(BF16)
            n.stat[t, H + h : H + h + 1] = delta
            return carry

        tiles(R, soft_back, together=4)
        total = jnp.zeros((R, HD), F32)
        for side in range(3):
            total = total + mm(n.low[:, side * R : (side + 1) * R], n.qkv[side, :, part(1, h)])
        n.gqkv[:, part(0, h)] = (total * scale).astype(BF16)
        if h < PIECES:
            hand_on(2, n.go, side_go[h : h + 1])
        service(2.3 + 1.1 * h)
    n.stats[1] = n.stat[...].T[0 : 2 * H]
    side_stats = to_sides(3, n.stats)
    phase("y")
    y = (n.resid[...] + mm(n.a[...], n.wdown[...])).astype(BF16)
    rows_gone(0, n.out_t)
    set_rows(2, n.place[...], y, n.out_t)
    send_rows(2, n.out_t, n.home_y)

    service(7.2)

    phase("sums step")
    for copy in side_stats:
        copy.wait_recv()
    far_in(2, n.go)
    phase("key back")
    for h in range(H):
        head = slice(h * HD, (h + 1) * HD)
        for side in range(3):
            span_q = slice(side * R, (side + 1) * R)
            n.s[:, span_q] = mm(n.qkv[1, :, part(1, h)], n.qkv[side, :, part(0, h)], NT)
            n.s2[:, span_q] = mm(n.qkv[1, :, part(2, h)], n.go[side, :, head], NT)

        def key_back(t, carry, h=h):
            for side in range(3):
                span_q = slice(side * R, (side + 1) * R)
                s = n.s[t, span_q] * (scale * LOG2E) + n.ck[side, t, :]
                w = jnp.exp2(s - n.stats[side, h : h + 1, :])
                n.low[t, span_q] = w.astype(BF16)
                n.low2[t, span_q] = (w * (n.s2[t, span_q] - n.stats[side, H + h : H + h + 1, :])).astype(BF16)
            return carry

        tiles(R, key_back, together=4)
        total_k = jnp.zeros((R, HD), F32)
        total_v = jnp.zeros((R, HD), F32)
        for side in range(3):
            span_q = slice(side * R, (side + 1) * R)
            total_k = total_k + mm(n.low2[:, span_q], n.qkv[side, :, part(0, h)])
            total_v = total_v + mm(n.low[:, span_q], n.go[side, :, head])
        n.gqkv[:, part(1, h)] = (total_k * scale).astype(BF16)
        n.gqkv[:, part(2, h)] = total_v.astype(BF16)
        service(9.5 + h)
    phase("send gqkv")
    wide = 3 * D // 2
    mate_gqkv = to_mate(7, n.gqkv.at[:, pl.ds(pl.multiple_of(mate * wide, 128), wide)], n.gqkv_p)
    phase("gx")
    n.tmp[...] = mm(n.gqkv[...], n.wqkv[...], NT)
    gx_ref = n.tok

    def keep1(t, gw):
        gx_ref[t, :] = (n.gresid[t, :] + gw).astype(BF16)

    gc1 = norm_back(n.tmp, 0, n.plain1, n.inv1, keep1)
    row = lax.broadcasted_iota(I32, (8, D), 0)
    sums = jnp.zeros((8, D), F32)
    for i, value in enumerate((*gc1, *gc2)):
        sums = jnp.where(row == i, value, sums)
    n.gcs[0] = sums

    def small_start(k):
        to = (me, mate) if k == 0 else (me ^ (1 << (k - 1)), rp)
        live["gc"] = remote(n.gcs.at[k], n.gcr.at[k], n.gc_ss.at[0], n.gc_rs.at[k], to)

    def small_end(k):
        live["gc"].wait_recv()
        n.gcs[k + 1] = n.gcs[k] + n.gcr[k]

    phase("wait gqkv")
    small_start(0)
    service(14.0)
    mate_gqkv.wait_recv()
    mate_normed.wait_recv()
    phase("grad qkv")
    for p in range(3):
        c = pl.ds(pl.multiple_of(rp * wide + p * BLOCK[1], 128), BLOCK[1])
        d = slice(p * BLOCK[1], (p + 1) * BLOCK[1])
        n.acc[QKV[p]] = (mm(n.normed[1], n.gqkv[:, c], TN) + mm(n.normed_p[...], n.gqkv_p[:, d], TN)).astype(BF16)
    phase("leave gx")
    service(15.6)
    small_end(0)
    rows_gone(1, n.out_c)
    set_rows(3, n.place[...], gx_ref[...], n.out_c)
    send_rows(3, n.out_c, n.home_g)
    phase("sums")
    share = -(-len(actions) // (z.bits + 1))
    for small in range(1, z.bits + 1):
        small_start(small)
        service(most=share)
        small_end(small)
    service()
    waits_for(n.grads_out.at[mate], n.core_rs.at[0])
    n.sums_out[...] = n.gcs[z.bits + 1]
    phase("home")
    rows_in(2, n.home_y)
    n.y_out[...] = mm(n.pick[...], n.home_y[...]).astype(BF16)
    rows_in(3, n.home_g)
    n.g_out[...] = mm(n.pick[...], n.home_g[...]).astype(BF16)

    phase("end")
    rows_gone(2, n.out_t)
    rows_gone(3, n.out_c)
    for copy in started:
        copy.wait_send()
    for i, ref in ((1, n.normed), (2, n.go)):
        for leg in range(2):
            waits_for(ref.at[1], n.side_ss.at[i, leg])
    waits_for(n.grads_out.at[:, :, pl.ds(0, BLOCK[0] - (BLOCK[0] >> z.halvings))], n.sum_ss.at[0])
    waits_for(n.grads_out.at[rp], n.core_ss.at[0])
    waits_for(n.gcr, n.gc_ss.at[0])


def lists_of(z, neighbours, me):
    within = neighbours & (z.R - 1)
    shift = (2 * z.R).bit_length() - 1
    away = (neighbours >> shift) - me
    after = (away == 1) | (away == 1 - z.P)
    base = jnp.where(away == 0, z.R, jnp.where(after, 2 * z.R, 0))
    return (base + within).astype(F32)


def finish(z, g_ref, sums_ref, y_ref, gx_ref, ada1_ref, ada2_ref, cond_ref, *outs):
    y_out, gx_out, qkv_out, out_out, up_out, down_out, ga1_out, ga2_out, gcond_out = outs
    i, p = pl.program_id(0), pl.program_id(1)
    down_out[...] = g_ref[i, DOWN[0] + p].astype(F32)
    up_out[...] = g_ref[i, UP[0] + p].astype(F32)

    @pl.when(p < 3)
    def _():
        qkv_out[...] = g_ref[i, QKV[0] + p].astype(F32)

    @pl.when(p == 3)
    def _():
        out_out[...] = g_ref[i, OUT[0]].astype(F32)

    @pl.when((i == 0) & (p == 0))
    def _():
        y_out[...] = y_ref[...]
        gx_out[...] = gx_ref[...]
        count = cond_ref.shape[1]
        eye = lax.broadcasted_iota(I32, (count, count), 0) == lax.broadcasted_iota(I32, (count, count), 1)
        cond = jnp.sum(jnp.where(eye, cond_ref[...], 0.0), axis=1, keepdims=True)
        d = z.D
        total = jnp.zeros((count, 1), F32)
        for row, ada, out in ((0, ada1_ref, ga1_out), (2, ada2_ref, ga2_out)):
            for j in range(2):
                c = slice(j * d, (j + 1) * d)
                sums = sums_ref[row + j : row + j + 1, :]
                out[:, c] = cond * sums
                total = total + jnp.sum(ada[:, c] * sums, axis=1, keepdims=True)
        gcond_out[...] = jnp.sum(jnp.where(eye, total, 0.0), axis=0, keepdims=True)


def local(tokens, cotangent, dest, neighbours, w_qkv, w_out, w_up, w_down, ada_attn, ada_mlp, cond):
    rows, width = tokens.shape
    z = sizes(lax.axis_size("patch"), rows, width, w_up.shape[1])
    dest = dest.reshape(1, rows)
    neighbours = neighbours.T
    cond = cond.reshape(1, cond.shape[0])
    inputs = dict(
        tokens=tokens,
        cotangent=cotangent,
        dest=dest,
        neighbours=neighbours,
        w_qkv=w_qkv,
        w_out=w_out,
        w_up=w_up,
        w_down=w_down,
        ada_attn=ada_attn,
        ada_mlp=ada_mlp,
        cond=cond,
    )
    small = ("dest", "neighbours", "cond")
    any_space = pl.BlockSpec(memory_space=pl.ANY)
    vmem = pl.BlockSpec(memory_space=pltpu.VMEM)
    shape = jax.ShapeDtypeStruct
    outs = dict(
        grads_out=pltpu.VMEM((2, STREAMS) + BLOCK, BF16),
        sums_out=pltpu.VMEM((8, width), F32),
        y_out=pltpu.VMEM((rows, width), BF16),
        g_out=pltpu.VMEM((rows, width), BF16),
    )
    held = scratch(z, neighbours.shape[0])
    held_out = pl.pallas_call(
        functools.partial(layer, z, [*inputs, *outs, *held]),
        out_shape=list(outs.values()),
        in_specs=[vmem if k in small else any_space for k in inputs],
        out_specs=[vmem, vmem, vmem, vmem],
        scratch_shapes=list(held.values()),
        compiler_params=pltpu.CompilerParams(collective_id=0, has_side_effects=True, vmem_limit_bytes=56 << 20),
        name="layer",
    )(*inputs.values())

    held_out = [pltpu.with_memory_space_constraint(v, pltpu.VMEM) for v in held_out]
    whole = lambda i, p: (0, 0)
    rows_spec = pl.BlockSpec((rows, width), whole)
    ada_spec = pl.BlockSpec(ada_attn.shape, whole)
    cond_spec = pl.BlockSpec((1, cond.shape[1]), whole)
    y, gx, g_qkv, g_out, g_up, g_down, g_ada1, g_ada2, g_cond = pl.pallas_call(
        functools.partial(finish, z),
        grid=(2, 4),
        in_specs=[
            vmem,
            vmem,
            vmem,
            vmem,
            ada_spec,
            ada_spec,
            cond_spec,
        ],
        out_specs=[
            rows_spec,
            rows_spec,
            pl.BlockSpec(BLOCK, lambda i, p: (0, i * 3 + jnp.minimum(p, 2))),
            pl.BlockSpec(BLOCK, lambda i, p: (0, i)),
            pl.BlockSpec(BLOCK, lambda i, p: (0, i * 4 + p)),
            pl.BlockSpec(BLOCK, lambda i, p: (i * 2 + p // 2, p % 2)),
            ada_spec,
            ada_spec,
            cond_spec,
        ],
        out_shape=[
            shape((rows, width), BF16),
            shape((rows, width), BF16),
            shape(w_qkv.shape, F32),
            shape(w_out.shape, F32),
            shape(w_up.shape, F32),
            shape(w_down.shape, F32),
            shape(ada_attn.shape, F32),
            shape(ada_mlp.shape, F32),
            shape(cond.shape, F32),
        ],
        compiler_params=pltpu.CompilerParams(vmem_limit_bytes=32 << 20),
        name="finish",
    )(*held_out, ada_attn, ada_mlp, cond)
    return y, gx, g_qkv, g_out, g_up, g_down, g_ada1, g_ada2, g_cond.reshape(cond.shape[1])


def solution(mesh):
    row = P(("patch", "rep"), None)
    return jax.shard_map(
        local,
        mesh=mesh,
        in_specs=(row, row, P(("patch", "rep")), row) + (P(),) * 7,
        out_specs=(row, row) + (P(),) * 7,
        check_vma=False,
    )
```

time: 161 us -> 127 us (0.79)
  Pallas kernels: 157 us -> 126 us
    pallas_call x1, Pallas kernels: 148 us -> 119 us  [local(): pl.pallas_call(functools.partial(layer, z, [*inputs, *outs, *held]), out_...]
    pallas_call x1, Pallas kernels: 9.86 us -> 6.24 us  [local(): pl.pallas_call(functools.partial(finish, z), grid=(2, 4), in_specs=[vmem,...]
where the time goes in v3:
time: 127 us; the launch traced here: 126 us
  Pallas kernels  126 us (99%)
    pallas_call x1, Pallas kernels, local(): pl.pallas_call(functools.partial(layer, z, [*inputs, *outs, *held]), out_...  119 us
    pallas_call x1, Pallas kernels, local(): pl.pallas_call(functools.partial(finish, z), grid=(2, 4), in_specs=[vmem,...  6.24 us

profile of v3, /device:TPU:0, one launch (start us, length us, event | category | flops | bytes accessed | tf_op | source)
XLA Modules:
  0.0 126.4 jit_solution(7371344246923763255)
XLA Ops:
  0.6 0.0 copy-start
  0.7 0.0 copy-start.1
  0.7 0.0 copy-start.2
  0.7 119.3 %layer.1 = (bf16[2,12,512,256]{3,2,1,0:T(8,128)(2,1)S(1)}, f32[8,512]{1,0:T(8,128)S(1)}, bf16[256,512]{1,0:T(8,128)(2,1)S(1)}, bf16[256,512]{1,0:T(8,128)(2,1)S(1)}) custom-call(bf16[256,512]{1,0:T(8,128)(2,1)} %refs_0_.1, bf16[256,512]{1,0:T(8,128)(2,1)} %refs_1_.1, s32[1,256]{1,0:T(1,128)} %bitcast.7, s32[16,256]{1,0:T(8,128)} %bitcast.6, ...), custom_call_target="tpu_custom_call" | custom-call | tf_op jit(solution)/shard_map/layer/pallas_call | solution.py:845
  120.0 0.0 copy-done
  120.0 0.0 copy-done.1
  120.0 0.0 copy-done.2
  120.0 6.2 %finish.1 = (bf16[256,512]{1,0:T(8,128)(2,1)}, bf16[256,512]{1,0:T(8,128)(2,1)}, f32[512,1536]{1,0:T(8,128)}, f32[512,512]{1,0:T(8,128)}, f32[512,2048]{1,0:T(8,...) custom-call(bf16[2,12,512,256]{3,2,1,0:T(8,128)(2,1)S(1)} %get-tuple-element.22.g_ref, ...), custom_call_target="tpu_custom_call" | custom-call | tf_op jit(solution)/shard_map/finish/pallas_call | solution.py:860
Async XLA Ops:
  0.6 119.3 %copy-start = (f32[32,1024]{1,0:T(8,128)S(1)}, f32[32,1024]{1,0:T(8,128)}, u32[]{:S(2)}) copy-start(f32[32,1024]{1,0:T(8,128)} %ada1_ref.1) | copy-start | bytes 393220
  0.7 119.3 %copy-start.1 = (f32[32,1024]{1,0:T(8,128)S(1)}, f32[32,1024]{1,0:T(8,128)}, u32[]{:S(2)}) copy-start(f32[32,1024]{1,0:T(8,128)} %ada2_ref.1) | copy-start | bytes 393220
  0.7 119.3 %copy-start.2 = (f32[32]{0:T(128)S(1)}, f32[32]{0:T(128)}, u32[]{:S(2)}) copy-start(f32[32]{0:T(128)} %param.21) | copy-start | bytes 388

commit v4 on v3

--- a/solution.py
+++ b/solution.py
@@ -43,40 +43,51 @@
     cap = rows // patches + 1
     block = -(-(cap - 1) // 16) * 16
     bits = patches.bit_length() - 1
-    halvings = 0
-    while halvings < bits and BLOCK[0] >> (halvings + 1) >= MIN_ROWS:
-        halvings += 1
     return types.SimpleNamespace(
-        P=patches, R=rows, D=width, FF=hidden, T=block, PT=patches * block, bits=bits, halvings=halvings
+        P=patches, R=rows, D=width, FF=hidden, T=block, PT=patches * block, bits=bits, stages=stages_of(bits)
     )
 
 
 XYZ, XZY, YXZ, YZX, ZXY, ZYX = itertools.permutations(range(3))
-ORDERS = [XZY, YXZ, ZYX, XZY, XYZ, YZX, ZYX, YXZ, ZYX, YXZ, XZY, XYZ]
+ORDERS = [XYZ, YXZ, ZYX, XYZ, YXZ, YXZ, XYZ, XYZ, ZXY, ZXY, YXZ, YXZ]
 DOWN, UP, OUT, QKV = range(0, 4), range(4, 8), range(8, 9), range(9, 12)
 STREAMS = len(ORDERS)
-QKV_AT = 15.3
-FREE_AT = (4.0, 5.0, 5.0)
-COMPUTES = ((-1.0, 1.2), (1.2, 2.3), (2.3, 3.4), (3.4, 4.5), (4.5, 5.6), (8.5, 9.5), (9.5, 10.5), (10.5, 11.5), (11.5, 12.5), (12.5, 14.0), (14.0, 15.3))
+SUMS_AT, QKV_AT, COEFF_AT = 6.5, 16.3, 15.5
+COMPUTES = ((-1.0, 1.2), (1.2, 2.2), (2.2, 3.6), (3.6, 5.1), (5.1, 6.5), (6.6, 7.8), (10.4, 11.4), (11.4, 12.4), (12.4, 13.4))
+COMPUTES += ((13.4, 14.4), (14.4, 15.5), (15.5, 16.2), (16.4, 17.0))
+ROWS_AT = (10.5, 17.1)
+ROW_TIMES = (3.2, 3.2, 4.8, 6.4)
 PIECES = 4
 
 
-def bit_orders(bits):
-    return [tuple(b for b in f if b < bits) + tuple(range(3, bits)) for f in ORDERS]
-
-
-def sum_plan(bits, halvings):
-    whole, delay, turn, depth = 5.7, 1.8, 0.12, 2
+def stages_of(bits):
+    found = []
+    for first in ORDERS:
+        order = [(b,) for b in first if b < bits] + [(b,) for b in range(3, bits)]
+        rows, stages = BLOCK[0], []
+        for over in order:
+            after = rows >> len(over)
+            if after < MIN_ROWS:
+                after = rows
+            stages.append((over, rows, after))
+            rows = after
+        found.append(stages)
+    return found
+
+
+def sum_plan(bits):
+    whole, delay, turn, depth = 5.7, 1.8, 0.12, 3
     steps = []
-    for order in bit_orders(bits):
-        places = [(order[k], min(k + 1, halvings)) for k in range(bits)]
-        places += [(order[k], k + 1) for k in range(halvings - 1, -1, -1)]
-        far = 2.0 if bits == 4 else 1.0
-        steps.append([(b, whole / (1 << k) * (far if b == 3 else 1.0)) for b, k in places] + [(None, 0.5)])
-    at = [0] * STREAMS
+    for stages in stages_of(bits):
+        places = stages + [stage for stage in reversed(stages) if stage[1] > stage[2]]
+        steps.append([(over[0], whole * after / BLOCK[0]) for over, _, after in places] + [(None, 0.5)])
+    steps.append([(None, 0.1)] + [(b, 0.4) for b in range(bits)])
+    at = [0] * len(steps)
     free, queued, waiting, plan = {}, {}, [], []
     number = itertools.count()
-    events = [(QKV_AT if p in QKV else FREE_AT[ORDERS[p][0]], next(number), "ready", p) for p in range(STREAMS)]
+    events = [(QKV_AT if p in QKV else SUMS_AT, next(number), "ready", p) for p in range(STREAMS)]
+    events.append((COEFF_AT, next(number), "ready", STREAMS))
+    events += [(t, next(number), "rows", None) for t in ROWS_AT]
     heapq.heapify(events)
     now = 0.0
 
@@ -85,6 +96,10 @@
 
     while events:
         t, _, kind, p = heapq.heappop(events)
+        if kind == "rows":
+            for link, time in enumerate(ROW_TIMES):
+                free[link] = max(free.get(link, 0.0), t) + time
+            continue
         if kind == "free":
             queued[p] -= 1
             kind = "look"
@@ -96,29 +111,31 @@
             waiting.append(p)
         elif kind == "end":
             now += turn
-            plan.append((now, "await", p))
+            plan.append((now, p))
             at[p] += 1
             if at[p] < len(steps[p]):
                 waiting.append(p)
-        for q in sorted(waiting):
+        for q in sorted(waiting, key=lambda q: (q < STREAMS, (q - QKV[0]) % STREAMS)):
             link, time = steps[q][at[q]]
-            if link is not None and queued.get(link, 0) >= depth:
+            uses = {None: ()}.get(link, ((2, 1), (3, 2)) if bits == 4 and link == 3 else ((link, 1),))
+            if any(queued.get(used, 0) >= depth for used, _ in uses):
                 continue
             waiting.remove(q)
             now += 0.03
-            plan.append((now, "start", q))
-            queued[link] = queued.get(link, 0) + 1
-            free[link] = max(free.get(link, 0.0), now) + time
-            heapq.heappush(events, (free[link] + delay, next(number), "end", q))
-            heapq.heappush(events, (free[link], next(number), "free", link))
+            plan.append((now, q))
+            done = now if uses else now + time
+            for used, share in uses:
+                queued[used] = queued.get(used, 0) + 1
+                free[used] = max(free.get(used, 0.0), now) + time * share
+                heapq.heappush(events, (free[used], next(number), "free", used))
+                done = max(done, free[used])
+            heapq.heappush(events, (done + delay, next(number), "end", q))
     return plan
 
 
 def scratch(z, nb):
     R, D, FF, PT, PS = z.R, z.D, z.FF, z.PT, z.PT + z.P
-    recv_rows = []
-    for k in range(z.bits):
-        recv_rows.append(BLOCK[0] >> (min(k + 1, z.halvings)))
+    stages = z.stages[0]
     vm, dma = pltpu.VMEM, pltpu.SemaphoreType.DMA
     s = dict(
         tok=vm((R, D), BF16),
@@ -177,7 +194,7 @@
         gqkv=vm((R, 3 * D), BF16),
         gqkv_p=vm((R, 3 * D // 2), BF16),
         acc=vm((STREAMS,) + BLOCK, BF16),
-        **{f"rcv{k}": vm((STREAMS, n, BLOCK[1]), BF16) for k, n in enumerate(recv_rows)},
+        **{f"rcv{k}": vm((STREAMS, (1 << len(b)) - 1, n, BLOCK[1]), BF16) for k, (b, _, n) in enumerate(stages)},
         gcs=vm((z.bits + 2, 8, D), F32),
         gcr=vm((z.bits + 1, 8, D), F32),
         load_sem=dma((8,)),
@@ -193,9 +210,9 @@
         pair_ss=dma((8,)),
         pair_rs=dma((8,)),
         sum_ss=dma((1,)),
-        late_ss=dma((STREAMS, max(z.bits - z.halvings, 1))),
-        rs_rs=dma((STREAMS, z.bits)),
-        ag_rs=dma((STREAMS, z.halvings)),
+        late_ss=dma((STREAMS, len(stages))),
+        rs_rs=dma((STREAMS, len(stages))),
+        ag_rs=dma((STREAMS, len(stages))),
         core_ss=dma((1,)),
         core_rs=dma((1,)),
         gc_ss=dma((1,)),
@@ -265,7 +282,7 @@
 
     def send_rows(i, src, dst):
         def one(j, carry):
-            to = lax.rem(me + j, Pn)
+            to = me ^ (Pn - j)
             pltpu.make_async_remote_copy(
                 src_ref=src.at[pl.ds(pl.multiple_of(to * T, 16), T)],
                 dst_ref=dst.at[pl.ds(pl.multiple_of(me * T, 16), T)],
@@ -320,18 +337,15 @@
             remote(ref.at[1], ref.at[2], n.side_ss.at[i, 1], n.side_rs.at[i, 1], (prv, rp), True),
         )
 
-    def to_near(i, ref):
+    def to_near(i, ref, c):
         size = R // PIECES
-        return [
-            remote(
-                ref.at[1, pl.ds(c * size, size)],
-                ref.at[far_slot, pl.ds(c * size, size)],
-                n.side_ss.at[i, 0],
-                n.piece_rs.at[i - 1, c],
-                (near, rp),
-            )
-            for c in range(PIECES)
-        ]
+        return remote(
+            ref.at[1, pl.ds(c * size, size)],
+            ref.at[far_slot, pl.ds(c * size, size)],
+            n.side_ss.at[i, 0],
+            n.piece_rs.at[i - 1, c],
+            (near, rp),
+        )
 
     def hand_on(i, ref, copies):
         size = R // PIECES
@@ -432,7 +446,7 @@
     place_t = place.T.astype(BF16)
     n.x[...] = mm(place_t, n.in_t[...])
 
-    def norm(src, coeffs, plain_ref, inv_ref, out):
+    def norm(src, coeffs, plain_ref, inv_ref, out, after=None):
         def one(t, carry):
             v = src[t, :]
             centred = v - jnp.sum(v, axis=-1, keepdims=True) * (1.0 / D)
@@ -443,7 +457,12 @@
             out[t, :] = (plain * (1.0 + n.c[coeffs : coeffs + 1, :D]) + n.c[coeffs : coeffs + 1, D:]).astype(BF16)
             return carry
 
-        tiles(R, one)
+        for c in range(PIECES):
+            size = R // PIECES
+            for j in range(size // TILE):
+                one(pl.ds(c * size + j * TILE, TILE), 0)
+            if after:
+                after(c)
 
     def norm_back(grad, coeffs, plain_ref, inv_ref, finish):
         def one(t, carry):
@@ -459,11 +478,11 @@
             )
 
         zero = jnp.zeros((1, D), F32)
-        return tiles(R, one, (zero, zero))
+        return tiles(R, one, (zero, zero), together=4)
 
     phase("norm")
-    norm(n.x, 0, n.plain1, n.inv1, n.normed.at[1])
-    side_normed = to_near(1, n.normed)
+    side_normed = []
+    norm(n.x, 0, n.plain1, n.inv1, n.normed.at[1], lambda c: side_normed.append(to_near(1, n.normed, c)))
     mate_normed = to_mate(0, n.normed.at[1], n.normed_p)
     phase("project")
     get_wqkv.wait()
@@ -502,7 +521,7 @@
             n.stat[t, h : h + 1] = top + jnp.log2(total)
             return carry
 
-        tiles(R, soft, together=4)
+        tiles(R, soft, together=8)
         mixed = jnp.zeros((R, HD), F32)
         for side in range(3):
             mixed = mixed + mm(n.w[h, :, side * R : (side + 1) * R], n.qkv[side, :, part(2, h)])
@@ -534,7 +553,7 @@
             n.gu[t, c] = (n.ga[t, :] * sig * (1.0 + u * (1.0 - sig))).astype(BF16)
             return carry
 
-        tiles(R, gate)
+        tiles(R, gate, together=8)
     theirs = pl.ds(pl.multiple_of(mate * half, 128), half)
     ours = pl.ds(pl.multiple_of(rp * half, 128), half)
     mate_a = to_mate(4, n.a.at[:, theirs], n.a_p)
@@ -550,53 +569,57 @@
     gc2 = norm_back(n.tmp, 8, n.plain2, n.inv2, keep2)
     phase("go")
     n.go[1] = mm(n.gr[...], n.wout[...], NT).astype(BF16)
-    side_go = to_near(2, n.go)
+    side_go = [to_near(2, n.go, c) for c in range(PIECES)]
     quarter = D // 2
     mate_gr = to_mate(6, n.gr.at[:, pl.ds(pl.multiple_of(mate * quarter, 128), quarter)], n.gr_p)
-    orders = bit_orders(z.bits)
-    top_rows = BLOCK[0]
-
-    def bit(p, k):
-        return (me >> orders[p][k]) & 1
+    live = {}
+
+    def place_in(p, k):
+        return sum(((me >> b) & 1) << i for i, b in enumerate(z.stages[p][k][0]))
 
     def start_of(p, k):
-        at = 0
-        for i in range(k):
-            at = at + bit(p, i) * (top_rows >> (i + 1))
-        return at
+        return sum(place_in(p, i) * z.stages[p][i][2] for i in range(k) if z.stages[p][i][1] > z.stages[p][i][2])
 
     def span(p, k):
-        k = min(k, z.halvings)
-        rows = top_rows >> k
+        rows = z.stages[p][k - 1][2] if k else BLOCK[0]
         return pl.ds(pl.multiple_of(start_of(p, k), rows) if k else 0, rows)
 
-    def partner(p, k):
-        return (me ^ (1 << orders[p][k]), rp)
-
-    live = {}
+    def partners(p, k):
+        over = z.stages[p][k][0]
+        for j in range(1, 1 << len(over)):
+            yield j, (me ^ sum(1 << b for i, b in enumerate(over) if j >> i & 1), rp)
 
     def reduce_start(p, k):
-        if k < z.halvings:
-            rows = top_rows >> (k + 1)
-            gone = (1 - bit(p, k)) * rows + start_of(p, k)
-            src = n.acc.at[p, pl.ds(pl.multiple_of(gone, rows), rows)]
-        else:
-            src = n.acc.at[p, span(p, k)]
-        ss = n.sum_ss.at[0] if k < z.halvings else n.late_ss.at[p, k - z.halvings]
-        live[p] = remote(src, getattr(n, f"rcv{k}").at[p], ss, n.rs_rs.at[p, k], partner(p, k))
+        _, rows, after = z.stages[p][k]
+        for j, to in partners(p, k):
+            if after < rows:
+                at = start_of(p, k) + (place_in(p, k) ^ j) * after
+                src, ss = n.acc.at[p, pl.ds(pl.multiple_of(at, after), after)], n.sum_ss.at[0]
+            else:
+                src, ss = n.acc.at[p, span(p, k)], n.late_ss.at[p, k]
+            live[p] = remote(src, getattr(n, f"rcv{k}").at[p, j - 1], ss, n.rs_rs.at[p, k], to)
 
     def reduce_end(p, k):
-        live[p].wait_recv()
-        if k >= z.halvings:
+        _, rows, after = z.stages[p][k]
+        got = getattr(n, f"rcv{k}")
+        waits_for(got.at[p], n.rs_rs.at[p, k])
+        if after == rows:
             live[p].wait_send()
         kept = span(p, k + 1)
-        total = n.acc[p, kept].astype(F32) + getattr(n, f"rcv{k}")[p].astype(F32)
-        into = n.grads_out.at[rp, p, kept] if k + 1 == z.bits else n.acc.at[p, kept]
+        total = n.acc[p, kept].astype(F32)
+        for j in range(got.shape[1]):
+            total = total + got[p, j].astype(F32)
+        into = n.grads_out.at[rp, p, kept] if k + 1 == len(z.stages[p]) else n.acc.at[p, kept]
         into[...] = total.astype(BF16)
 
     def gather_start(p, k):
         ref = n.grads_out.at[rp, p, span(p, k + 1)]
-        live[p] = remote(ref, ref, n.sum_ss.at[0], n.ag_rs.at[p, k], partner(p, k))
+        for _, to in partners(p, k):
+            remote(ref, ref, n.sum_ss.at[0], n.ag_rs.at[p, k], to)
+
+    def gather_end(p, k):
+        _, rows, after = z.stages[p][k]
+        waits_for(n.grads_out.at[rp, p, pl.ds(0, rows - after)], n.ag_rs.at[p, k])
 
     def core_start(p):
         ref = n.grads_out.at[rp, p]
@@ -605,18 +628,32 @@
     steps_left = {}
     for p in range(STREAMS):
         steps = []
-        for k in range(z.bits):
+        kept = [k for k, stage in enumerate(z.stages[p]) if stage[1] > stage[2]]
+        for k in range(len(z.stages[p])):
             steps += [functools.partial(reduce_start, p, k), functools.partial(reduce_end, p, k)]
-        for k in range(z.halvings - 1, -1, -1):
-            steps += [functools.partial(gather_start, p, k), lambda p=p: live[p].wait_recv()]
+        for k in reversed(kept):
+            steps += [functools.partial(gather_start, p, k), functools.partial(gather_end, p, k)]
         steps += [functools.partial(core_start, p), lambda: None]
         steps_left[p] = steps
-    actions = sum_plan(z.bits, z.halvings)
-
-    def service(until=None, most=None):
-        while actions and (until is None or actions[0][0] <= until) and (most is None or most > 0):
-            most = None if most is None else most - 1
-            steps_left[actions.pop(0)[2]].pop(0)()
+
+    def small_start(k):
+        to = (me, mate) if k == 0 else (me ^ (1 << (k - 1)), rp)
+        live["gc"] = remote(n.gcs.at[k], n.gcr.at[k], n.gc_ss.at[0], n.gc_rs.at[k], to)
+
+    def small_end(k):
+        live["gc"].wait_recv()
+        n.gcs[k + 1] = n.gcs[k] + n.gcr[k]
+
+    steps = []
+    for k in range(z.bits + 1):
+        steps += [functools.partial(small_start, k), functools.partial(small_end, k)]
+    steps_left[STREAMS] = steps
+    actions = sum_plan(z.bits)
+
+    def service(until=None):
+        while actions and (until is None or actions[0][0] <= until):
+            phase(f"sums {2 * int(actions[0][0] / 2)}")
+            steps_left[actions.pop(0)[1]].pop(0)()
 
     phase("grad down")
     mate_ups.wait_recv()
@@ -653,28 +690,27 @@
             n.stat[t, H + h : H + h + 1] = delta
             return carry
 
-        tiles(R, soft_back, together=4)
+        tiles(R, soft_back, together=8)
         total = jnp.zeros((R, HD), F32)
         for side in range(3):
             total = total + mm(n.low[:, side * R : (side + 1) * R], n.qkv[side, :, part(1, h)])
         n.gqkv[:, part(0, h)] = (total * scale).astype(BF16)
         if h < PIECES:
             hand_on(2, n.go, side_go[h : h + 1])
-        service(2.3 + 1.1 * h)
     n.stats[1] = n.stat[...].T[0 : 2 * H]
     side_stats = to_sides(3, n.stats)
     phase("y")
     y = (n.resid[...] + mm(n.a[...], n.wdown[...])).astype(BF16)
     rows_gone(0, n.out_t)
     set_rows(2, n.place[...], y, n.out_t)
-    send_rows(2, n.out_t, n.home_y)
-
-    service(7.2)
+
+    service(10.3)
 
     phase("sums step")
     for copy in side_stats:
         copy.wait_recv()
     far_in(2, n.go)
+    send_rows(2, n.out_t, n.home_y)
     phase("key back")
     for h in range(H):
         head = slice(h * HD, (h + 1) * HD)
@@ -701,7 +737,7 @@
             total_v = total_v + mm(n.low[:, span_q], n.go[side, :, head])
         n.gqkv[:, part(1, h)] = (total_k * scale).astype(BF16)
         n.gqkv[:, part(2, h)] = total_v.astype(BF16)
-        service(9.5 + h)
+        service(11.45 + h)
     phase("send gqkv")
     wide = 3 * D // 2
     mate_gqkv = to_mate(7, n.gqkv.at[:, pl.ds(pl.multiple_of(mate * wide, 128), wide)], n.gqkv_p)
@@ -719,17 +755,7 @@
         sums = jnp.where(row == i, value, sums)
     n.gcs[0] = sums
 
-    def small_start(k):
-        to = (me, mate) if k == 0 else (me ^ (1 << (k - 1)), rp)
-        live["gc"] = remote(n.gcs.at[k], n.gcr.at[k], n.gc_ss.at[0], n.gc_rs.at[k], to)
-
-    def small_end(k):
-        live["gc"].wait_recv()
-        n.gcs[k + 1] = n.gcs[k] + n.gcr[k]
-
-    phase("wait gqkv")
-    small_start(0)
-    service(14.0)
+    service(15.6)
     mate_gqkv.wait_recv()
     mate_normed.wait_recv()
     phase("grad qkv")
@@ -738,17 +764,11 @@
         d = slice(p * BLOCK[1], (p + 1) * BLOCK[1])
         n.acc[QKV[p]] = (mm(n.normed[1], n.gqkv[:, c], TN) + mm(n.normed_p[...], n.gqkv_p[:, d], TN)).astype(BF16)
     phase("leave gx")
-    service(15.6)
-    small_end(0)
+    service(16.5)
     rows_gone(1, n.out_c)
     set_rows(3, n.place[...], gx_ref[...], n.out_c)
     send_rows(3, n.out_c, n.home_g)
     phase("sums")
-    share = -(-len(actions) // (z.bits + 1))
-    for small in range(1, z.bits + 1):
-        small_start(small)
-        service(most=share)
-        small_end(small)
     service()
     waits_for(n.grads_out.at[mate], n.core_rs.at[0])
     n.sums_out[...] = n.gcs[z.bits + 1]
@@ -766,7 +786,7 @@
     for i, ref in ((1, n.normed), (2, n.go)):
         for leg in range(2):
             waits_for(ref.at[1], n.side_ss.at[i, leg])
-    waits_for(n.grads_out.at[:, :, pl.ds(0, BLOCK[0] - (BLOCK[0] >> z.halvings))], n.sum_ss.at[0])
+    waits_for(n.grads_out.at[:, :, pl.ds(0, BLOCK[0] - z.stages[0][-1][2])], n.sum_ss.at[0])
     waits_for(n.grads_out.at[rp], n.core_ss.at[0])
     waits_for(n.gcr, n.gc_ss.at[0])
 
@@ -780,36 +800,41 @@
     return (base + within).astype(F32)
 
 
-def finish(z, g_ref, sums_ref, y_ref, gx_ref, ada1_ref, ada2_ref, cond_ref, *outs):
-    y_out, gx_out, qkv_out, out_out, up_out, down_out, ga1_out, ga2_out, gcond_out = outs
-    i, p = pl.program_id(0), pl.program_id(1)
-    down_out[...] = g_ref[i, DOWN[0] + p].astype(F32)
-    up_out[...] = g_ref[i, UP[0] + p].astype(F32)
-
-    @pl.when(p < 3)
-    def _():
-        qkv_out[...] = g_ref[i, QKV[0] + p].astype(F32)
-
-    @pl.when(p == 3)
-    def _():
-        out_out[...] = g_ref[i, OUT[0]].astype(F32)
-
-    @pl.when((i == 0) & (p == 0))
-    def _():
-        y_out[...] = y_ref[...]
-        gx_out[...] = gx_ref[...]
-        count = cond_ref.shape[1]
-        eye = lax.broadcasted_iota(I32, (count, count), 0) == lax.broadcasted_iota(I32, (count, count), 1)
-        cond = jnp.sum(jnp.where(eye, cond_ref[...], 0.0), axis=1, keepdims=True)
-        d = z.D
-        total = jnp.zeros((count, 1), F32)
-        for row, ada, out in ((0, ada1_ref, ga1_out), (2, ada2_ref, ga2_out)):
-            for j in range(2):
-                c = slice(j * d, (j + 1) * d)
-                sums = sums_ref[row + j : row + j + 1, :]
-                out[:, c] = cond * sums
-                total = total + jnp.sum(ada[:, c] * sums, axis=1, keepdims=True)
-        gcond_out[...] = jnp.sum(jnp.where(eye, total, 0.0), axis=0, keepdims=True)
+def finish(z, g_ref, sums_ref, y_ref, gx_ref, ada1_ref, ada2_ref, cond_ref, *rest):
+    y_out, gx_out, qkv_out, out_out, up_out, down_out, ga1_out, ga2_out, gcond_out, wide, wide_sem, row_sem = rest
+    rows = [pltpu.make_async_copy(a, b, row_sem.at[i]) for i, (a, b) in enumerate(((y_ref, y_out), (gx_ref, gx_out)))]
+    for copy in rows:
+        copy.start()
+    high, across = BLOCK
+    copies = []
+    for i in range(2):
+        for p in range(STREAMS):
+            if p in DOWN:
+                r, c, out = 2 * i + p // 2, p % 2, down_out
+            elif p in UP:
+                r, c, out = 0, len(UP) * i + p - UP[0], up_out
+            elif p in OUT:
+                r, c, out = 0, i, out_out
+            else:
+                r, c, out = 0, len(QKV) * i + p - QKV[0], qkv_out
+            wide[i, p] = g_ref[i, p].astype(F32)
+            to = out.at[r * high : (r + 1) * high, c * across : (c + 1) * across]
+            copies.append(pltpu.make_async_copy(wide.at[i, p], to, wide_sem.at[i, p]))
+            copies[-1].start()
+    count = cond_ref.shape[1]
+    eye = lax.broadcasted_iota(I32, (count, count), 0) == lax.broadcasted_iota(I32, (count, count), 1)
+    cond = jnp.sum(jnp.where(eye, cond_ref[...], 0.0), axis=1, keepdims=True)
+    d = z.D
+    total = jnp.zeros((count, 1), F32)
+    for row, ada, out in ((0, ada1_ref, ga1_out), (2, ada2_ref, ga2_out)):
+        for j in range(2):
+            c = slice(j * d, (j + 1) * d)
+            sums = sums_ref[row + j : row + j + 1, :]
+            out[:, c] = cond * sums
+            total = total + jnp.sum(ada[:, c] * sums, axis=1, keepdims=True)
+    gcond_out[...] = jnp.sum(jnp.where(eye, total, 0.0), axis=0, keepdims=True)
+    for copy in (*copies, *rows):
+        copy.wait()
 
 
 def local(tokens, cotangent, dest, neighbours, w_qkv, w_out, w_up, w_down, ada_attn, ada_mlp, cond):
@@ -853,32 +878,14 @@
     )(*inputs.values())
 
     held_out = [pltpu.with_memory_space_constraint(v, pltpu.VMEM) for v in held_out]
-    whole = lambda i, p: (0, 0)
-    rows_spec = pl.BlockSpec((rows, width), whole)
-    ada_spec = pl.BlockSpec(ada_attn.shape, whole)
-    cond_spec = pl.BlockSpec((1, cond.shape[1]), whole)
     y, gx, g_qkv, g_out, g_up, g_down, g_ada1, g_ada2, g_cond = pl.pallas_call(
         functools.partial(finish, z),
-        grid=(2, 4),
-        in_specs=[
-            vmem,
-            vmem,
-            vmem,
-            vmem,
-            ada_spec,
-            ada_spec,
-            cond_spec,
-        ],
-        out_specs=[
-            rows_spec,
-            rows_spec,
-            pl.BlockSpec(BLOCK, lambda i, p: (0, i * 3 + jnp.minimum(p, 2))),
-            pl.BlockSpec(BLOCK, lambda i, p: (0, i)),
-            pl.BlockSpec(BLOCK, lambda i, p: (0, i * 4 + p)),
-            pl.BlockSpec(BLOCK, lambda i, p: (i * 2 + p // 2, p % 2)),
-            ada_spec,
-            ada_spec,
-            cond_spec,
+        in_specs=[vmem] * 7,
+        out_specs=[any_space] * 6 + [vmem] * 3,
+        scratch_shapes=[
+            pltpu.VMEM((2, STREAMS) + BLOCK, F32),
+            pltpu.SemaphoreType.DMA((2, STREAMS)),
+            pltpu.SemaphoreType.DMA((2,)),
         ],
         out_shape=[
             shape((rows, width), BF16),

time: 127 us -> 124 us (0.976)
  Pallas kernels: 126 us -> 122 us
    pallas_call x1, Pallas kernels: 119 us -> 116 us  [local(): pl.pallas_call(functools.partial(layer, z, [*inputs, *outs, *held]), out_...]
where the time goes in v4:
time: 124 us; the launch traced here: 123 us
  Pallas kernels  122 us (98%)
    pallas_call x1, Pallas kernels, local(): pl.pallas_call(functools.partial(layer, z, [*inputs, *outs, *held]), out_...  116 us
    pallas_call x1, Pallas kernels, local(): pl.pallas_call(functools.partial(finish, z), in_specs=[vmem] * 7, out_spe...  5.68 us

profile of v4, /device:TPU:0, one launch (start us, length us, event | category | flops | bytes accessed | tf_op | source)
XLA Modules:
  0.0 123.0 jit_solution(417291795658034553)
XLA Ops:
  0.6 0.0 copy-start
  0.7 0.0 copy-start.1
  0.7 0.0 copy-start.2
  0.7 116.4 %layer.1 = (bf16[2,12,512,256]{3,2,1,0:T(8,128)(2,1)S(1)}, f32[8,512]{1,0:T(8,128)S(1)}, bf16[256,512]{1,0:T(8,128)(2,1)S(1)}, bf16[256,512]{1,0:T(8,128)(2,1)S(1)}) custom-call(bf16[256,512]{1,0:T(8,128)(2,1)} %refs_0_.1, bf16[256,512]{1,0:T(8,128)(2,1)} %refs_1_.1, s32[1,256]{1,0:T(1,128)} %bitcast.7, s32[16,256]{1,0:T(8,128)} %bitcast.6, ...), custom_call_target="tpu_custom_call" | custom-call | tf_op jit(solution)/shard_map/layer/pallas_call | solution.py:870
  117.1 0.0 copy-done
  117.1 0.0 copy-done.1
  117.1 0.0 copy-done.2
  117.2 5.7 %finish.1 = (bf16[256,512]{1,0:T(8,128)(2,1)}, bf16[256,512]{1,0:T(8,128)(2,1)}, f32[512,1536]{1,0:T(8,128)}, f32[512,512]{1,0:T(8,128)}, f32[512,2048]{1,0:T(8,...) custom-call(bf16[2,12,512,256]{3,2,1,0:T(8,128)(2,1)S(1)} %get-tuple-element.22.g_ref, ...), custom_call_target="tpu_custom_call" | custom-call | tf_op jit(solution)/shard_map/finish/pallas_call | solution.py:881
Async XLA Ops:
  0.6 116.5 %copy-start = (f32[32,1024]{1,0:T(8,128)S(1)}, f32[32,1024]{1,0:T(8,128)}, u32[]{:S(2)}) copy-start(f32[32,1024]{1,0:T(8,128)} %ada1_ref.1) | copy-start | bytes 393220
  0.7 116.5 %copy-start.1 = (f32[32,1024]{1,0:T(8,128)S(1)}, f32[32,1024]{1,0:T(8,128)}, u32[]{:S(2)}) copy-start(f32[32,1024]{1,0:T(8,128)} %ada2_ref.1) | copy-start | bytes 393220
  0.7 116.5 %copy-start.2 = (f32[32]{0:T(128)S(1)}, f32[32]{0:T(128)}, u32[]{:S(2)}) copy-start(f32[32]{0:T(128)} %param.21) | copy-start | bytes 388

commit v5 on v4

--- a/solution.py
+++ b/solution.py
@@ -24,7 +24,7 @@
 NEVER = -1e30
 LOG2E = 1.4426950408889634
 BLOCK = (512, 256)
-MIN_ROWS = 16
+MIN_ROWS = 64
 
 
 def mm(a, b, dims=NN):
@@ -49,14 +49,14 @@
 
 
 XYZ, XZY, YXZ, YZX, ZXY, ZYX = itertools.permutations(range(3))
-ORDERS = [XYZ, YXZ, ZYX, XYZ, YXZ, YXZ, XYZ, XYZ, ZXY, ZXY, YXZ, YXZ]
+ORDERS = [ZXY, ZXY, ZXY, YXZ, XYZ, XYZ, YXZ, XYZ, YXZ, YZX, XYZ, YXZ]
 DOWN, UP, OUT, QKV = range(0, 4), range(4, 8), range(8, 9), range(9, 12)
 STREAMS = len(ORDERS)
-SUMS_AT, QKV_AT, COEFF_AT = 6.5, 16.3, 15.5
-COMPUTES = ((-1.0, 1.2), (1.2, 2.2), (2.2, 3.6), (3.6, 5.1), (5.1, 6.5), (6.6, 7.8), (10.4, 11.4), (11.4, 12.4), (12.4, 13.4))
+SUMS_AT, FIRST_AT = (6.4, 8.5, 9.5), (6.4, 2.2, 2.2)
+QKV_AT, COEFF_AT = 16.3, 15.5
+COMPUTES = ((-1.0, 2.2), (2.3, 3.0), (3.0, 3.6), (3.6, 5.1), (5.1, 6.4), (10.4, 11.4), (11.4, 12.4), (12.4, 13.4))
 COMPUTES += ((13.4, 14.4), (14.4, 15.5), (15.5, 16.2), (16.4, 17.0))
-ROWS_AT = (10.5, 17.1)
-ROW_TIMES = (3.2, 3.2, 4.8, 6.4)
+ROW_LOADS = ((1.2, (0.0, 1.6, 2.4, 3.2)), (3.0, (3.0, 5.7, 2.9)), (10.5, (3.2, 1.6, 2.4, 3.2)), (17.1, (3.2, 3.2, 4.8, 6.4)))
 PIECES = 4
 
 
@@ -85,9 +85,14 @@
     at = [0] * len(steps)
     free, queued, waiting, plan = {}, {}, [], []
     number = itertools.count()
-    events = [(QKV_AT if p in QKV else SUMS_AT, next(number), "ready", p) for p in range(STREAMS)]
+    events, begun = [], set()
+    for p in range(STREAMS):
+        first = ORDERS[p][0]
+        begin = QKV_AT if p in QKV else SUMS_AT[first] if first in begun else FIRST_AT[first]
+        events.append((begin, next(number), "ready", p))
+        begun.add(first)
     events.append((COEFF_AT, next(number), "ready", STREAMS))
-    events += [(t, next(number), "rows", None) for t in ROWS_AT]
+    events += [(t, next(number), "rows", times) for t, times in ROW_LOADS]
     heapq.heapify(events)
     now = 0.0
 
@@ -97,7 +102,7 @@
     while events:
         t, _, kind, p = heapq.heappop(events)
         if kind == "rows":
-            for link, time in enumerate(ROW_TIMES):
+            for link, time in enumerate(p):
                 free[link] = max(free.get(link, 0.0), t) + time
             continue
         if kind == "free":
@@ -179,6 +184,7 @@
         low=vm((R, 3 * R), BF16),
         low2=vm((R, 3 * R), BF16),
         o=vm((2, R, D), BF16),
+        wide_o=vm((R, D), F32),
         u=vm((R, D), F32),
         ga=vm((R, D), F32),
         a=vm((R, FF), BF16),
@@ -280,9 +286,9 @@
             started.append(copy)
         return copy
 
-    def send_rows(i, src, dst):
+    def send_rows(i, src, dst, odd=None):
         def one(j, carry):
-            to = me ^ (Pn - j)
+            to = me ^ (Pn - j if odd is None else Pn + odd - 2 * j)
             pltpu.make_async_remote_copy(
                 src_ref=src.at[pl.ds(pl.multiple_of(to * T, 16), T)],
                 dst_ref=dst.at[pl.ds(pl.multiple_of(me * T, 16), T)],
@@ -301,7 +307,9 @@
             ).start()
             return carry
 
-        lax.fori_loop(1, Pn, one, 0)
+        lax.fori_loop(1, Pn if odd is None else Pn // 2 + odd, one, 0)
+        if odd == 0:
+            return
         mine = pl.ds(pl.multiple_of(me * T, 16), T)
         pltpu.make_async_copy(src.at[mine], dst.at[mine], n.own_sem.at[i]).start()
         pltpu.make_async_copy(n.more_out.at[i, me], n.more_in.at[i, me], n.more_own.at[i]).start()
@@ -484,6 +492,7 @@
     side_normed = []
     norm(n.x, 0, n.plain1, n.inv1, n.normed.at[1], lambda c: side_normed.append(to_near(1, n.normed, c)))
     mate_normed = to_mate(0, n.normed.at[1], n.normed_p)
+    send_rows(1, n.out_c, n.in_c, 0)
     phase("project")
     get_wqkv.wait()
 
@@ -495,7 +504,7 @@
     project(1)
     phase("wait halo")
     hand_on(1, n.normed, side_normed)
-    send_rows(1, n.out_c, n.in_c)
+    send_rows(1, n.out_c, n.in_c, 1)
     project(near_slot)
     phase("wait far")
     far_in(1, n.normed)
@@ -525,6 +534,7 @@
         mixed = jnp.zeros((R, HD), F32)
         for side in range(3):
             mixed = mixed + mm(n.w[h, :, side * R : (side + 1) * R], n.qkv[side, :, part(2, h)])
+        n.wide_o[:, h * HD : (h + 1) * HD] = mixed
         n.o[0, :, h * HD : (h + 1) * HD] = mixed.astype(BF16)
     mate_o = to_mate(2, n.o.at[0], n.o.at[1])
 
@@ -570,6 +580,16 @@
     phase("go")
     n.go[1] = mm(n.gr[...], n.wout[...], NT).astype(BF16)
     side_go = [to_near(2, n.go, c) for c in range(PIECES)]
+
+    def against(t, carry):
+        product = n.go[1, t, :].astype(F32) * n.wide_o[t, :]
+        for h in range(H):
+            n.stat[t, H + h : H + h + 1] = jnp.sum(product[:, h * HD : (h + 1) * HD], axis=-1, keepdims=True)
+        return carry
+
+    tiles(R, against, together=8)
+    n.stats[1] = n.stat[...].T[0 : 2 * H]
+    side_stats = to_sides(3, n.stats)
     quarter = D // 2
     mate_gr = to_mate(6, n.gr.at[:, pl.ds(pl.multiple_of(mate * quarter, 128), quarter)], n.gr_p)
     live = {}
@@ -655,6 +675,11 @@
             phase(f"sums {2 * int(actions[0][0] / 2)}")
             steps_left[actions.pop(0)[1]].pop(0)()
 
+    phase("y")
+    y = (n.resid[...] + mm(n.a[...], n.wdown[...])).astype(BF16)
+    rows_gone(0, n.out_t)
+    set_rows(2, n.place[...], y, n.out_t)
+    send_rows(2, n.out_t, n.home_y, 0)
     phase("grad down")
     mate_ups.wait_recv()
     mate_a.wait_recv()
@@ -677,6 +702,7 @@
     n.acc[OUT[0]] = (mm(n.o[0], n.gr[:, c], TN) + mm(n.o[1], n.gr_p[...], TN)).astype(BF16)
 
     phase("query back")
+    service(2.25)
     for h in range(H):
         head = slice(h * HD, (h + 1) * HD)
         for side in range(3):
@@ -685,9 +711,7 @@
         def soft_back(t, carry, h=h):
             w = n.w[h, t, :].astype(F32)
             gp = n.s[t, :]
-            delta = jnp.sum(w * gp, axis=-1, keepdims=True)
-            n.low[t, :] = (w * (gp - delta)).astype(BF16)
-            n.stat[t, H + h : H + h + 1] = delta
+            n.low[t, :] = (w * (gp - n.stat[t, H + h : H + h + 1])).astype(BF16)
             return carry
 
         tiles(R, soft_back, together=8)
@@ -697,20 +721,16 @@
         n.gqkv[:, part(0, h)] = (total * scale).astype(BF16)
         if h < PIECES:
             hand_on(2, n.go, side_go[h : h + 1])
-    n.stats[1] = n.stat[...].T[0 : 2 * H]
-    side_stats = to_sides(3, n.stats)
-    phase("y")
-    y = (n.resid[...] + mm(n.a[...], n.wdown[...])).astype(BF16)
-    rows_gone(0, n.out_t)
-    set_rows(2, n.place[...], y, n.out_t)
-
+        service((3.05, 3.65, 5.15, 6.45)[h])
     service(10.3)
 
     phase("sums step")
     for copy in side_stats:
         copy.wait_recv()
+    phase("far go")
     far_in(2, n.go)
-    send_rows(2, n.out_t, n.home_y)
+    phase("send y")
+    send_rows(2, n.out_t, n.home_y, 1)
     phase("key back")
     for h in range(H):
         head = slice(h * HD, (h + 1) * HD)

time: 124 us -> 112 us (0.903)
  Pallas kernels: 122 us -> 110 us
    pallas_call x1, Pallas kernels: 116 us -> 104 us  [local(): pl.pallas_call(functools.partial(layer, z, [*inputs, *outs, *held]), out_...]
where the time goes in v5:
time: 112 us; the launch traced here: 111 us
  Pallas kernels  110 us (98%)
    pallas_call x1, Pallas kernels, local(): pl.pallas_call(functools.partial(layer, z, [*inputs, *outs, *held]), out_...  104 us
    pallas_call x1, Pallas kernels, local(): pl.pallas_call(functools.partial(finish, z), in_specs=[vmem] * 7, out_spe...  5.68 us

profile of v5, /device:TPU:0, one launch (start us, length us, event | category | flops | bytes accessed | tf_op | source)
XLA Modules:
  0.0 111.0 jit_solution(17557622278485073823)
XLA Ops:
  0.6 0.0 copy-start
  0.7 0.0 copy-start.1
  0.7 0.0 copy-start.2
  0.7 104.5 %layer.1 = (bf16[2,12,512,256]{3,2,1,0:T(8,128)(2,1)S(1)}, f32[8,512]{1,0:T(8,128)S(1)}, bf16[256,512]{1,0:T(8,128)(2,1)S(1)}, bf16[256,512]{1,0:T(8,128)(2,1)S(1)}) custom-call(bf16[256,512]{1,0:T(8,128)(2,1)} %refs_0_.1, bf16[256,512]{1,0:T(8,128)(2,1)} %refs_1_.1, s32[1,256]{1,0:T(1,128)} %bitcast.7, s32[16,256]{1,0:T(8,128)} %bitcast.6, ...), custom_call_target="tpu_custom_call" | custom-call | tf_op jit(solution)/shard_map/layer/pallas_call | solution.py:890
  105.2 0.0 copy-done
  105.2 0.0 copy-done.1
  105.2 0.0 copy-done.2
  105.2 5.7 %finish.1 = (bf16[256,512]{1,0:T(8,128)(2,1)}, bf16[256,512]{1,0:T(8,128)(2,1)}, f32[512,1536]{1,0:T(8,128)}, f32[512,512]{1,0:T(8,128)}, f32[512,2048]{1,0:T(8,...) custom-call(bf16[2,12,512,256]{3,2,1,0:T(8,128)(2,1)S(1)} %get-tuple-element.22.g_ref, ...), custom_call_target="tpu_custom_call" | custom-call | tf_op jit(solution)/shard_map/finish/pallas_call | solution.py:901
Async XLA Ops:
  0.6 104.5 %copy-start = (f32[32,1024]{1,0:T(8,128)S(1)}, f32[32,1024]{1,0:T(8,128)}, u32[]{:S(2)}) copy-start(f32[32,1024]{1,0:T(8,128)} %ada1_ref.1) | copy-start | bytes 393220
  0.7 104.5 %copy-start.1 = (f32[32,1024]{1,0:T(8,128)S(1)}, f32[32,1024]{1,0:T(8,128)}, u32[]{:S(2)}) copy-start(f32[32,1024]{1,0:T(8,128)} %ada2_ref.1) | copy-start | bytes 393220
  0.7 104.5 %copy-start.2 = (f32[32]{0:T(128)S(1)}, f32[32]{0:T(128)}, u32[]{:S(2)}) copy-start(f32[32]{0:T(128)} %param.21) | copy-start | bytes 388

commit v6 on v5

--- a/solution.py
+++ b/solution.py
@@ -49,15 +49,15 @@
 
 
 XYZ, XZY, YXZ, YZX, ZXY, ZYX = itertools.permutations(range(3))
-ORDERS = [ZXY, ZXY, ZXY, YXZ, XYZ, XYZ, YXZ, XYZ, YXZ, YZX, XYZ, YXZ]
+ORDERS = [XYZ, ZXY, YXZ, XYZ, XYZ, XZY, YXZ, ZYX, ZYX, XZY, YZX, XYZ]
 DOWN, UP, OUT, QKV = range(0, 4), range(4, 8), range(8, 9), range(9, 12)
 STREAMS = len(ORDERS)
 SUMS_AT, FIRST_AT = (6.4, 8.5, 9.5), (6.4, 2.2, 2.2)
-QKV_AT, COEFF_AT = 16.3, 15.5
-COMPUTES = ((-1.0, 2.2), (2.3, 3.0), (3.0, 3.6), (3.6, 5.1), (5.1, 6.4), (10.4, 11.4), (11.4, 12.4), (12.4, 13.4))
-COMPUTES += ((13.4, 14.4), (14.4, 15.5), (15.5, 16.2), (16.4, 17.0))
-ROW_LOADS = ((1.2, (0.0, 1.6, 2.4, 3.2)), (3.0, (3.0, 5.7, 2.9)), (10.5, (3.2, 1.6, 2.4, 3.2)), (17.1, (3.2, 3.2, 4.8, 6.4)))
-PIECES = 4
+QKV_AT, COEFF_AT = 14.8, 13.6
+COMPUTES = ((-1.0, 2.2), (2.3, 3.0), (3.0, 3.6), (3.6, 5.1), (5.1, 6.4), (10.4, 11.0), (11.0, 11.6), (11.6, 12.2))
+COMPUTES += ((12.2, 12.8), (12.8, 13.6), (13.6, 14.8), (14.9, 15.4))
+ROW_LOADS = ((1.2, (0.0, 1.6, 2.4, 3.2)), (3.0, (3.0, 5.7, 2.9)), (10.5, (3.2, 1.6, 2.4, 3.2)), (15.5, (3.2, 3.2, 4.8, 6.4)))
+PIECES = 8
 
 
 def stages_of(bits):
@@ -89,8 +89,8 @@
     for p in range(STREAMS):
         first = ORDERS[p][0]
         begin = QKV_AT if p in QKV else SUMS_AT[first] if first in begun else FIRST_AT[first]
+        begun.add(first)
         events.append((begin, next(number), "ready", p))
-        begun.add(first)
     events.append((COEFF_AT, next(number), "ready", STREAMS))
     events += [(t, next(number), "rows", times) for t, times in ROW_LOADS]
     heapq.heapify(events)
@@ -141,6 +141,7 @@
 def scratch(z, nb):
     R, D, FF, PT, PS = z.R, z.D, z.FF, z.PT, z.PT + z.P
     stages = z.stages[0]
+    halved = sum(before > after for _, before, after in stages)
     vm, dma = pltpu.VMEM, pltpu.SemaphoreType.DMA
     s = dict(
         tok=vm((R, D), BF16),
@@ -204,21 +205,21 @@
         gcs=vm((z.bits + 2, 8, D), F32),
         gcr=vm((z.bits + 1, 8, D), F32),
         load_sem=dma((8,)),
-        row_ss=dma((4,)),
+        row_ss=dma((2,)),
         row_rs=dma((4,)),
-        own_sem=dma((4,)),
-        more_ss=dma((4,)),
+        own_sem=dma((2,)),
+        more_ss=dma((2,)),
         more_rs=dma((4,)),
-        more_own=dma((4,)),
+        more_own=dma((2,)),
         side_ss=dma((4, 2)),
         side_rs=dma((4, 2)),
         piece_rs=dma((2, PIECES)),
-        pair_ss=dma((8,)),
+        pair_ss=dma((1,)),
         pair_rs=dma((8,)),
         sum_ss=dma((1,)),
-        late_ss=dma((STREAMS, len(stages))),
+        late_ss=dma((STREAMS, len(stages) - halved) if len(stages) > halved + 1 else (1, 1)),
         rs_rs=dma((STREAMS, len(stages))),
-        ag_rs=dma((STREAMS, len(stages))),
+        ag_rs=dma((STREAMS,)),
         core_ss=dma((1,)),
         core_rs=dma((1,)),
         gc_ss=dma((1,)),
@@ -286,21 +287,24 @@
             started.append(copy)
         return copy
 
+    def more(ref, i, at):
+        return ref.at[i, at] if i == 0 else ref.at[i, at, :, pl.ds(0, D)]
+
     def send_rows(i, src, dst, odd=None):
         def one(j, carry):
             to = me ^ (Pn - j if odd is None else Pn + odd - 2 * j)
             pltpu.make_async_remote_copy(
                 src_ref=src.at[pl.ds(pl.multiple_of(to * T, 16), T)],
                 dst_ref=dst.at[pl.ds(pl.multiple_of(me * T, 16), T)],
-                send_sem=n.row_ss.at[i],
+                send_sem=n.row_ss.at[i % 2],
                 recv_sem=n.row_rs.at[i],
                 device_id=(to, rp),
                 device_id_type=MESH,
             ).start()
             pltpu.make_async_remote_copy(
-                src_ref=n.more_out.at[i, to],
-                dst_ref=n.more_in.at[i, me],
-                send_sem=n.more_ss.at[i],
+                src_ref=more(n.more_out, i, to),
+                dst_ref=more(n.more_in, i, me),
+                send_sem=n.more_ss.at[i % 2],
                 recv_sem=n.more_rs.at[i],
                 device_id=(to, rp),
                 device_id_type=MESH,
@@ -311,22 +315,22 @@
         if odd == 0:
             return
         mine = pl.ds(pl.multiple_of(me * T, 16), T)
-        pltpu.make_async_copy(src.at[mine], dst.at[mine], n.own_sem.at[i]).start()
-        pltpu.make_async_copy(n.more_out.at[i, me], n.more_in.at[i, me], n.more_own.at[i]).start()
+        pltpu.make_async_copy(src.at[mine], dst.at[mine], n.own_sem.at[i // 3]).start()
+        pltpu.make_async_copy(more(n.more_out, i, me), more(n.more_in, i, me), n.more_own.at[i // 3]).start()
 
     def waits_for(ref, sem):
         pltpu.make_async_copy(ref, ref, sem).wait()
 
     def rows_in(i, dst):
-        waits_for(n.more_in.at[i, pl.ds(0, Pn - 1)], n.more_rs.at[i])
-        waits_for(n.more_in.at[i, 0], n.more_own.at[i])
+        waits_for(more(n.more_in, i, pl.ds(0, Pn - 1)), n.more_rs.at[i])
+        waits_for(more(n.more_in, i, 0), n.more_own.at[i // 3])
         waits_for(dst.at[pl.ds(0, PT - T)], n.row_rs.at[i])
-        waits_for(dst.at[pl.ds(0, T)], n.own_sem.at[i])
+        waits_for(dst.at[pl.ds(0, T)], n.own_sem.at[i // 3])
         dst[PT:PS] = n.more_in[i, :, 0, :D].astype(BF16)
 
     def rows_gone(i, src):
-        waits_for(src.at[pl.ds(0, PT - T)], n.row_ss.at[i])
-        waits_for(n.more_out.at[i, pl.ds(0, Pn - 1)], n.more_ss.at[i])
+        waits_for(src.at[pl.ds(0, PT - T)], n.row_ss.at[i % 2])
+        waits_for(more(n.more_out, i, pl.ds(0, Pn - 1)), n.more_ss.at[i % 2])
 
     def set_rows(i, hot_rows, values, out):
         total = mm(hot_rows, values)
@@ -376,7 +380,7 @@
         waits_for(ref.at[far_slot], n.side_rs.at[i, 1])
 
     def to_mate(i, src, dst):
-        return remote(src, dst, n.pair_ss.at[i], n.pair_rs.at[i], (me, mate), True)
+        return remote(src, dst, n.pair_ss.at[0], n.pair_rs.at[i], (me, mate))
 
     n.cols[1] = lists_of(z, n.neighbours[...], me)
     dest = n.dest[...].astype(F32)
@@ -445,6 +449,7 @@
     earlier_sources = hot(iota((Pn, Pn), 0) > iota((Pn, Pn), 1)).astype(BF16)
     phase("wait tokens")
     rows_in(0, n.in_t)
+    send_rows(1, n.out_c, n.in_c, 0)
     phase("place rows")
     count = n.more_in[0, :, 0, D:].astype(BF16)
     offset = mm(earlier_sources, count).astype(BF16)
@@ -486,13 +491,12 @@
             )
 
         zero = jnp.zeros((1, D), F32)
-        return tiles(R, one, (zero, zero), together=4)
+        return tiles(R, one, (zero, zero), together=8)
 
     phase("norm")
     side_normed = []
     norm(n.x, 0, n.plain1, n.inv1, n.normed.at[1], lambda c: side_normed.append(to_near(1, n.normed, c)))
     mate_normed = to_mate(0, n.normed.at[1], n.normed_p)
-    send_rows(1, n.out_c, n.in_c, 0)
     phase("project")
     get_wqkv.wait()
 
@@ -593,6 +597,7 @@
     quarter = D // 2
     mate_gr = to_mate(6, n.gr.at[:, pl.ds(pl.multiple_of(mate * quarter, 128), quarter)], n.gr_p)
     live = {}
+    one_late = sum(rows == after for _, rows, after in z.stages[0]) == 1
 
     def place_in(p, k):
         return sum(((me >> b) & 1) << i for i, b in enumerate(z.stages[p][k][0]))
@@ -616,14 +621,15 @@
                 at = start_of(p, k) + (place_in(p, k) ^ j) * after
                 src, ss = n.acc.at[p, pl.ds(pl.multiple_of(at, after), after)], n.sum_ss.at[0]
             else:
-                src, ss = n.acc.at[p, span(p, k)], n.late_ss.at[p, k]
+                src = n.acc.at[p, span(p, k)]
+                ss = n.sum_ss.at[0] if one_late else n.late_ss.at[p, len(z.stages[p]) - 1 - k]
             live[p] = remote(src, getattr(n, f"rcv{k}").at[p, j - 1], ss, n.rs_rs.at[p, k], to)
 
     def reduce_end(p, k):
         _, rows, after = z.stages[p][k]
         got = getattr(n, f"rcv{k}")
         waits_for(got.at[p], n.rs_rs.at[p, k])
-        if after == rows:
+        if after == rows and not one_late:
             live[p].wait_send()
         kept = span(p, k + 1)
         total = n.acc[p, kept].astype(F32)
@@ -635,14 +641,17 @@
     def gather_start(p, k):
         ref = n.grads_out.at[rp, p, span(p, k + 1)]
         for _, to in partners(p, k):
-            remote(ref, ref, n.sum_ss.at[0], n.ag_rs.at[p, k], to)
+            remote(ref, ref, n.sum_ss.at[0], n.ag_rs.at[p] if k == 0 else n.rs_rs.at[p, k - 1], to)
+        if k == 0:
+            remote(ref, ref, n.core_ss.at[0], n.core_rs.at[0], (me, mate))
 
     def gather_end(p, k):
         _, rows, after = z.stages[p][k]
-        waits_for(n.grads_out.at[rp, p, pl.ds(0, rows - after)], n.ag_rs.at[p, k])
+        waits_for(n.grads_out.at[rp, p, pl.ds(0, rows - after)], n.ag_rs.at[p] if k == 0 else n.rs_rs.at[p, k - 1])
 
     def core_start(p):
-        ref = n.grads_out.at[rp, p]
+        rows = z.stages[p][0][2]
+        ref = n.grads_out.at[rp, p, pl.ds(pl.multiple_of((1 - place_in(p, 0)) * rows, rows), rows)]
         remote(ref, ref, n.core_ss.at[0], n.core_rs.at[0], (me, mate))
 
     steps_left = {}
@@ -720,7 +729,7 @@
             total = total + mm(n.low[:, side * R : (side + 1) * R], n.qkv[side, :, part(1, h)])
         n.gqkv[:, part(0, h)] = (total * scale).astype(BF16)
         if h < PIECES:
-            hand_on(2, n.go, side_go[h : h + 1])
+            hand_on(2, n.go, side_go[PIECES // H * h : PIECES // H * (h + 1)])
         service((3.05, 3.65, 5.15, 6.45)[h])
     service(10.3)
 
@@ -748,7 +757,7 @@
                 n.low2[t, span_q] = (w * (n.s2[t, span_q] - n.stats[side, H + h : H + h + 1, :])).astype(BF16)
             return carry
 
-        tiles(R, key_back, together=4)
+        tiles(R, key_back, together=8)
         total_k = jnp.zeros((R, HD), F32)
         total_v = jnp.zeros((R, HD), F32)
         for side in range(3):
@@ -757,7 +766,7 @@
             total_v = total_v + mm(n.low[:, span_q], n.go[side, :, head])
         n.gqkv[:, part(1, h)] = (total_k * scale).astype(BF16)
         n.gqkv[:, part(2, h)] = total_v.astype(BF16)
-        service(11.45 + h)
+        service(11.05 + 0.6 * h)
     phase("send gqkv")
     wide = 3 * D // 2
     mate_gqkv = to_mate(7, n.gqkv.at[:, pl.ds(pl.multiple_of(mate * wide, 128), wide)], n.gqkv_p)
@@ -775,7 +784,7 @@
         sums = jnp.where(row == i, value, sums)
     n.gcs[0] = sums
 
-    service(15.6)
+    service(13.7)
     mate_gqkv.wait_recv()
     mate_normed.wait_recv()
     phase("grad qkv")
@@ -784,29 +793,33 @@
         d = slice(p * BLOCK[1], (p + 1) * BLOCK[1])
         n.acc[QKV[p]] = (mm(n.normed[1], n.gqkv[:, c], TN) + mm(n.normed_p[...], n.gqkv_p[:, d], TN)).astype(BF16)
     phase("leave gx")
-    service(16.5)
+    service(14.95)
     rows_gone(1, n.out_c)
     set_rows(3, n.place[...], gx_ref[...], n.out_c)
     send_rows(3, n.out_c, n.home_g)
     phase("sums")
-    service()
-    waits_for(n.grads_out.at[mate], n.core_rs.at[0])
-    n.sums_out[...] = n.gcs[z.bits + 1]
+    service(50.0)
     phase("home")
     rows_in(2, n.home_y)
     n.y_out[...] = mm(n.pick[...], n.home_y[...]).astype(BF16)
     rows_in(3, n.home_g)
     n.g_out[...] = mm(n.pick[...], n.home_g[...]).astype(BF16)
 
+    service()
+    waits_for(n.grads_out.at[mate], n.core_rs.at[0])
+    n.sums_out[...] = n.gcs[z.bits + 1]
     phase("end")
     rows_gone(2, n.out_t)
     rows_gone(3, n.out_c)
     for copy in started:
         copy.wait_send()
+    blocks = R * (6 * D + FF) // (BLOCK[0] * BLOCK[1])
+    waits_for(n.grads_out.at[0, pl.ds(0, blocks)], n.pair_ss.at[0])
     for i, ref in ((1, n.normed), (2, n.go)):
         for leg in range(2):
             waits_for(ref.at[1], n.side_ss.at[i, leg])
-    waits_for(n.grads_out.at[:, :, pl.ds(0, BLOCK[0] - z.stages[0][-1][2])], n.sum_ss.at[0])
+    last = z.stages[0][-1][2]
+    waits_for(n.grads_out.at[:, :, pl.ds(0, BLOCK[0] - last + (last // 2 if one_late else 0))], n.sum_ss.at[0])
     waits_for(n.grads_out.at[rp], n.core_ss.at[0])
     waits_for(n.gcr, n.gc_ss.at[0])
 
@@ -821,8 +834,21 @@
 
 
 def finish(z, g_ref, sums_ref, y_ref, gx_ref, ada1_ref, ada2_ref, cond_ref, *rest):
-    y_out, gx_out, qkv_out, out_out, up_out, down_out, ga1_out, ga2_out, gcond_out, wide, wide_sem, row_sem = rest
-    rows = [pltpu.make_async_copy(a, b, row_sem.at[i]) for i, (a, b) in enumerate(((y_ref, y_out), (gx_ref, gx_out)))]
+    y_out, gx_out, qkv_out, out_out, up_out, down_out, ga1_out, ga2_out, gcond_out, wide, ga1, ga2, gcond, wide_sem, row_sem = rest
+    count = cond_ref.shape[1]
+    eye = lax.broadcasted_iota(I32, (count, count), 0) == lax.broadcasted_iota(I32, (count, count), 1)
+    cond = jnp.sum(jnp.where(eye, cond_ref[...], 0.0), axis=1, keepdims=True)
+    d = z.D
+    total = jnp.zeros((count, 1), F32)
+    for row, ada, out in ((0, ada1_ref, ga1), (2, ada2_ref, ga2)):
+        for j in range(2):
+            c = slice(j * d, (j + 1) * d)
+            sums = sums_ref[row + j : row + j + 1, :]
+            out[:, c] = cond * sums
+            total = total + jnp.sum(ada[:, c] * sums, axis=1, keepdims=True)
+    gcond[...] = jnp.sum(jnp.where(eye, total, 0.0), axis=0, keepdims=True)
+    pairs = ((y_ref, y_out), (gx_ref, gx_out), (ga1, ga1_out), (ga2, ga2_out), (gcond, gcond_out))
+    rows = [pltpu.make_async_copy(a, b, row_sem.at[i]) for i, (a, b) in enumerate(pairs)]
     for copy in rows:
         copy.start()
     high, across = BLOCK
@@ -841,18 +867,6 @@
             to = out.at[r * high : (r + 1) * high, c * across : (c + 1) * across]
             copies.append(pltpu.make_async_copy(wide.at[i, p], to, wide_sem.at[i, p]))
             copies[-1].start()
-    count = cond_ref.shape[1]
-    eye = lax.broadcasted_iota(I32, (count, count), 0) == lax.broadcasted_iota(I32, (count, count), 1)
-    cond = jnp.sum(jnp.where(eye, cond_ref[...], 0.0), axis=1, keepdims=True)
-    d = z.D
-    total = jnp.zeros((count, 1), F32)
-    for row, ada, out in ((0, ada1_ref, ga1_out), (2, ada2_ref, ga2_out)):
-        for j in range(2):
-            c = slice(j * d, (j + 1) * d)
-            sums = sums_ref[row + j : row + j + 1, :]
-            out[:, c] = cond * sums
-            total = total + jnp.sum(ada[:, c] * sums, axis=1, keepdims=True)
-    gcond_out[...] = jnp.sum(jnp.where(eye, total, 0.0), axis=0, keepdims=True)
     for copy in (*copies, *rows):
         copy.wait()
 
@@ -901,11 +915,14 @@
     y, gx, g_qkv, g_out, g_up, g_down, g_ada1, g_ada2, g_cond = pl.pallas_call(
         functools.partial(finish, z),
         in_specs=[vmem] * 7,
-        out_specs=[any_space] * 6 + [vmem] * 3,
+        out_specs=[any_space] * 9,
         scratch_shapes=[
             pltpu.VMEM((2, STREAMS) + BLOCK, F32),
+            pltpu.VMEM(ada_attn.shape, F32),
+            pltpu.VMEM(ada_mlp.shape, F32),
+            pltpu.VMEM(cond.shape, F32),
             pltpu.SemaphoreType.DMA((2, STREAMS)),
-            pltpu.SemaphoreType.DMA((2,)),
+            pltpu.SemaphoreType.DMA((5,)),
         ],
         out_shape=[
             shape((rows, width), BF16),

time: 112 us -> 109 us (0.973)
  Pallas kernels: 110 us -> 108 us
    pallas_call x1, Pallas kernels: 104 us -> 103 us  [local(): pl.pallas_call(functools.partial(layer, z, [*inputs, *outs, *held]), out_...]
where the time goes in v6:
time: 109 us
  Pallas kernels  108 us (99%)
    pallas_call x1, Pallas kernels, local(): pl.pallas_call(functools.partial(layer, z, [*inputs, *outs, *held]), out_...  103 us
    pallas_call x1, Pallas kernels, local(): pl.pallas_call(functools.partial(finish, z), in_specs=[vmem] * 7, out_spe...  5.09 us

profile of v6, /device:TPU:0, one launch (start us, length us, event | category | flops | bytes accessed | tf_op | source)
XLA Modules:
  0.0 108.5 jit_solution(13648332184365279400)
XLA Ops:
  0.6 0.0 copy-start
  0.7 0.0 copy-start.1
  0.7 0.0 copy-start.2
  0.7 102.5 %layer.1 = (bf16[2,12,512,256]{3,2,1,0:T(8,128)(2,1)S(1)}, f32[8,512]{1,0:T(8,128)S(1)}, bf16[256,512]{1,0:T(8,128)(2,1)S(1)}, bf16[256,512]{1,0:T(8,128)(2,1)S(1)}) custom-call(bf16[256,512]{1,0:T(8,128)(2,1)} %refs_0_.1, bf16[256,512]{1,0:T(8,128)(2,1)} %refs_1_.1, s32[1,256]{1,0:T(1,128)} %bitcast.7, s32[16,256]{1,0:T(8,128)} %bitcast.6, ...), custom_call_target="tpu_custom_call" | custom-call | tf_op jit(solution)/shard_map/layer/pallas_call | solution.py:904
  103.2 0.0 copy-done
  103.2 0.0 copy-done.1
  103.2 0.0 copy-done.2
  103.2 5.1 %finish.1 = (bf16[256,512]{1,0:T(8,128)(2,1)}, bf16[256,512]{1,0:T(8,128)(2,1)}, f32[512,1536]{1,0:T(8,128)}, f32[512,512]{1,0:T(8,128)}, f32[512,2048]{1,0:T(8,...) custom-call(bf16[2,12,512,256]{3,2,1,0:T(8,128)(2,1)S(1)} %get-tuple-element.22.g_ref, ...), custom_call_target="tpu_custom_call" | custom-call | tf_op jit(solution)/shard_map/finish/pallas_call | solution.py:915
Async XLA Ops:
  0.6 102.6 %copy-start = (f32[32,1024]{1,0:T(8,128)S(1)}, f32[32,1024]{1,0:T(8,128)}, u32[]{:S(2)}) copy-start(f32[32,1024]{1,0:T(8,128)} %ada1_ref.1) | copy-start | bytes 393220
  0.7 102.6 %copy-start.1 = (f32[32,1024]{1,0:T(8,128)S(1)}, f32[32,1024]{1,0:T(8,128)}, u32[]{:S(2)}) copy-start(f32[32,1024]{1,0:T(8,128)} %ada2_ref.1) | copy-start | bytes 393220
  0.7 102.6 %copy-start.2 = (f32[32]{0:T(128)S(1)}, f32[32]{0:T(128)}, u32[]{:S(2)}) copy-start(f32[32]{0:T(128)} %param.21) | copy-start | bytes 388

commit v7 on v6

--- a/solution.py
+++ b/solution.py
@@ -49,7 +49,7 @@
 
 
 XYZ, XZY, YXZ, YZX, ZXY, ZYX = itertools.permutations(range(3))
-ORDERS = [XYZ, ZXY, YXZ, XYZ, XYZ, XZY, YXZ, ZYX, ZYX, XZY, YZX, XYZ]
+ORDERS = [XYZ, ZXY, XYZ, YXZ, XYZ, XZY, YXZ, ZYX, ZYX, XZY, YZX, XYZ]
 DOWN, UP, OUT, QKV = range(0, 4), range(4, 8), range(8, 9), range(9, 12)
 STREAMS = len(ORDERS)
 SUMS_AT, FIRST_AT = (6.4, 8.5, 9.5), (6.4, 2.2, 2.2)
@@ -144,6 +144,9 @@
     halved = sum(before > after for _, before, after in stages)
     vm, dma = pltpu.VMEM, pltpu.SemaphoreType.DMA
     s = dict(
+        dest_in=vm((1, R), I32),
+        lists_in=vm((nb, R), I32),
+        cond_in=vm((1, 32), F32),
         tok=vm((R, D), BF16),
         cot=vm((R, D), BF16),
         wqkv=vm((D, 3 * D), BF16),
@@ -204,7 +207,7 @@
         **{f"rcv{k}": vm((STREAMS, (1 << len(b)) - 1, n, BLOCK[1]), BF16) for k, (b, _, n) in enumerate(stages)},
         gcs=vm((z.bits + 2, 8, D), F32),
         gcr=vm((z.bits + 1, 8, D), F32),
-        load_sem=dma((8,)),
+        load_sem=dma((11,)),
         row_ss=dma((2,)),
         row_rs=dma((4,)),
         own_sem=dma((2,)),
@@ -260,7 +263,18 @@
         return copy
 
     phase("entry")
+    barrier = pltpu.get_barrier_semaphore()
+
+    def greet(i, carry):
+        pl.semaphore_signal(barrier, inc=1, device_id=(lax.rem(me + i, Pn), rp), device_id_type=MESH)
+        return carry
+
+    lax.fori_loop(1, Pn, greet, 0)
+    pl.semaphore_signal(barrier, inc=1, device_id=(me, mate), device_id_type=MESH)
+    get_dest = load(8, n.dest, n.dest_in)
     get_tok = load(0, n.tokens, n.tok)
+    get_lists = load(9, n.neighbours, n.lists_in)
+    get_cond = load(10, n.cond, n.cond_in)
     get_cot = load(1, n.cotangent, n.cot)
     get_ada1 = load(2, n.ada_attn, n.ada1)
     get_ada2 = load(3, n.ada_mlp, n.ada2)
@@ -268,15 +282,6 @@
     get_wdown = load(5, n.w_down, n.wdown)
     get_wout = load(6, n.w_out, n.wout)
     get_wup = load(7, n.w_up, n.wup)
-
-    barrier = pltpu.get_barrier_semaphore()
-
-    def greet(i, carry):
-        pl.semaphore_signal(barrier, inc=1, device_id=(lax.rem(me + i, Pn), rp), device_id_type=MESH)
-        return carry
-
-    lax.fori_loop(1, Pn, greet, 0)
-    pl.semaphore_signal(barrier, inc=1, device_id=(me, mate), device_id_type=MESH)
 
     def remote(src, dst, ss, rs, to, keep=False):
         copy = pltpu.make_async_remote_copy(
@@ -382,8 +387,8 @@
     def to_mate(i, src, dst):
         return remote(src, dst, n.pair_ss.at[0], n.pair_rs.at[i], (me, mate))
 
-    n.cols[1] = lists_of(z, n.neighbours[...], me)
-    dest = n.dest[...].astype(F32)
+    get_dest.wait()
+    dest = n.dest_in[...].astype(F32)
     mine_hot = iota((Pn, R), 0) == dest
     before = hot(iota((R, R), 0) < iota((R, R), 1)).astype(BF16)
     earlier = mm(hot(mine_hot).astype(BF16), before)
@@ -394,6 +399,8 @@
     get_tok.wait()
     set_rows(0, pick_low, n.tok[...], n.out_t)
     n.more_out[0, :, 0, D:] = jnp.broadcast_to(jnp.sum(hot(mine_hot), axis=1, keepdims=True), (Pn, 128))
+    get_lists.wait()
+    n.cols[1] = lists_of(z, n.lists_in[...], me)
     phase("barrier")
     pl.semaphore_wait(barrier, Pn)
     phase("send tokens")
@@ -406,7 +413,8 @@
     phase("counts")
     get_ada1.wait()
     get_ada2.wait()
-    cond = jnp.broadcast_to(n.cond[...], (8, n.cond.shape[1]))
+    get_cond.wait()
+    cond = jnp.broadcast_to(n.cond_in[...], (8, n.cond_in.shape[1]))
     n.c[0:8] = jnp.dot(cond, n.ada1[...], precision=lax.Precision.HIGHEST, preferred_element_type=F32)
     n.c[8:16] = jnp.dot(cond, n.ada2[...], precision=lax.Precision.HIGHEST, preferred_element_type=F32)
     n.colq[...] = n.cols[1].T
@@ -890,7 +898,6 @@
         ada_mlp=ada_mlp,
         cond=cond,
     )
-    small = ("dest", "neighbours", "cond")
     any_space = pl.BlockSpec(memory_space=pl.ANY)
     vmem = pl.BlockSpec(memory_space=pltpu.VMEM)
     shape = jax.ShapeDtypeStruct
@@ -904,7 +911,7 @@
     held_out = pl.pallas_call(
         functools.partial(layer, z, [*inputs, *outs, *held]),
         out_shape=list(outs.values()),
-        in_specs=[vmem if k in small else any_space for k in inputs],
+        in_specs=[any_space] * len(inputs),
         out_specs=[vmem, vmem, vmem, vmem],
         scratch_shapes=list(held.values()),
         compiler_params=pltpu.CompilerParams(collective_id=0, has_side_effects=True, vmem_limit_bytes=56 << 20),

time: 109 us -> 107 us (0.982)
  Pallas kernels: 108 us -> 106 us
    pallas_call x1, Pallas kernels: 103 us -> 101 us  [local(): pl.pallas_call(functools.partial(layer, z, [*inputs, *outs, *held]), out_...]
where the time goes in v7:
time: 107 us
  Pallas kernels  106 us (99%)
    pallas_call x1, Pallas kernels, local(): pl.pallas_call(functools.partial(layer, z, [*inputs, *outs, *held]), out_...  101 us
    pallas_call x1, Pallas kernels, local(): pl.pallas_call(functools.partial(finish, z), in_specs=[vmem] * 7, out_spe...  5.09 us

profile of v7, /device:TPU:0, one launch (start us, length us, event | category | flops | bytes accessed | tf_op | source)
XLA Modules:
  0.0 107.2 jit_solution(2304309904707895258)
XLA Ops:
  0.6 0.0 copy-start
  0.7 0.0 copy-start.1
  0.7 0.0 copy-start.2
  0.7 101.2 %layer.1 = (bf16[2,12,512,256]{3,2,1,0:T(8,128)(2,1)S(1)}, f32[8,512]{1,0:T(8,128)S(1)}, bf16[256,512]{1,0:T(8,128)(2,1)S(1)}, bf16[256,512]{1,0:T(8,128)(2,1)S(1)}) custom-call(bf16[256,512]{1,0:T(8,128)(2,1)} %refs_0_.1, bf16[256,512]{1,0:T(8,128)(2,1)} %refs_1_.1, s32[1,256]{1,0:T(1,128)} %bitcast.7, s32[16,256]{1,0:T(8,128)} %bitcast.6, ...), custom_call_target="tpu_custom_call" | custom-call | tf_op jit(solution)/shard_map/layer/pallas_call | solution.py:911
  101.9 0.0 copy-done
  101.9 0.0 copy-done.1
  101.9 0.0 copy-done.2
  101.9 5.1 %finish.1 = (bf16[256,512]{1,0:T(8,128)(2,1)}, bf16[256,512]{1,0:T(8,128)(2,1)}, f32[512,1536]{1,0:T(8,128)}, f32[512,512]{1,0:T(8,128)}, f32[512,2048]{1,0:T(8,...) custom-call(bf16[2,12,512,256]{3,2,1,0:T(8,128)(2,1)S(1)} %get-tuple-element.22.g_ref, ...), custom_call_target="tpu_custom_call" | custom-call | tf_op jit(solution)/shard_map/finish/pallas_call | solution.py:922
Async XLA Ops:
  0.6 101.3 %copy-start = (f32[32,1024]{1,0:T(8,128)S(1)}, f32[32,1024]{1,0:T(8,128)}, u32[]{:S(2)}) copy-start(f32[32,1024]{1,0:T(8,128)} %ada1_ref.1) | copy-start | bytes 393220
  0.7 101.3 %copy-start.1 = (f32[32,1024]{1,0:T(8,128)S(1)}, f32[32,1024]{1,0:T(8,128)}, u32[]{:S(2)}) copy-start(f32[32,1024]{1,0:T(8,128)} %ada2_ref.1) | copy-start | bytes 393220
  0.7 101.3 %copy-start.2 = (f32[32]{0:T(128)S(1)}, f32[32]{0:T(128)}, u32[]{:S(2)}) copy-start(f32[32]{0:T(128)} %param.21) | copy-start | bytes 388
